TPU v7x, 32 devices: a whole 2x2x4 slice. The times are simulated.
32 devices in a mesh: grp: 2 (over core), cell: 16 (over z, y, x).
Axes of the slice: x: 2, y: 2, z: 4, core: 2. Of those that a mesh axis runs over, the one named last changes fastest.
Arguments:
- path_delay: float32 [133120], P('cell'), may hold values from 0 to 64
- path_angle: float32 [133120], P('cell'), may hold values from -3.140625 to 3.140625
- path_gain: float32 [2, 133120], P(None, 'cell'), may hold values from -0.9 to 0.9
- slot_counts: int32 [4096], P('cell'), may hold values from 1 to 64, as said below
- slot_offsets: int32 [4096], P('cell'), may hold values from 0 to 8319, as said below
- ray_link: int32 [4096], P('cell'), may hold values from 0 to 4095, as said below
- nearby_sectors: int32 [8, 512], P(None, 'cell'), may hold values from 0 to 511, as said below
- serving_slot: int32 [512], P('cell'), may hold values from 0 to 7
- symbols: bfloat16 [512, 2, 128], P('cell'), may hold values from -4 to 4
Outputs:
- received: float32 [512, 2, 128], P('cell')
Inputs may be any that keep to these rules, and one draw needn't show every extreme that they name: `slot_counts`: the counts of one device's 256 ray slots sum to 8320, and every device has a slot of 64 paths. The ray slots of one device hold at most 1040 paths of links of one owner, and exactly 1040 for some owner. Within one device, the ranges slot_offsets to slot_offsets + slot_counts - 1 of its 256 slots cover the device's 8320 paths once each. `ray_link`: every link appears in exactly one ray slot. The owner of link g is the device g // 256, which holds its user; within the ray slots of one device the owners never fall. The ray slots of one device hold at most 32 links of one owner, and exactly 32 of some owner; every owner has 256 links in all. `nearby_sectors`: entry serving_slot[u] of user u is its serving sector, one of the sectors of the device that holds the user; every other entry lies within 16 sector indices of the serving sector, and on every device some user has entries at distance exactly 16.
All inputs are finite; a program needn't handle non-finite values.
Results may differ from a plain program's by a relative error of at most 0.0027.
Values may be sent and summed in bfloat16 or wider, within the bound.
No kernel may reach another device: no remote copies, remote signals or barrier semaphores. Data moves between devices by JAX's collectives and lax.ppermute only.
A program may use at most 64 MiB of HBM per device.

v0:
```python
import math

import jax
import jax.numpy as jnp
from jax import lax
from jax.sharding import PartitionSpec as P

SECTOR_ANTENNAS = 64
FRAME_TONES = 128
PMAX = 64
NEARBY_COUNT = 8
CELL_SECTORS = 32
REACH = 16


EPSILON = 1e-06
FINE_STEPS = 16


def extended(x, sides, width):
    for axis, dim in sides:
        size, length = (lax.axis_size(axis), x.shape[dim])
        up = [(i, (i + 1) % size) for i in range(size - 1)]
        down = [(j, i) for i, j in up]
        last = lax.slice_in_dim(x, length - width, length, axis=dim)
        initial = lax.slice_in_dim(x, 0, width, axis=dim)
        before = lax.ppermute(last, axis, up)
        after = lax.ppermute(initial, axis, down)
        x = jnp.concatenate([before, x, after], axis=dim)
    return x


def delay_table(delay_rows):
    coarse_count = FRAME_TONES // FINE_STEPS
    coarse_freq = (
        jnp.arange(coarse_count, dtype=jnp.float32) * FINE_STEPS - FRAME_TONES // 2
    ) / FRAME_TONES
    fine_freq = jnp.arange(FINE_STEPS, dtype=jnp.float32) / FRAME_TONES
    coarse_phase = 2 * math.pi * delay_rows[:, :, None] * coarse_freq[None, None, :]
    fine_phase = 2 * math.pi * delay_rows[:, :, None] * fine_freq[None, None, :]
    coarse_cos = jnp.cos(coarse_phase)[:, :, :, None]
    coarse_sin = jnp.sin(coarse_phase)[:, :, :, None]
    fine_cos = jnp.cos(fine_phase)[:, :, None, :]
    fine_sin = jnp.sin(fine_phase)[:, :, None, :]
    shape_out = (delay_rows.shape[0], delay_rows.shape[1], FRAME_TONES)
    delay_real = (coarse_cos * fine_cos - coarse_sin * fine_sin).reshape(shape_out)
    delay_imag = (-(coarse_sin * fine_cos + coarse_cos * fine_sin)).reshape(shape_out)
    return jnp.concatenate([delay_real, delay_imag], axis=1).astype(jnp.bfloat16)


def make_response(delay_rows, angle_rows, real_rows, imag_rows, antenna_array):
    delay_stack = delay_table(delay_rows)
    steer_phase = math.pi * antenna_array[None, :, None] * jnp.sin(angle_rows)[:, None, :]
    steer_cos = jnp.cos(steer_phase)
    steer_sin = jnp.sin(steer_phase)
    spread_real = (real_rows[:, None, :] * steer_cos + imag_rows[:, None, :] * steer_sin).astype(
        jnp.bfloat16
    )
    spread_imag = (imag_rows[:, None, :] * steer_cos - real_rows[:, None, :] * steer_sin).astype(
        jnp.bfloat16
    )
    upper = jnp.concatenate([spread_real, -spread_imag], axis=2)
    lower = jnp.concatenate([spread_imag, spread_real], axis=2)
    mixing = jnp.concatenate([upper, lower], axis=1)
    response = jnp.einsum("bap,bpf->baf", mixing, delay_stack, preferred_element_type=jnp.float32)
    return response.astype(jnp.bfloat16).reshape(
        delay_rows.shape[0], 2, antenna_array.shape[0], FRAME_TONES
    )


def link_signal(response, padded, sector_local):
    remote = padded[sector_local]
    resp_real = response[:, 0]
    resp_imag = response[:, 1]
    remote_real = remote[:, 0]
    remote_imag = remote[:, 1]

    def product(left, right):
        return jnp.einsum("baf,baf->bf", left, right, preferred_element_type=jnp.float32)

    recv_real = product(resp_real, remote_real) - product(resp_imag, remote_imag)
    recv_imag = product(resp_real, remote_imag) + product(resp_imag, remote_real)
    return jnp.stack([recv_real, recv_imag], axis=1)


def shards(
    path_delay,
    path_angle,
    path_gain,
    slot_counts,
    slot_offsets,
    ray_link,
    nearby_sectors,
    serving_slot,
    symbols,
):
    devices = lax.axis_size("cell")
    here = lax.axis_index("cell")
    worker_count = lax.axis_size("grp")
    worker_index = lax.axis_index("grp")
    path_total = path_delay.shape[0]
    link_total = slot_counts.shape[0]
    total_users = serving_slot.shape[0]
    capacity = 2 * link_total // devices
    owner_grid = jnp.arange(devices, dtype=jnp.int32)
    owner_of = ray_link // link_total
    bucket_size = jnp.sum((owner_of[:, None] == owner_grid[None, :]).astype(jnp.int32), axis=0)
    bucket_start = jnp.cumsum(bucket_size) - bucket_size
    slot_grid = jnp.arange(capacity, dtype=jnp.int32)
    send_live = slot_grid[None, :] < bucket_size[:, None]
    send_slot = jnp.where(send_live, bucket_start[:, None] + slot_grid[None, :], 0).reshape(
        devices * capacity
    )
    send_live = send_live.reshape(devices * capacity)
    local_link = jnp.where(
        send_live, ray_link[send_slot] - jnp.repeat(owner_grid, capacity) * link_total, -1
    )
    link_tags = local_link.astype(jnp.float32)[None, :]
    send_counts = jnp.where(send_live, slot_counts[send_slot], 0)
    send_first = slot_offsets[send_slot]
    path_width = PMAX // worker_count
    path_begin = worker_index * path_width
    path_steps = path_begin + jnp.arange(path_width, dtype=jnp.int32)
    live_mask = send_live[:, None] & (path_steps[None, :] < send_counts[:, None])
    where_path = jnp.clip(send_first[:, None] + path_steps[None, :], 0, path_total - 1)
    columns = (path_delay, path_angle, path_gain[0], path_gain[1])
    packed = jnp.stack([jnp.where(live_mask, column[where_path], 0.0) for column in columns])
    arrived, arrived_tags = (
        lax.all_to_all(packed, "cell", split_axis=1, concat_axis=1, tiled=True),
        lax.all_to_all(link_tags, "cell", split_axis=1, concat_axis=1, tiled=True),
    )
    arrived = lax.all_gather(arrived, "grp", axis=2, tiled=True)
    target = arrived_tags[0].astype(jnp.int32)
    target = jnp.where(target >= 0, target, link_total)
    placed = (
        jnp.zeros((4, link_total, PMAX), jnp.float32).at[:, target, :].set(arrived, mode="drop")
    )
    antenna_portion = SECTOR_ANTENNAS // worker_count
    antenna_array = (
        worker_index * antenna_portion + jnp.arange(antenna_portion, dtype=jnp.int32)
    ).astype(jnp.float32)

    def respond(link_rows):
        return make_response(link_rows[0], link_rows[1], link_rows[2], link_rows[3], antenna_array)

    user_grid = jnp.arange(total_users, dtype=jnp.int32)
    serve_links = user_grid * NEARBY_COUNT + serving_slot
    serve_sector = (
        jnp.take_along_axis(nearby_sectors, serving_slot[None, :], axis=0)[0] - here * CELL_SECTORS
    )
    nearby_local = nearby_sectors - here * CELL_SECTORS + REACH
    user_block = 16
    block_count = total_users // user_block
    link_index = jnp.arange(link_total, dtype=jnp.int32)

    def one_block(block_id):
        chosen = lax.dynamic_slice_in_dim(
            link_index, block_id * user_block * NEARBY_COUNT, user_block * NEARBY_COUNT
        )
        return respond(placed[:, chosen, :])

    final_output = lax.map(one_block, jnp.arange(block_count, dtype=jnp.int32))
    channel_responses = final_output.reshape(
        total_users * NEARBY_COUNT, 2, antenna_portion, FRAME_TONES
    )
    serving_response = channel_responses[serve_links]
    symbol_rows = symbols.astype(jnp.float32)
    resp_real = serving_response[:, 0].astype(jnp.float32)
    resp_imag = serving_response[:, 1].astype(jnp.float32)
    contribution_real = (
        resp_real * symbol_rows[:, 0, None, :] + resp_imag * symbol_rows[:, 1, None, :]
    )
    contribution_imag = (
        resp_real * symbol_rows[:, 1, None, :] - resp_imag * symbol_rows[:, 0, None, :]
    )
    path_contribution = jnp.stack([contribution_real, contribution_imag], axis=1).reshape(
        total_users, 2 * antenna_portion * FRAME_TONES
    )
    selector = (jnp.arange(CELL_SECTORS, dtype=jnp.int32)[:, None] == serve_sector[None, :]).astype(
        jnp.float32
    )
    unscaled_signal = jnp.dot(
        selector,
        path_contribution,
        precision=lax.Precision.HIGHEST,
        preferred_element_type=jnp.float32,
    )
    unscaled_signal = unscaled_signal.reshape(CELL_SECTORS, 2, antenna_portion, FRAME_TONES)
    antenna_power = jnp.mean(
        unscaled_signal[:, 0] * unscaled_signal[:, 0]
        + unscaled_signal[:, 1] * unscaled_signal[:, 1],
        axis=2,
    )
    transmit_weights = (
        unscaled_signal / jnp.sqrt(antenna_power + EPSILON)[:, None, :, None]
    ).astype(jnp.bfloat16)
    padded = extended(transmit_weights, (("cell", 0),), REACH)
    every_part = link_signal(channel_responses, padded, nearby_local.T.reshape(link_total))
    partial_value = jnp.sum(every_part.reshape(total_users, NEARBY_COUNT, 2, FRAME_TONES), axis=1)
    summed_signal = lax.psum(partial_value, "grp")
    return summed_signal / math.sqrt(SECTOR_ANTENNAS)


def solution(mesh):
    placed = (
        P("cell"),
        P("cell"),
        P(None, "cell"),
        P("cell"),
        P("cell"),
        P("cell"),
        P(None, "cell"),
        P("cell"),
        P("cell", None, None),
    )
    return jax.shard_map(
        shards, mesh=mesh, in_specs=placed, out_specs=P("cell", None, None), check_vma=False
    )
```

profile of v0, /device:TPU:9, one launch (start us, length us, event | category | flops | bytes accessed | tf_op | source)
XLA Modules:
  0.0 536.7 jit_solution(7085916476988025946)
XLA Ops:
  1.3 3.7 gather_fusion.1
  5.7 6.7 %all-to-all-start = ((f32[1,16,32]{2,0,1:T(1,128)}), f32[1,16,32]{2,0,1:T(1,128)}, u32[]{:S(2)}, u32[]{:S(2)}) async-start(f32[1,16,32]{2,0,1:T(1,128)} %fusion.44), calls=%async_computation | async-start | bytes 16384 | tf_op jit(solution)/shard_map/all_to_all | solution.py:130
  13.0 3.5 gather_fusion.3
  17.6 90.5 %gather_fusion.6 = f32[16384]{0:T(1024)S(1)} fusion(f32[8320]{0:T(1024)S(1)} %get-tuple-element.109, s32[16384]{0:T(1024)S(1)} %broadcast_clamp_fusion), kind=kCustom, calls=%fused_computation.6 | custom fusion | bytes 196608 | tf_op jit(solution)/shard_map/gather | solution.py:127
  109.0 90.5 %gather_fusion.7 = f32[16384]{0:T(1024)S(1)} fusion(f32[8320]{0:T(1024)S(1)} %get-tuple-element.110, s32[16384]{0:T(1024)S(1)} %broadcast_clamp_fusion), kind=kCustom, calls=%fused_computation.7 | custom fusion | bytes 196608 | tf_op jit(solution)/shard_map/gather | solution.py:127
  200.3 90.5 %gather_fusion.4 = f32[16384]{0:T(1024)S(1)} fusion(f32[8320]{0:T(1024)S(1)} %copy-done, s32[16384]{0:T(1024)S(1)} %broadcast_clamp_fusion), kind=kCustom, calls=%fused_computation.4 | custom fusion | bytes 196608 | tf_op jit(solution)/shard_map/gather | solution.py:127
  291.7 90.5 %gather_fusion.5 = f32[16384]{0:T(1024)S(1)} fusion(f32[8320]{0:T(1024)S(1)} %copy-done.1, s32[16384]{0:T(1024)S(1)} %broadcast_clamp_fusion), kind=kCustom, calls=%fused_computation.5 | custom fusion | bytes 196608 | tf_op jit(solution)/shard_map/gather | solution.py:127
  382.4 3.5 gather_fusion.2
  389.2 6.4 %all-to-all-start.1 = ((f32[16,1,4096]{2,1,0:T(1,128)}), f32[16,1,4096]{2,1,0:T(1,128)S(1)}, u32[]{:S(2)}, u32[]{:S(2)}) async-start(f32[16,1,4096]{2,1,0:T(1,128)} %reshape.815), calls=%async_computation.1 | async-start | bytes 524288 | tf_op jit(solution)/shard_map/all_to_all | solution.py:129
  396.6 5.8 %all-to-all-done.1 = f32[16,1,4096]{2,1,0:T(1,128)S(1)} async-done(((f32[16,1,4096]{2,1,0:T(1,128)}), f32[16,1,4096]{2,1,0:T(1,128)S(1)}, u32[]{:S(2)}, u32[]{:S(2)}) %all-to-all-start.1) | async-done | bytes 262176 | tf_op jit(solution)/shard_map/all_to_all | solution.py:129
  405.1 5.3 all_gather.3
  410.8 14.2 %scatter_fusion = f32[4,256,64]{2,0,1:T(4,128)S(1)} fusion(f32[4,256,64]{2,0,1:T(4,128)S(1)} %broadcast_in_dim.55, s32[512]{0:T(512)S(1)} %bitcast.131, f32[512,4,64]{2,1,0:T(4,128)S(1)} %copy.43), kind=kCustom, calls=%fused_computation.11 | custom fusion | bytes 1574912 | tf_op jit(solution)/shard_map/scatter | solution.py:136
  425.1 74.8 %while.13 = (s32[]{:T(128)}, bf16[2,128,2,32,128]{4,3,2,1,0:T(8,128)(2,1)}, s32[2]{0:T(128)S(1)}, s32[256]{0:T(256)S(1)}, f32[4,256,64]{2,0,1:T(4,128)S(1)}, /*i...) while((s32[]{:T(128)}, bf16[2,128,2,32,128]{4,3,2,1,0:T(8,128)(2,1)}, ...), condition=%wide.region_4.5_spmd.clone, body=%wide.region_3.4_spmd.clone.sunk | while | flops 300361216 | bytes 38608128 | solution.py:162
  434.8 4.2 copy.89
  441.8 8.1 %fusion.60 = (bf16[128,32,64]{2,1,0:T(8,128)(2,1)S(1)}, bf16[128,32,64]{2,1,0:T(8,128)(2,1)S(1)}) fusion(f32[128,64]{1,0:T(8,128)S(1)} %bitcast.117, f32[128,64]{1,0:T(8,128)S(1)} %bitcast.119, f32[32]{0:T(128)S(1)} %convert_multiply_fusion.10, f32[128,64]{1,0:T(8,128)S(1)} %bitcast.115), kind=kLoop, calls=%fused_computation.28.clone.2 | loop fusion | flops 2359296 | bytes 1147008 | tf_op jit(solution)/shard_map/while/body/eval_jaxpr/convert_element_type | solution.py:59
  449.9 7.9 %fusion.61 = bf16[128,32,64]{2,1,0:T(8,128)(2,1)S(1)} fusion(f32[128,64]{1,0:T(8,128)S(1)} %bitcast.116, f32[128,64]{1,0:T(8,128)S(1)} %bitcast.120, f32[32]{0:T(128)S(1)} %convert_multiply_fusion.10, f32[128,64]{1,0:T(8,128)S(1)} %bitcast.118), kind=kLoop, calls=%fused_computation.50.clone.1 | loop fusion | flops 2097152 | bytes 622720 | tf_op jit(solution)/shard_map/while/body/eval_jaxpr/neg | solution.py:62
  472.1 4.2 copy.89
  479.1 8.1 %fusion.60 = (bf16[128,32,64]{2,1,0:T(8,128)(2,1)S(1)}, bf16[128,32,64]{2,1,0:T(8,128)(2,1)S(1)}) fusion(f32[128,64]{1,0:T(8,128)S(1)} %bitcast.117, f32[128,64]{1,0:T(8,128)S(1)} %bitcast.119, f32[32]{0:T(128)S(1)} %convert_multiply_fusion.10, f32[128,64]{1,0:T(8,128)S(1)} %bitcast.115), kind=kLoop, calls=%fused_computation.28.clone.2 | loop fusion | flops 2359296 | bytes 1147008 | tf_op jit(solution)/shard_map/while/body/eval_jaxpr/convert_element_type | solution.py:59
  487.3 7.9 %fusion.61 = bf16[128,32,64]{2,1,0:T(8,128)(2,1)S(1)} fusion(f32[128,64]{1,0:T(8,128)S(1)} %bitcast.116, f32[128,64]{1,0:T(8,128)S(1)} %bitcast.120, f32[32]{0:T(128)S(1)} %convert_multiply_fusion.10, f32[128,64]{1,0:T(8,128)S(1)} %bitcast.118), kind=kLoop, calls=%fused_computation.50.clone.1 | loop fusion | flops 2097152 | bytes 622720 | tf_op jit(solution)/shard_map/while/body/eval_jaxpr/neg | solution.py:62
  507.8 4.9 collective-permute-start.1
  512.7 4.1 collective-permute-done
  516.8 4.0 collective-permute-done.1
  524.6 6.8 %fusion.30 = (f32[256,128]{1,0:T(8,128)S(1)}, f32[256,128]{1,0:T(8,128)S(1)}, f32[256,128]{1,0:T(8,128)S(1)}, f32[256,128]{1,0:T(8,128)S(1)}) fusion(bf16[256,2,32,128]{3,2,1,0:T(8,128)(2,1)} %bitcast.12, bf16[256,2,32,128]{3,2,1,0:T(8,128)(2,1)} %gather_fusion.9), kind=kLoop, calls=%fused_computation.57 | loop fusion | flops 12451840 | bytes 8912896 | tf_op jit(solution)/shard_map/baf,baf->bf/dot_general | solution.py:79
  531.5 4.5 psum.7
  (136 shorter events, 58.8 us)
Async XLA Ops:
  0.0 200.3 %copy-start = (f32[8320]{0:T(1024)S(1)}, f32[8320]{0:T(1024)}, u32[]{:S(2)}) copy-start(f32[8320]{0:T(1024)} %param.11) | copy-start | bytes 99844
  0.0 13.0 %copy-start.2 = (s32[256]{0:T(256)S(1)}, s32[256]{0:T(256)}, u32[]{:S(2)}) copy-start(s32[256]{0:T(256)} %param.15) | copy-start | bytes 3076
  1.3 15.3 %copy-start.10 = (s32[1024]{0:T(1024)}, s32[1024]{0:T(1024)S(1)}, u32[]{:S(2)}) copy-start(s32[1024]{0:T(1024)S(1)} %pad_clamp_fusion.3) | copy-start | bytes 12292
  1.3 16.2 %copy-start.8 = (f32[2,8320]{1,0:T(2,128)S(1)}, f32[2,8320]{1,0:T(2,128)}, u32[]{:S(2)}) copy-start(f32[2,8320]{1,0:T(2,128)} %param.13) | copy-start | bytes 199684
  5.7 383.5 %all-to-all-start = ((f32[1,16,32]{2,0,1:T(1,128)}), f32[1,16,32]{2,0,1:T(1,128)}, u32[]{:S(2)}, u32[]{:S(2)}) async-start(f32[1,16,32]{2,0,1:T(1,128)} %fusion.44), calls=%async_computation | async-start | bytes 16384 | tf_op jit(solution)/shard_map/all_to_all | solution.py:130
  16.6 0.6 copy-start.13
  290.9 0.8 copy-start.1
  291.6 90.7 %copy-start.3 = (s32[256]{0:T(256)S(1)}, s32[256]{0:T(256)}, u32[]{:S(2)}) copy-start(s32[256]{0:T(256)} %param.14) | copy-start | bytes 3076
  291.7 90.7 %copy-start.11 = (s32[1024]{0:T(1024)S(1)}, s32[1024]{0:T(1024)}, u32[]{:S(2)}) copy-start(s32[1024]{0:T(1024)} %copy-done.10) | copy-start | bytes 12292
  382.2 3.7 copy-start.12
  382.2 3.8 copy-start.15
  382.2 3.9 copy-start.9
  382.2 3.9 copy-start.4
  382.2 3.9 copy-start.6
  382.2 3.9 copy-start.7
  382.3 3.9 copy-start.14
  389.2 13.2 %all-to-all-start.1 = ((f32[16,1,4096]{2,1,0:T(1,128)}), f32[16,1,4096]{2,1,0:T(1,128)S(1)}, u32[]{:S(2)}, u32[]{:S(2)}) async-start(f32[16,1,4096]{2,1,0:T(1,128)} %reshape.815), calls=%async_computation.1 | async-start | bytes 524288 | tf_op jit(solution)/shard_map/all_to_all | solution.py:129
  441.8 16.1 %copy-start.5 = (bf16[128,64,128]{2,1,0:T(8,128)(2,1)S(1)}, bf16[128,64,128]{2,1,0:T(8,128)(2,1)}, u32[]{:S(2)}) copy-start(bf16[128,64,128]{2,1,0:T(8,128)(2,1)} %copy.89) | copy-start | bytes 6291460 | tf_op jit(solution)/shard_map/while
  479.1 16.1 %copy-start.5 = (bf16[128,64,128]{2,1,0:T(8,128)(2,1)S(1)}, bf16[128,64,128]{2,1,0:T(8,128)(2,1)}, u32[]{:S(2)}) copy-start(bf16[128,64,128]{2,1,0:T(8,128)(2,1)} %copy.89) | copy-start | bytes 6291460 | tf_op jit(solution)/shard_map/while
  505.6 11.2 %collective-permute-start = (bf16[16,2,32,128]{3,0,2,1:T(8,128)(2,1)S(1)}, bf16[16,2,32,128]{3,0,2,1:T(8,128)(2,1)S(1)}, u32[]{:S(2)}, u32[]{:S(2)}) collective-permute-start(bf16[16,2,32,128]{3,0,2,1:T(8,128)(2,1)S(1)} %get-tuple-element.137), channel_id=1, source_target_pairs={{0,1},{1,2},{2,3},{3,4},{4,5},{5,6},{6,7},{7,8},{8,9},{9,10},{10,1... | collective-permute-start | bytes 786440 | tf_op jit(solution)/shard_map/ppermute | solution.py:27
  507.8 13.0 %collective-permute-start.1 = (bf16[16,2,32,128]{3,0,2,1:T(8,128)(2,1)S(1)}, bf16[16,2,32,128]{3,0,2,1:T(8,128)(2,1)S(1)}, u32[]{:S(2)}, u32[]{:S(2)}) collective-permute-start(bf16[16,2,32,128]{3,0,2,1:T(8,128)(2,1)S(1)} %get-tuple-element.138), channel_id=1, source_target_pairs={{1,0},{2,1},{3,2},{4,3},{5,4},{6,5},{7,6},{8,7},{9,8},{10,9},{11,1... | collective-permute-start | bytes 786440 | tf_op jit(solution)/shard_map/ppermute | solution.py:28
where the time goes:
time: 539 us; the launch traced here: 537 us
  local copies, waits for them, and re-layouts  424 us (79%)
  other arithmetic  59.6 us (11%)
  starting transfers between devices  20.1 us (4%)
  waiting for transfers between devices  13.9 us (3%)
  blocking collectives  9.71 us (2%)
  matrix products  7.12 us (1%)
    gather x8, local copies, waits for them, and re-layouts, shards(): column[where_path]  364 us
    convert_element_type x2, other arithmetic, make_response(): (imag_rows[:, None, :] * steer_cos - real_rows[:, None, :] * steer_sin).a...  16.2 us
    neg x2, other arithmetic, make_response(): upper = jnp.concatenate([spread_real, -spread_imag], axis=2)  15.8 us
    scatter x1, local copies, waits for them, and re-layouts, shards(): jnp.zeros((4, link_total, PMAX), jnp.float32).at[:, target, :]  14.2 us
  transfers between devices with their start and end apart: 4, of which 3 were waited for; matrix products, arithmetic and copies ran while one was open for 70% of the time, Pallas kernels for 0%

commit v1 on v0

v1 whole, which is shorter than its diff:
```python
import functools
import math

import jax
import jax.numpy as jnp
from jax import lax
from jax.experimental import pallas as pl
from jax.experimental.pallas import tpu as pltpu
from jax.sharding import PartitionSpec as P

SECTOR_ANTENNAS = 64
FRAME_TONES = 128
PMAX = 64
NEARBY_COUNT = 8
CELL_SECTORS = 32
REACH = 16
EPSILON = 1e-06

LANES = 128
GROUP = 8
HALF = FRAME_TONES // 2
COARSE = HALF // GROUP

SIN_TERMS = tuple((-1.0) ** n / math.factorial(2 * n + 1) for n in range(6))
COS_TERMS = tuple((-1.0) ** n / math.factorial(2 * n) for n in range(8))


def polynomial(terms, square):
    total = terms[-1]
    for term in terms[-2::-1]:
        total = total * square + term
    return total


def quarter_cos_sin(x):
    square = x * x
    return polynomial(COS_TERMS, square), x * polynomial(SIN_TERMS, square)


def cos_sin_turns(turns):
    turns = turns - jnp.round(turns)
    c, s = quarter_cos_sin(math.pi * turns)
    return 1.0 - 2.0 * s * s, 2.0 * s * c


def times(x, y):
    return x[0] * y[0] - x[1] * y[1], x[0] * y[1] + x[1] * y[0]


def powers(base, count):
    found = {1: base}
    for n in range(2, count + 1):
        found[n] = times(found[n // 2], found[n - n // 2])
    return found


def lane_index(rows):
    return lax.broadcasted_iota(jnp.int32, (rows, LANES), 1)


def pack_kernel(link_ref, count_ref, offset_ref, x_ref, y_ref, out_ref, *, link_total, capacity, stride):
    lane = lane_index(1)
    within = lane % PMAX
    upper = lane >= PMAX
    out_ref[...] = jnp.zeros_like(out_ref)
    empty = jnp.full((1, LANES), -1.0, jnp.float32)
    for owner in range(out_ref.shape[0] // stride):
        out_ref[owner * stride + capacity : owner * stride + capacity + 1, :] = empty

    def step(slot, carry):
        last_owner, place, tags = carry
        link = link_ref[slot]
        owner = lax.div(link, link_total)
        fresh = owner != last_owner
        place = jnp.where(fresh, 0, place + 1)
        offset = offset_ref[slot]
        row = lax.div(offset, LANES)
        shift = lax.rem(offset, LANES)
        early = lane >= shift
        x = jnp.where(early, x_ref[pl.ds(row, 1), :], x_ref[pl.ds(row + 1, 1), :])
        y = jnp.where(early, y_ref[pl.ds(row, 1), :], y_ref[pl.ds(row + 1, 1), :])
        x = pltpu.roll(x, lax.rem(LANES - shift, LANES), 1)
        y = pltpu.roll(y, lax.rem(LANES + PMAX - shift, LANES), 1)
        both = jnp.where(upper, y, x)
        both = jnp.where(within < count_ref[slot], both, 0.0)
        base = owner * stride
        out_ref[pl.ds(base + place, 1), :] = both
        local = (link - owner * link_total).astype(jnp.float32)
        tags = jnp.where(fresh, -1.0, tags)
        tags = jnp.where(lane == place, local, tags)
        out_ref[pl.ds(base + capacity, 1), :] = tags
        return owner, place, tags

    lax.fori_loop(0, link_total, step, (jnp.int32(-1), jnp.int32(0), empty), unroll=8)


def take_rows(source_ref, first, count, worker_index, own_ref, other_ref, even, odd):
    swap = worker_index == 0
    for n in range(count):
        row = source_ref[first + n]
        own = own_ref[pl.ds(row, 1), :]
        other = other_ref[pl.ds(row, 1), :]
        target = even if n % 2 == 0 else odd
        target[0, n // 2 : n // 2 + 1, :] = jnp.where(swap, own, other)
        target[1, n // 2 : n // 2 + 1, :] = jnp.where(swap, other, own)


def make_tables(even, odd, pairs, first_antenna, tables):
    fine_re, fine_im, coarse_re, coarse_im, near_re, near_im, far_re, far_im = tables
    steps = far_re.shape[0] // pairs
    left = lane_index(GROUP) < PMAX
    for group in range(pairs // GROUP):
        rows = pl.ds(group * GROUP, GROUP)
        pieces = []
        for field in range(2):
            a, b = even[field, rows, :], odd[field, rows, :]
            pieces.append(jnp.where(left, a, pltpu.roll(b, PMAX, 1)))
            pieces.append(jnp.where(left, pltpu.roll(a, PMAX, 1), b))
        delay, sine, gain_re, gain_im = pieces

        def put(ref_re, ref_im, n, count, value):
            at = pl.ds(group * GROUP * count + n, GROUP, stride=count)
            ref_re[at, :] = value[0]
            ref_im[at, :] = value[1]

        c, s = quarter_cos_sin(delay * (math.pi / FRAME_TONES))
        half = (c, -s)
        whole = times(half, half)
        fine = {0: half}
        up = powers(whole, GROUP - 1)
        put(fine_re, fine_im, 0, GROUP, half)
        for n in range(1, GROUP):
            fine[n] = times(half, up[n])
            put(fine_re, fine_im, n, GROUP, fine[n])
        stride = times(fine[GROUP - 1], half)
        for n, value in powers(stride, COARSE - 1).items():
            put(coarse_re, coarse_im, n, COARSE, value)
        c, s = cos_sin_turns(sine * 0.5)
        near = powers((c, -s), GROUP)
        put(near_re, near_im, 0, GROUP, (jnp.ones_like(c), jnp.zeros_like(c)))
        for n in range(1, GROUP):
            put(near_re, near_im, n, GROUP, near[n])
        c, s = cos_sin_turns(sine * (0.5 * first_antenna))
        value = times(times((gain_re, gain_im), (half[0], -half[1])), (c, -s))
        put(far_re, far_im, 0, steps, value)
        for n in range(1, steps):
            value = times(value, near[GROUP])
            put(far_re, far_im, n, steps, value)


def pair_response(pair, tables, steps):
    fine_re, fine_im, coarse_re, coarse_im, near_re, near_im, far_re, far_im = tables
    at = pl.ds(pl.multiple_of(pair * GROUP, GROUP), GROUP)
    fine = (fine_re[at, :], fine_im[at, :])
    delay = [fine]
    for n in range(1, COARSE):
        row = pl.ds(pair * COARSE + n, 1)
        delay.append(times((coarse_re[row, :], coarse_im[row, :]), fine))
    delay_re = jnp.concatenate([v[0] for v in delay], axis=0).astype(jnp.bfloat16)
    delay_im = jnp.concatenate([v[1] for v in delay], axis=0).astype(jnp.bfloat16)
    tones = jnp.concatenate(
        [
            jnp.concatenate([delay_re, -delay_im], axis=1),
            jnp.concatenate([delay_re, delay_im], axis=1),
        ],
        axis=0,
    )
    near = (near_re[at, :], near_im[at, :])
    spread = []
    for n in range(steps):
        row = pl.ds(pair * steps + n, 1)
        spread.append(times((far_re[row, :], far_im[row, :]), near))
    spread_re = jnp.concatenate([v[0] for v in spread], axis=0).astype(jnp.bfloat16)
    spread_im = jnp.concatenate([v[1] for v in spread], axis=0).astype(jnp.bfloat16)
    lane = lane_index(1)
    blocks = []
    for keep in (lane < PMAX, lane >= PMAX):
        keep = jnp.where(keep, 1.0, 0.0).astype(jnp.bfloat16)
        re, im = spread_re * keep, spread_im * keep
        blocks.append(jnp.concatenate([re, im], axis=1))
        blocks.append(jnp.concatenate([im, -re], axis=1))
    mixing = jnp.concatenate(blocks, axis=0)
    return lax.dot_general(
        mixing, tones, (((1,), (1,)), ((), ())), preferred_element_type=jnp.float32
    )


def reorder(values, index):
    pieces = [
        jnp.take_along_axis(values[n : n + GROUP], index, axis=1)
        for n in range(0, values.shape[0], GROUP)
    ]
    return jnp.concatenate(pieces, axis=0)


def serve_kernel(
    scalar_ref, source_ref, sector_ref, own_ref, other_ref, symbol_ref, low_ref, high_ref,
    even, odd, raw, symbols, *tables, portion,
):
    users = source_ref.shape[0]
    steps = portion // GROUP
    worker_index = scalar_ref[0]
    take_rows(source_ref, 0, users, worker_index, own_ref, other_ref, even, odd)
    make_tables(even, odd, users // 2, (worker_index * portion).astype(jnp.float32), tables)
    lane = lane_index(GROUP)
    index = jnp.where(lane < HALF, lane + HALF, FRAME_TONES - 1 - lane)
    symbols[...] = reorder(symbol_ref[...].astype(jnp.float32), index)
    raw[...] = jnp.zeros_like(raw)

    def one_pair(pair, carry):
        response = pair_response(pair, tables, steps).astype(jnp.bfloat16).astype(jnp.float32)
        for n in range(2):
            user = pair * 2 + n
            sym_re = symbols[pl.ds(user * 2, 1), :]
            sym_im = symbols[pl.ds(user * 2 + 1, 1), :]
            re = response[2 * n * portion : (2 * n + 1) * portion]
            im = response[(2 * n + 1) * portion : (2 * n + 2) * portion]
            sector = sector_ref[user]
            raw[sector, :portion, :] += re * sym_re + im * sym_im
            raw[sector, portion:, :] += re * sym_im - im * sym_re
        return carry

    lax.fori_loop(0, users // 2, one_pair, 0, unroll=2)
    half = CELL_SECTORS // 2

    def finish(sector, out_ref, row):
        value = raw[sector]
        re, im = value[:portion], value[portion:]
        power = jnp.sum(re * re + im * im, axis=1, keepdims=True) * (1.0 / FRAME_TONES)
        scale = 1.0 / jnp.sqrt(power + EPSILON)
        out_ref[row, :portion, :] = (re * scale).astype(jnp.bfloat16)
        out_ref[row, portion:, :] = (im * scale).astype(jnp.bfloat16)

    def one_sector(row, carry):
        finish(row, low_ref, row)
        finish(row + half, high_ref, row)
        return carry

    lax.fori_loop(0, half, one_sector, 0, unroll=2)


def respond_kernel(scalar_ref, source_ref, own_ref, other_ref, out_ref, even, odd, *tables, portion):
    pairs = out_ref.shape[0]
    steps = portion // GROUP
    worker_index = scalar_ref[0]
    first = pl.program_id(0) * pairs * 2
    take_rows(source_ref, first, pairs * 2, worker_index, own_ref, other_ref, even, odd)
    make_tables(even, odd, pairs, (worker_index * portion).astype(jnp.float32), tables)

    def one_pair(pair, carry):
        out_ref[pair] = pair_response(pair, tables, steps).astype(jnp.bfloat16)
        return carry

    lax.fori_loop(0, pairs, one_pair, 0, unroll=4)


def receive_kernel(
    sector_ref, response_ref, before_ref, low_ref, high_ref, after_ref, out_ref, remote, *, portion
):
    @pl.when(pl.program_id(0) == 0)
    def _():
        place = 0
        for part in (before_ref, low_ref, high_ref, after_ref):
            for n in range(part.shape[0]):
                remote[place] = part[n].astype(jnp.float32)
                place += 1

    users = out_ref.shape[0] // 2
    first = pl.program_id(0) * users

    def one_user(user, carry):
        total_re = jnp.zeros((GROUP, LANES), jnp.float32)
        total_im = jnp.zeros((GROUP, LANES), jnp.float32)
        for k in range(NEARBY_COUNT):
            sector = sector_ref[k, first + user]
            pair = user * (NEARBY_COUNT // 2) + k // 2
            base = (k % 2) * 2 * portion
            value = response_ref[pair, base : base + 2 * portion, :].astype(jnp.float32)
            other = remote[sector]
            for n in range(0, portion, GROUP):
                re, im = value[n : n + GROUP], value[portion + n : portion + n + GROUP]
                o_re, o_im = other[n : n + GROUP], other[portion + n : portion + n + GROUP]
                total_re = total_re + (re * o_re - im * o_im)
                total_im = total_im + (re * o_im + im * o_re)
        out_ref[pl.ds(user * 2, 1), :] = jnp.sum(total_re, axis=0, keepdims=True)
        out_ref[pl.ds(user * 2 + 1, 1), :] = jnp.sum(total_im, axis=0, keepdims=True)
        return carry

    lax.fori_loop(0, users, one_user, 0, unroll=2)
    lane = lane_index(GROUP)
    index = jnp.where(lane >= HALF, lane - HALF, FRAME_TONES - 1 - lane)
    out_ref[...] = reorder(out_ref[...], index)


VMEM = pl.BlockSpec(memory_space=pltpu.VMEM)
SMEM = pl.BlockSpec(memory_space=pltpu.SMEM)


def table_shapes(pairs, steps):
    return [pltpu.VMEM((pairs * n, LANES), jnp.float32) for n in (8, 8, 8, 8, 8, 8, steps, steps)]


def shards(
    path_delay,
    path_angle,
    path_gain,
    slot_counts,
    slot_offsets,
    ray_link,
    nearby_sectors,
    serving_slot,
    symbols,
):
    devices = lax.axis_size("cell")
    here = lax.axis_index("cell")
    worker_count = lax.axis_size("grp")
    worker_index = lax.axis_index("grp")
    path_total = path_delay.shape[0]
    link_total = slot_counts.shape[0]
    total_users = serving_slot.shape[0]
    capacity = 2 * link_total // devices
    stride = pl.cdiv(capacity + 1, GROUP) * GROUP
    portion = SECTOR_ANTENNAS // worker_count
    steps = portion // GROUP
    scalar = worker_index.astype(jnp.int32).reshape(1)

    path_rows = pl.cdiv(pl.cdiv(path_total, LANES) + 1, GROUP) * GROUP
    lower = worker_index == 0

    def rows_of(values):
        return jnp.pad(values, (0, path_rows * LANES - path_total)).reshape(path_rows, LANES)

    x = rows_of(jnp.where(lower, path_delay, path_gain[0]))
    y = rows_of(jnp.where(lower, jnp.sin(path_angle), path_gain[1]))
    packed = pl.pallas_call(
        functools.partial(
            pack_kernel, link_total=link_total, capacity=capacity, stride=stride
        ),
        out_shape=jax.ShapeDtypeStruct((devices * stride, LANES), jnp.float32),
        in_specs=[SMEM, SMEM, SMEM, VMEM, VMEM],
        out_specs=VMEM,
    )(ray_link, slot_counts, slot_offsets, x, y)
    arrived = lax.all_to_all(
        packed.reshape(devices, stride, LANES), "cell", split_axis=0, concat_axis=0, tiled=True
    )
    other = lax.ppermute(arrived, "grp", [(n, worker_count - 1 - n) for n in range(worker_count)])
    tags = arrived[:, capacity, :capacity].astype(jnp.int32).reshape(devices * capacity)
    slot_rows = (
        jnp.arange(devices, dtype=jnp.int32)[:, None] * stride
        + jnp.arange(capacity, dtype=jnp.int32)[None, :]
    ).reshape(devices * capacity)

    def find(links):
        return jnp.sum(jnp.where(links[:, None] == tags[None, :], slot_rows[None, :], 0), axis=1)

    source = find(jnp.arange(link_total, dtype=jnp.int32))
    serve_source = find(
        jnp.arange(total_users, dtype=jnp.int32) * NEARBY_COUNT + serving_slot
    )
    chosen = jnp.arange(NEARBY_COUNT, dtype=jnp.int32)[:, None] == serving_slot[None, :]
    serve_sector = jnp.sum(jnp.where(chosen, nearby_sectors, 0), axis=0) - here * CELL_SECTORS
    nearby_local = nearby_sectors - here * CELL_SECTORS + REACH

    own_rows = arrived.reshape(devices * stride, LANES)
    other_rows = other.reshape(devices * stride, LANES)
    half = CELL_SECTORS // 2
    part = jax.ShapeDtypeStruct((half, 2 * portion, LANES), jnp.bfloat16)
    serve_pairs = total_users // 2
    low, high = pl.pallas_call(
        functools.partial(serve_kernel, portion=portion),
        out_shape=(part, part),
        in_specs=[SMEM, SMEM, SMEM, VMEM, VMEM, VMEM],
        out_specs=(VMEM, VMEM),
        scratch_shapes=[
            pltpu.VMEM((2, serve_pairs, LANES), jnp.float32),
            pltpu.VMEM((2, serve_pairs, LANES), jnp.float32),
            pltpu.VMEM((CELL_SECTORS, 2 * portion, LANES), jnp.float32),
            pltpu.VMEM((2 * total_users, LANES), jnp.float32),
        ]
        + table_shapes(serve_pairs, steps),
    )(scalar, serve_source, serve_sector, own_rows, other_rows, symbols.reshape(2 * total_users, LANES))

    up = [(n, n + 1) for n in range(devices - 1)]
    down = [(m, n) for n, m in up]
    before = lax.ppermute(high, "cell", up)
    after = lax.ppermute(low, "cell", down)

    pair_total = link_total // 2
    block = 16
    response = pl.pallas_call(
        functools.partial(respond_kernel, portion=portion),
        out_shape=jax.ShapeDtypeStruct((pair_total, 4 * portion, LANES), jnp.bfloat16),
        grid=(pair_total // block,),
        in_specs=[SMEM, SMEM, VMEM, VMEM],
        out_specs=pl.BlockSpec((block, 4 * portion, LANES), lambda n: (n, 0, 0)),
        scratch_shapes=[
            pltpu.VMEM((2, block, LANES), jnp.float32),
            pltpu.VMEM((2, block, LANES), jnp.float32),
        ]
        + table_shapes(block, steps),
        cost_estimate=pl.CostEstimate(
            flops=pair_total * 2 * 128 * 128 * 256 * 40,
            bytes_accessed=pair_total * 4 * portion * LANES * 2,
            transcendentals=0,
        ),
    )(scalar, source, own_rows, other_rows)

    user_block = 8
    partial_value = pl.pallas_call(
        functools.partial(receive_kernel, portion=portion),
        out_shape=jax.ShapeDtypeStruct((2 * total_users, LANES), jnp.float32),
        grid=(total_users // user_block,),
        in_specs=[
            SMEM,
            pl.BlockSpec(
                (user_block * NEARBY_COUNT // 2, 4 * portion, LANES), lambda n: (n, 0, 0)
            ),
            VMEM,
            VMEM,
            VMEM,
            VMEM,
        ],
        out_specs=pl.BlockSpec((2 * user_block, LANES), lambda n: (n, 0)),
        scratch_shapes=[
            pltpu.VMEM((CELL_SECTORS + 2 * REACH, 2 * portion, LANES), jnp.float32)
        ],
    )(nearby_local, response, before, low, high, after)
    summed = partial_value + lax.ppermute(
        partial_value, "grp", [(n, worker_count - 1 - n) for n in range(worker_count)]
    )
    return (summed * (1.0 / math.sqrt(SECTOR_ANTENNAS))).reshape(total_users, 2, FRAME_TONES)


def solution(mesh):
    placed = (
        P("cell"),
        P("cell"),
        P(None, "cell"),
        P("cell"),
        P("cell"),
        P("cell"),
        P(None, "cell"),
        P("cell"),
        P("cell", None, None),
    )
    return jax.shard_map(
        shards, mesh=mesh, in_specs=placed, out_specs=P("cell", None, None), check_vma=False
    )
```

time: 539 us -> 61.8 us (0.11)
  local copies, waits for them, and re-layouts: 424 us -> 4.04 us
  other arithmetic: 59.6 us -> 6.4 us
  Pallas kernels: 0 us -> 26.3 us
  blocking collectives: 9.71 us -> 0 us
  matrix products: 7.12 us -> 0 us
  waiting for transfers between devices: 13.9 us -> 6.78 us
    gather x17 -> x0, local copies, waits for them, and re-layouts: 383 us -> none  [the longest x8 364 us: shards(): column[where_path]]
    pallas_call x0 -> x4, Pallas kernels: none -> 26.3 us  [the longest x1 11.2 us: shards(): pl.pallas_call(functools.partial(respond_kernel, portion=portion), out_sh...]
    convert_element_type x5 -> x1, other arithmetic: 17.8 us -> 0.03 us  [shards(): arrived[:, capacity, :capacity].astype(jnp.int32)]
    neg x2 -> x0, other arithmetic: 15.8 us -> none  [make_response(): upper = jnp.concatenate([spread_real, -spread_imag], axis=2)]
    scatter x1 -> x0, local copies, waits for them, and re-layouts: 14.2 us -> none  [shards(): jnp.zeros((4, link_total, PMAX), jnp.float32).at[:, target, :]]
    neg x2 -> x0, local copies, waits for them, and re-layouts: 8.33 us -> none  [delay_table(): -(coarse_sin * fine_cos + coarse_cos * fine_sin)]
    dot_general x3 -> x0, matrix products: 7.12 us -> none  [the longest x2 5.84 us: make_response(): jnp.einsum('bap,bpf->baf', mixing, delay_stack, preferred_element_type=jn...]
    ppermute x2 -> x4, waiting for transfers between devices: 8.06 us -> 1.08 us  [the longest x1 1.07 us: shards(): lax.ppermute(partial_value, 'grp', [(n, worker_count - 1 - n) for n in ra...]
  transfers between devices with their start and end apart: 4 -> 5, of which waited for: 3 -> 2; matrix products, arithmetic and copies ran while one was open for 70% -> 7% of each run, Pallas kernels for 0% -> 18%
where the time goes in v1:
time: 61.8 us; the launch traced here: 61.1 us
  Pallas kernels  26.3 us (43%)
  starting transfers between devices  17.6 us (28%)
  waiting for transfers between devices  6.78 us (11%)
  other arithmetic  6.4 us (10%)
  local copies, waits for them, and re-layouts  4.04 us (7%)
    pallas_call x1, Pallas kernels, shards(): pl.pallas_call(functools.partial(respond_kernel, portion=portion), out_sh...  11.2 us
    all_to_all x1, starting transfers between devices, shards(): lax.all_to_all(packed.reshape(devices, stride, LANES), 'cell', split_axis...  6.66 us
    all_to_all x1, waiting for transfers between devices, shards(): lax.all_to_all(packed.reshape(devices, stride, LANES), 'cell', split_axis...  5.7 us
    pallas_call x1, Pallas kernels, shards(): pl.pallas_call(functools.partial(receive_kernel, portion=portion), out_sh...  5.2 us
    pallas_call x1, Pallas kernels, shards(): pl.pallas_call(functools.partial(pack_kernel, link_total=link_total, capa...  5.12 us
    ppermute x1, starting transfers between devices, shards(): after = lax.ppermute(low, 'cell', down)  4.89 us
    pallas_call x1, Pallas kernels, shards(): pl.pallas_call(functools.partial(serve_kernel, portion=portion), out_shap...  4.75 us
    ppermute x1, starting transfers between devices, shards(): lax.ppermute(arrived, 'grp', [(n, worker_count - 1 - n) for n in range(wo...  3.23 us
  transfers between devices with their start and end apart: 5, of which 2 were waited for; matrix products, arithmetic and copies ran while one was open for 7% of the time, Pallas kernels for 18%

profile of v1, /device:TPU:9, one launch (start us, length us, event | category | flops | bytes accessed | tf_op | source)
XLA Modules:
  0.0 61.1 jit_solution(2807255073196861581)
XLA Ops:
  0.0 1.1 %slice_reduce_fusion = (f32[8320]{0:T(1024)S(1)}, f32[8320]{0:T(1024)S(1)}) fusion(f32[2,8320]{1,0:T(2,128)} %param.11), kind=kLoop, calls=%fused_computation.6 | loop fusion | bytes 133120 | tf_op jit(solution)/shard_map/slice | solution.py:334
  1.1 0.9 %sine_select_fusion = (f32[8320]{0:T(1024)S(1)}, f32[8320]{0:T(1024)S(1)}) fusion(f32[8320]{0:T(1024)S(1)} %get-tuple-element.9, f32[8320]{0:T(1024)} %param.10, pred[]{:T(512)S(6)} %eq.21, f32[8320]{0:T(1024)} %param.9, f32[8320]{0:T(1024)S(1)} %get-tuple-element.10), kind=kLoop, calls=%fused_computation.4 | loop fusion | flops 16640 | bytes 199681 | tf_op jit(solution)/shard_map/jit(_where)/select_n | solution.py:334
  2.1 0.6 %pad_bitcast_fusion.1.x_ref = f32[72,128]{1,0:T(8,128)} fusion(f32[8320]{0:T(1024)S(1)} %get-tuple-element.14), kind=kLoop, calls=%fused_computation.5 | loop fusion | bytes 70144 | tf_op jit(solution)/shard_map/reshape | solution.py:331
  2.7 0.6 pad_bitcast_fusion.y_ref
  3.3 5.1 %shard_map.91 = f32[640,128]{1,0:T(8,128)} custom-call(s32[256]{0:T(256)} %link_ref.1, s32[256]{0:T(256)} %count_ref.1, s32[256]{0:T(256)} %offset_ref.1, f32[72,128]{1,0:T(8,128)} %pad_bitcast_fusion.1.x_ref, f32[72,128]{1,0:T(8,128)} %pad_bitcast_fusion.y_ref), custom_call_target="tpu_custom_call" | custom-call | tf_op jit(solution)/shard_map/pallas_call | solution.py:335
  8.4 6.7 %all-to-all-start = ((f32[16,40,128]{2,1,0:T(8,128)}), f32[16,40,128]{2,1,0:T(8,128)S(1)}, u32[]{:S(2)}, u32[]{:S(2)}) async-start(f32[16,40,128]{2,1,0:T(8,128)} %bitcast.12), calls=%async_computation | async-start | bytes 655360 | tf_op jit(solution)/shard_map/all_to_all | solution.py:343
  15.2 0.7 %multiply_add_fusion = s32[32]{0:T(128)S(1)} fusion(s32[32]{0:T(128)} %param.16), kind=kLoop, calls=%fused_computation.16 | loop fusion | flops 64 | bytes 256 | tf_op jit(solution)/shard_map/add | solution.py:358
  15.9 1.3 %select_reduce_fusion.2 = (s32[32]{0:T(128)S(1)}, s32[8,32]{1,0:T(8,128)}) fusion(s32[8,32]{1,0:T(8,128)} %param.15, s32[32]{0:T(128)} %param.16, s32[]{:T(128)S(6)} %mul.26), kind=kLoop, calls=%fused_computation.13 | loop fusion | flops 1248 | bytes 2308 | tf_op jit(solution)/shard_map/reduce_sum | solution.py:361
  17.2 0.6 broadcast_subtract_fusion.sector_ref
  17.8 5.7 %all-to-all-done = f32[16,40,128]{2,1,0:T(8,128)S(1)} async-done(((f32[16,40,128]{2,1,0:T(8,128)}), f32[16,40,128]{2,1,0:T(8,128)S(1)}, u32[]{:S(2)}, u32[]{:S(2)}) %all-to-all-start) | async-done | bytes 327712 | tf_op jit(solution)/shard_map/all_to_all | solution.py:343
  23.5 3.2 %collective-permute-start = (f32[16,40,128]{2,1,0:T(8,128)S(1)}, f32[16,40,128]{2,1,0:T(8,128)S(1)}, u32[]{:S(2)}, u32[]{:S(2)}) collective-permute-start(f32[16,40,128]{2,1,0:T(8,128)S(1)} %all-to-all-done), channel_id=1, source_target_pairs={{0,16},{16,0},{1,17},{17,1},{2,18},{18,2},{3,19},{19,3},{4,20},{20... | collective-permute-start | bytes 983048 | tf_op jit(solution)/shard_map/ppermute | solution.py:346
  26.8 0.8 %select_reduce_fusion.1.source_ref = s32[32]{0:T(128)} fusion(s32[512]{0:T(512)S(1)} %add.49, s32[512]{0:T(512)S(1)} %convert_element_type.14, s32[32]{0:T(128)S(1)} %multiply_add_fusion), kind=kLoop, calls=%fused_computation.2 | loop fusion | flops 49120 | bytes 4352 | tf_op jit(solution)/shard_map/reduce_sum | solution.py:354
  27.6 0.7 %select_reduce_fusion.source_ref = s32[256]{0:T(256)} fusion(s32[512]{0:T(512)S(1)} %add.49, s32[512]{0:T(512)S(1)} %convert_element_type.14), kind=kLoop, calls=%fused_computation | loop fusion | flops 392960 | bytes 5120 | tf_op jit(solution)/shard_map/reduce_sum | solution.py:354
  28.3 0.7 %copy-done.1 = f32[16,40,128]{2,1,0:T(8,128)} copy-done((f32[16,40,128]{2,1,0:T(8,128)}, f32[16,40,128]{2,1,0:T(8,128)S(1)}, u32[]{:S(2)}) %copy-start.1) | copy-done | bytes 327704
  29.0 4.8 %shard_map.93 = (bf16[16,64,128]{2,1,0:T(8,128)(2,1)}, bf16[16,64,128]{2,1,0:T(8,128)(2,1)}) custom-call(s32[1]{0:T(128)} %bitcast.scalar_ref, s32[32]{0:T(128)} %select_reduce_fusion.1.source_ref, s32[32]{0:T(128)} %broadcast_subtract_fusion.sector_ref, f32[640,128]{1,0:T(8,128)} %bitcast.10, f32[640,128]{1,0:T(8,128)} %bitcast.13, bf16[64,128]{1,0:T(8,128)(2,1)} %bitcast.15), custom_call_target="tpu_custom_call" | custom-call | tf_op jit(solution)/shard_map/pallas_call | solution.py:369
  33.8 2.2 %collective-permute-start.1 = (bf16[16,64,128]{2,1,0:T(8,128)(2,1)}, bf16[16,64,128]{2,1,0:T(8,128)(2,1)S(1)}, u32[]{:S(2)}, u32[]{:S(2)}) collective-permute-start(bf16[16,64,128]{2,1,0:T(8,128)(2,1)} %get-tuple-element.7.high_ref), channel_id=1, source_target_pairs={{0,1},{1,2},{2,3},{3,4},{4,5},{5,6},{6,7},{7,8},{8,9},{9,10},{10,1... | collective-permute-start | bytes 786440 | tf_op jit(solution)/shard_map/ppermute | solution.py:385
  36.0 4.9 %collective-permute-start.2 = (bf16[16,64,128]{2,1,0:T(8,128)(2,1)}, bf16[16,64,128]{2,1,0:T(8,128)(2,1)S(1)}, u32[]{:S(2)}, u32[]{:S(2)}) collective-permute-start(bf16[16,64,128]{2,1,0:T(8,128)(2,1)} %get-tuple-element.8.low_ref), channel_id=1, source_target_pairs={{1,0},{2,1},{3,2},{4,3},{5,4},{6,5},{7,6},{8,7},{9,8},{10,9},{11,1... | collective-permute-start | bytes 786440 | tf_op jit(solution)/shard_map/ppermute | solution.py:386
  40.9 11.2 %shard_map.92.response_ref = bf16[128,128,128]{2,1,0:T(8,128)(2,1)} custom-call(s32[1]{0:T(128)} %bitcast.scalar_ref, s32[256]{0:T(256)} %select_reduce_fusion.source_ref, f32[640,128]{1,0:T(8,128)} %bitcast.11, f32[640,128]{1,0:T(8,128)} %bitcast.14), custom_call_target="tpu_custom_call" | custom-call | flops 42949672960 | bytes 4194304 | tf_op jit(solution)/shard_map/pallas_call | solution.py:390
  52.1 0.7 %copy-done.2 = bf16[16,64,128]{2,1,0:T(8,128)(2,1)} copy-done((bf16[16,64,128]{2,1,0:T(8,128)(2,1)}, bf16[16,64,128]{2,1,0:T(8,128)(2,1)S(1)}, u32[]{:S(2)}) %copy-start.2) | copy-done | bytes 262168
  52.8 0.1 copy-done.3
  52.9 5.2 %shard_map.94 = f32[64,128]{1,0:T(8,128)} custom-call(s32[8,32]{1,0:T(8,128)} %get-tuple-element.12.sector_ref, bf16[128,128,128]{2,1,0:T(8,128)(2,1)} %shard_map.92.response_ref, bf16[16,64,128]{2,1,0:T(8,128)(2,1)} %copy-done.2, bf16[16,64,128]{2,1,0:T(8,128)(2,1)} %get-tuple-element.8.low_ref, bf16[16,64,128]{2,1,0:T(8,128)(2,1)} %get-tuple-element.7.high_ref, ...), custom_call_target="tpu_custom_call" | custom-call | tf_op jit(solution)/shard_map/pallas_call | solution.py:409
  58.1 0.6 collective-permute-start.3
  58.7 1.1 %collective-permute-done.3 = f32[64,128]{1,0:T(8,128)S(1)} collective-permute-done((f32[64,128]{1,0:T(8,128)}, f32[64,128]{1,0:T(8,128)S(1)}, u32[]{:S(2)}, u32[]{:S(2)}) %collective-permute-start.3) | collective-permute-done | bytes 32800 | tf_op jit(solution)/shard_map/ppermute | solution.py:428
  59.8 1.4 %add_multiply_fusion = f32[64,128]{1,0:T(8,128)} fusion(f32[64,128]{1,0:T(8,128)} %shard_map.94, f32[64,128]{1,0:T(8,128)S(1)} %collective-permute-done.3), kind=kLoop, calls=%fused_computation.8 | loop fusion | flops 16384 | bytes 98304 | tf_op jit(solution)/shard_map/mul | solution.py:431
  (13 shorter events, 0.3 us)
Async XLA Ops:
  8.4 15.1 %all-to-all-start = ((f32[16,40,128]{2,1,0:T(8,128)}), f32[16,40,128]{2,1,0:T(8,128)S(1)}, u32[]{:S(2)}, u32[]{:S(2)}) async-start(f32[16,40,128]{2,1,0:T(8,128)} %bitcast.12), calls=%async_computation | async-start | bytes 655360 | tf_op jit(solution)/shard_map/all_to_all | solution.py:343
  23.5 4.8 %copy-start = (f32[16,40,128]{2,1,0:T(8,128)}, f32[16,40,128]{2,1,0:T(8,128)S(1)}, u32[]{:S(2)}) copy-start(f32[16,40,128]{2,1,0:T(8,128)S(1)} %all-to-all-done) | copy-start | bytes 983044
  23.5 4.8 %collective-permute-start = (f32[16,40,128]{2,1,0:T(8,128)S(1)}, f32[16,40,128]{2,1,0:T(8,128)S(1)}, u32[]{:S(2)}, u32[]{:S(2)}) collective-permute-start(f32[16,40,128]{2,1,0:T(8,128)S(1)} %all-to-all-done), channel_id=1, source_target_pairs={{0,16},{16,0},{1,17},{17,1},{2,18},{18,2},{3,19},{19,3},{4,20},{20... | collective-permute-start | bytes 983048 | tf_op jit(solution)/shard_map/ppermute | solution.py:346
  28.3 0.7 %copy-start.1 = (f32[16,40,128]{2,1,0:T(8,128)}, f32[16,40,128]{2,1,0:T(8,128)S(1)}, u32[]{:S(2)}) copy-start(f32[16,40,128]{2,1,0:T(8,128)S(1)} %collective-permute-done) | copy-start | bytes 983044
  33.8 18.3 %collective-permute-start.1 = (bf16[16,64,128]{2,1,0:T(8,128)(2,1)}, bf16[16,64,128]{2,1,0:T(8,128)(2,1)S(1)}, u32[]{:S(2)}, u32[]{:S(2)}) collective-permute-start(bf16[16,64,128]{2,1,0:T(8,128)(2,1)} %get-tuple-element.7.high_ref), channel_id=1, source_target_pairs={{0,1},{1,2},{2,3},{3,4},{4,5},{5,6},{6,7},{7,8},{8,9},{9,10},{10,1... | collective-permute-start | bytes 786440 | tf_op jit(solution)/shard_map/ppermute | solution.py:385
  36.0 16.1 %collective-permute-start.2 = (bf16[16,64,128]{2,1,0:T(8,128)(2,1)}, bf16[16,64,128]{2,1,0:T(8,128)(2,1)S(1)}, u32[]{:S(2)}, u32[]{:S(2)}) collective-permute-start(bf16[16,64,128]{2,1,0:T(8,128)(2,1)} %get-tuple-element.8.low_ref), channel_id=1, source_target_pairs={{1,0},{2,1},{3,2},{4,3},{5,4},{6,5},{7,6},{8,7},{9,8},{10,9},{11,1... | collective-permute-start | bytes 786440 | tf_op jit(solution)/shard_map/ppermute | solution.py:386
  52.1 0.7 %copy-start.2 = (bf16[16,64,128]{2,1,0:T(8,128)(2,1)}, bf16[16,64,128]{2,1,0:T(8,128)(2,1)S(1)}, u32[]{:S(2)}) copy-start(bf16[16,64,128]{2,1,0:T(8,128)(2,1)S(1)} %collective-permute-done.1.before_ref) | copy-start | bytes 786436
  52.1 0.8 %copy-start.3 = (bf16[16,64,128]{2,1,0:T(8,128)(2,1)}, bf16[16,64,128]{2,1,0:T(8,128)(2,1)S(1)}, u32[]{:S(2)}) copy-start(bf16[16,64,128]{2,1,0:T(8,128)(2,1)S(1)} %collective-permute-done.2.after_ref) | copy-start | bytes 786436
  58.1 1.7 %collective-permute-start.3 = (f32[64,128]{1,0:T(8,128)}, f32[64,128]{1,0:T(8,128)S(1)}, u32[]{:S(2)}, u32[]{:S(2)}) collective-permute-start(f32[64,128]{1,0:T(8,128)} %shard_map.94), channel_id=1, source_target_pairs={{0,16},{16,0},{1,17},{17,1},{2,18},{18,2},{3,19},{19,3},{4,20},{20... | collective-permute-start | bytes 98312 | tf_op jit(solution)/shard_map/ppermute | solution.py:428

commit v2 on v1

v2 whole, which is shorter than its diff:
```python
import functools
import math

import jax
import jax.numpy as jnp
from jax import lax
from jax.experimental import pallas as pl
from jax.experimental.pallas import tpu as pltpu
from jax.sharding import PartitionSpec as P

SECTOR_ANTENNAS = 64
FRAME_TONES = 128
PMAX = 64
NEARBY_COUNT = 8
CELL_SECTORS = 32
REACH = 16
EPSILON = 1e-06

LANES = 128
GROUP = 8
HALF = FRAME_TONES // 2
COARSE = HALF // GROUP

SIN_TERMS = tuple((-1.0) ** n / math.factorial(2 * n + 1) for n in range(6))
COS_TERMS = tuple((-1.0) ** n / math.factorial(2 * n) for n in range(8))


def polynomial(terms, square):
    total = terms[-1]
    for term in terms[-2::-1]:
        total = total * square + term
    return total


def quarter_cos_sin(x):
    square = x * x
    return polynomial(COS_TERMS, square), x * polynomial(SIN_TERMS, square)


def cos_sin_turns(turns):
    turns = turns - jnp.round(turns)
    c, s = quarter_cos_sin(math.pi * turns)
    return 1.0 - 2.0 * s * s, 2.0 * s * c


def times(x, y):
    return x[0] * y[0] - x[1] * y[1], x[0] * y[1] + x[1] * y[0]


def powers(base, count):
    found = {1: base}
    for n in range(2, count + 1):
        found[n] = times(found[n // 2], found[n - n // 2])
    return found


def lane_index(rows):
    return lax.broadcasted_iota(jnp.int32, (rows, LANES), 1)


def pack_kernel(
    scalar_ref, link_ref, count_ref, offset_ref, delay_ref, angle_ref, gain_ref, out_ref, x_ref, y_ref,
    *, link_total, capacity, stride,
):
    rows = delay_ref.shape[0]
    lower = scalar_ref[0] == 0
    c, s = quarter_cos_sin(angle_ref[...] * 0.5)
    x_ref[:rows, :] = jnp.where(lower, delay_ref[...], gain_ref[:, 0, :])
    y = jnp.where(lower, 2.0 * s * c, gain_ref[:, 1, :])
    y = pltpu.roll(y, PMAX, 1)
    late = lane_index(1) >= PMAX
    y_ref[: rows + 1, :] = jnp.zeros((rows + 1, LANES), jnp.float32)
    pltpu.store(y_ref.at[:rows, :], y, mask=jnp.broadcast_to(late, y.shape))
    pltpu.store(y_ref.at[1 : rows + 1, :], y, mask=jnp.broadcast_to(~late, y.shape))
    lane = lane_index(1)
    within = lane & (PMAX - 1)
    out_ref[...] = jnp.zeros_like(out_ref)
    empty = jnp.full((1, LANES), -1.0, jnp.float32)
    for owner in range(out_ref.shape[0] // stride):
        out_ref[owner * stride + capacity : owner * stride + capacity + 1, :] = empty
    link_bits = link_total.bit_length() - 1

    def step(slot, carry):
        last_owner, place, tags = carry
        link = link_ref[slot]
        owner = link >> link_bits
        fresh = owner != last_owner
        place = jnp.where(fresh, 0, place + 1)
        offset = offset_ref[slot]
        row = offset >> 7
        shift = offset & (LANES - 1)
        early = lane >= shift
        first = ((lane - shift) & (LANES - 1)) < PMAX
        x = jnp.where(early, x_ref[pl.ds(row, 1), :], x_ref[pl.ds(row + 1, 1), :])
        y = jnp.where(early, y_ref[pl.ds(row, 1), :], y_ref[pl.ds(row + 1, 1), :])
        both = pltpu.roll(jnp.where(first, x, y), (LANES - shift) & (LANES - 1), 1)
        both = jnp.where(within < count_ref[slot], both, 0.0)
        base = owner * stride
        out_ref[pl.ds(base + place, 1), :] = both
        local = (link - (owner << link_bits)).astype(jnp.float32)
        tags = jnp.where(fresh, -1.0, tags)
        tags = jnp.where(lane == place, local, tags)
        out_ref[pl.ds(base + capacity, 1), :] = tags
        return owner, place, tags

    lax.fori_loop(0, link_total, step, (jnp.int32(-1), jnp.int32(0), empty), unroll=8)


def find_sources(own_ref, table_ref, source_ref, sem, capacity, stride):
    senders = own_ref.shape[0] // stride
    tags = own_ref[pl.ds(capacity, senders, stride=stride), :].T
    rows = table_ref.shape[0]
    depth = min(pl.cdiv(capacity, GROUP) * GROUP, LANES)
    tags = tags[:depth]
    place = lax.broadcasted_iota(jnp.int32, (depth, LANES), 0)
    inside = place < capacity
    place = place.astype(jnp.float32)
    lane = lane_index(depth).astype(jnp.float32)
    totals = [jnp.zeros((depth, LANES), jnp.float32) for _ in range(rows)]
    for sender in range(senders):
        column = jnp.where(inside, jnp.broadcast_to(tags[:, sender : sender + 1], (depth, LANES)), -1.0)
        value = place + float(sender * stride)
        for n in range(rows):
            totals[n] += jnp.where(column == lane + float(n * LANES), value, 0.0)
    for n in range(rows):
        table_ref[n : n + 1, :] = jnp.sum(totals[n], axis=0, keepdims=True).astype(jnp.int32)
    copy = pltpu.make_async_copy(table_ref, source_ref, sem)
    copy.start()
    copy.wait()


def take_row(row, n, lower, own_ref, other_ref, even, odd):
    own = own_ref[pl.ds(row, 1), :]
    other = other_ref[pl.ds(row, 1), :]
    target = even if n % 2 == 0 else odd
    target[0, n // 2 : n // 2 + 1, :] = jnp.where(lower, own, other)
    target[1, n // 2 : n // 2 + 1, :] = jnp.where(lower, other, own)


def make_tables(even, odd, pairs, first_antenna, tables):
    fine, centre, last, near, far = tables
    spans = centre.shape[1] // pairs
    steps = far.shape[1] // pairs
    left = lane_index(GROUP) < PMAX
    for group in range(pairs // GROUP):
        rows = pl.ds(group * GROUP, GROUP)
        pieces = []
        for field in range(2):
            a, b = even[field, rows, :], odd[field, rows, :]
            pieces.append(jnp.where(left, a, pltpu.roll(b, PMAX, 1)))
            pieces.append(jnp.where(left, pltpu.roll(a, PMAX, 1), b))
        delay, sine, gain_re, gain_im = pieces

        def put(ref, n, count, value):
            at = pl.ds(group * GROUP * count + n, GROUP, stride=count) if count > 1 else rows
            ref[0, at, :] = value[0]
            ref[1, at, :] = value[1]

        def half_steps(half):
            whole = times(half, half)
            up = powers(whole, GROUP - 1)
            found = [half] + [times(half, up[n]) for n in range(1, GROUP)]
            return whole, found

        c, s = quarter_cos_sin(delay * (math.pi / FRAME_TONES))
        whole, found = half_steps((c, -s))
        for n in range(GROUP):
            put(fine, n, GROUP, found[n])
        top = found[GROUP - 1]
        wide = times(times(top, top), whole)
        value = top
        for n in range(spans):
            if n:
                value = times(value, wide)
            put(centre, n, spans, value)
        put(last, 0, 1, times(value, times(top, whole)))

        c, s = cos_sin_turns(sine * 0.25)
        whole, found = half_steps((c, -s))
        for n in range(GROUP):
            put(near, n, GROUP, found[n])
        top = found[GROUP - 1]
        wide = times(times(top, top), whole)
        c, s = cos_sin_turns(sine * (0.5 * first_antenna))
        value = times(times((gain_re, gain_im), (c, -s)), top)
        for n in range(steps):
            if n:
                value = times(value, wide)
            put(far, n, steps, value)


def both_sides(centre, fine):
    a, b = centre[0] * fine[0], centre[1] * fine[1]
    c, d = centre[0] * fine[1], centre[1] * fine[0]
    return (a - b, c + d), (a + b, d - c)


def sides_of(centre_ref, fine_ref, pair, spans):
    at = pl.ds(pl.multiple_of(pair * GROUP, GROUP), GROUP)
    fine = (fine_ref[0, at, :], fine_ref[1, at, :])
    found = []
    for n in range(spans):
        row = pl.ds(pair * spans + n, 1)
        found.extend(both_sides((centre_ref[0, row, :], centre_ref[1, row, :]), fine))
    return found


def stack(values, part):
    return jnp.concatenate([v[part] for v in values], axis=0).astype(jnp.bfloat16)


def pair_response(pair, tables, pairs):
    fine, centre, last, near, far = tables
    delay = sides_of(centre, fine, pair, centre.shape[1] // pairs)
    delay_re, delay_im = stack(delay, 0), stack(delay, 1)
    row = pl.ds(pair, 1)
    final = lax.broadcasted_iota(jnp.int32, (GROUP, LANES), 0) == GROUP - 1
    swapped = tuple(jnp.where(final, last[n, row, :], delay[1][n]) for n in range(2))
    head = [delay[0], swapped]
    low_re = jnp.concatenate([stack(head, 0), delay_re[2 * GROUP :]], axis=0)
    low_im = jnp.concatenate([stack(head, 1), delay_im[2 * GROUP :]], axis=0)
    tones = jnp.concatenate(
        [
            jnp.concatenate([delay_re, -delay_im], axis=1),
            jnp.concatenate([low_re, low_im], axis=1),
        ],
        axis=0,
    )
    spread = sides_of(far, near, pair, far.shape[1] // pairs)
    spread_re, spread_im = stack(spread, 0), stack(spread, 1)
    lane = lane_index(1)
    blocks = []
    for keep in (lane < PMAX, lane >= PMAX):
        keep = jnp.where(keep, 1.0, 0.0).astype(jnp.bfloat16)
        re, im = spread_re * keep, spread_im * keep
        blocks.append(jnp.concatenate([re, im], axis=1))
        blocks.append(jnp.concatenate([im, -re], axis=1))
    mixing = jnp.concatenate(blocks, axis=0)
    return lax.dot_general(
        mixing, tones, (((1,), (1,)), ((), ())), preferred_element_type=jnp.float32
    )


def tone_of_place(lane):
    place = lane & (HALF - 1)
    within = place & 15
    above = (place & ~15) + jnp.where(within < GROUP, within + GROUP, 15 - within)
    below = jnp.where(above == 0, HALF, above)
    return HALF + jnp.where(lane < HALF, above, -below)


def place_of_tone(lane):
    away = jnp.where(lane >= HALF, lane - HALF, (HALF - lane) & (HALF - 1))
    within = away & 15
    place = (away & ~15) + jnp.where(within >= GROUP, within - GROUP, 15 - within)
    return jnp.where(lane >= HALF, place, HALF + place)


def reorder(values, index):
    pieces = [
        jnp.take_along_axis(values[n : n + GROUP], index, axis=1)
        for n in range(0, values.shape[0], GROUP)
    ]
    return jnp.concatenate(pieces, axis=0)


def serve_kernel(
    scalar_ref, nearby_ref, slot_ref, own_ref, other_ref, symbol_ref, low_ref, high_ref,
    table_ref, source_ref, sem, even, odd, raw, symbols, *tables, portion, capacity, stride,
):
    users = slot_ref.shape[0]
    worker_index = scalar_ref[0]
    find_sources(own_ref, table_ref, source_ref, sem, capacity, stride)
    for user in range(users):
        link = user * NEARBY_COUNT + slot_ref[user]
        row = source_ref[user * NEARBY_COUNT // LANES, link & (LANES - 1)]
        take_row(row, user, worker_index == 0, own_ref, other_ref, even, odd)
    pairs = users // 2
    make_tables(even, odd, pairs, (worker_index * portion).astype(jnp.float32), tables)
    symbols[...] = reorder(symbol_ref[...].astype(jnp.float32), tone_of_place(lane_index(GROUP)))
    raw[...] = jnp.zeros_like(raw)
    first_sector = scalar_ref[1] * CELL_SECTORS

    def one_pair(pair, carry):
        response = pair_response(pair, tables, pairs).astype(jnp.bfloat16).astype(jnp.float32)
        for n in range(2):
            user = pair * 2 + n
            sym_re = symbols[pl.ds(user * 2, 1), :]
            sym_im = symbols[pl.ds(user * 2 + 1, 1), :]
            re = response[2 * n * portion : (2 * n + 1) * portion]
            im = response[(2 * n + 1) * portion : (2 * n + 2) * portion]
            sector = nearby_ref[slot_ref[user], user] - first_sector
            raw[sector, :portion, :] += re * sym_re + im * sym_im
            raw[sector, portion:, :] += re * sym_im - im * sym_re
        return carry

    lax.fori_loop(0, pairs, one_pair, 0, unroll=4)
    half = CELL_SECTORS // 2

    def finish(sector, out_ref, row):
        value = raw[sector]
        re, im = value[:portion], value[portion:]
        power = jnp.sum(re * re + im * im, axis=1, keepdims=True) * (1.0 / FRAME_TONES)
        scale = 1.0 / jnp.sqrt(power + EPSILON)
        out_ref[row, :portion, :] = (re * scale).astype(jnp.bfloat16)
        out_ref[row, portion:, :] = (im * scale).astype(jnp.bfloat16)

    def one_sector(row, carry):
        finish(row, low_ref, row)
        finish(row + half, high_ref, row)
        return carry

    lax.fori_loop(0, half, one_sector, 0, unroll=4)


def respond_kernel(
    scalar_ref, own_ref, other_ref, out_ref, table_ref, source_ref, sem, even, odd, *tables,
    portion, capacity, stride,
):
    pairs = out_ref.shape[0]
    worker_index = scalar_ref[0]

    @pl.when(pl.program_id(0) == 0)
    def _():
        find_sources(own_ref, table_ref, source_ref, sem, capacity, stride)

    first = pl.program_id(0) * pairs * 2
    for n in range(2 * pairs):
        link = first + n
        row = source_ref[link >> 7, link & (LANES - 1)]
        take_row(row, n, worker_index == 0, own_ref, other_ref, even, odd)
    make_tables(even, odd, pairs, (worker_index * portion).astype(jnp.float32), tables)

    def one_pair(pair, carry):
        out_ref[pair] = pair_response(pair, tables, pairs).astype(jnp.bfloat16)
        return carry

    lax.fori_loop(0, pairs, one_pair, 0, unroll=UNROLL)


def receive_kernel(
    scalar_ref, nearby_ref, response_ref, before_ref, low_ref, high_ref, after_ref, out_ref, remote,
    *, portion,
):
    @pl.when(pl.program_id(0) == 0)
    def _():
        place = 0
        for part in (before_ref, low_ref, high_ref, after_ref):
            for n in range(part.shape[0]):
                remote[place] = part[n].astype(jnp.float32)
                place += 1

    users = out_ref.shape[0] // 2
    first = pl.program_id(0) * users
    first_sector = scalar_ref[1] * CELL_SECTORS - REACH

    def one_user(user, carry):
        total_re = jnp.zeros((GROUP, LANES), jnp.float32)
        total_im = jnp.zeros((GROUP, LANES), jnp.float32)
        for k in range(NEARBY_COUNT):
            sector = nearby_ref[k, first + user] - first_sector
            pair = user * (NEARBY_COUNT // 2) + k // 2
            base = (k % 2) * 2 * portion
            value = response_ref[pair, base : base + 2 * portion, :].astype(jnp.float32)
            other = remote[sector]
            for n in range(0, portion, GROUP):
                re, im = value[n : n + GROUP], value[portion + n : portion + n + GROUP]
                o_re, o_im = other[n : n + GROUP], other[portion + n : portion + n + GROUP]
                total_re = total_re + (re * o_re - im * o_im)
                total_im = total_im + (re * o_im + im * o_re)
        scale = 1.0 / math.sqrt(SECTOR_ANTENNAS)
        out_ref[pl.ds(user * 2, 1), :] = jnp.sum(total_re, axis=0, keepdims=True) * scale
        out_ref[pl.ds(user * 2 + 1, 1), :] = jnp.sum(total_im, axis=0, keepdims=True) * scale
        return carry

    lax.fori_loop(0, users, one_user, 0, unroll=2)
    out_ref[...] = reorder(out_ref[...], place_of_tone(lane_index(GROUP)))


UNROLL = 4
VMEM = pl.BlockSpec(memory_space=pltpu.VMEM)
SMEM = pl.BlockSpec(memory_space=pltpu.SMEM)


def table_shapes(pairs, steps):
    counts = (GROUP, COARSE // 2, 1, GROUP, steps // 2)
    return [pltpu.VMEM((2, pairs * n, LANES), jnp.float32) for n in counts]


def link_scratch(link_total, pairs):
    return [
        pltpu.VMEM((link_total // LANES, LANES), jnp.int32),
        pltpu.SMEM((link_total // LANES, LANES), jnp.int32),
        pltpu.SemaphoreType.DMA,
        pltpu.VMEM((2, pairs, LANES), jnp.float32),
        pltpu.VMEM((2, pairs, LANES), jnp.float32),
    ]


LIMIT = pltpu.CompilerParams(vmem_limit_bytes=16 << 20)


def shards(
    path_delay,
    path_angle,
    path_gain,
    slot_counts,
    slot_offsets,
    ray_link,
    nearby_sectors,
    serving_slot,
    symbols,
):
    devices = lax.axis_size("cell")
    worker_count = lax.axis_size("grp")
    path_total = path_delay.shape[0]
    link_total = slot_counts.shape[0]
    total_users = serving_slot.shape[0]
    capacity = 2 * link_total // devices
    stride = pl.cdiv(capacity + 1, GROUP) * GROUP
    portion = SECTOR_ANTENNAS // worker_count
    steps = portion // GROUP
    scalar = jnp.stack([lax.axis_index("grp"), lax.axis_index("cell")]).astype(jnp.int32)
    swap = [(n, worker_count - 1 - n) for n in range(worker_count)]

    path_rows = path_total // LANES
    work_rows = pl.cdiv(path_rows + 1, GROUP) * GROUP
    packed = pl.pallas_call(
        functools.partial(
            pack_kernel, link_total=link_total, capacity=capacity, stride=stride
        ),
        out_shape=jax.ShapeDtypeStruct((devices * stride, LANES), jnp.float32),
        in_specs=[SMEM, SMEM, SMEM, SMEM, VMEM, VMEM, VMEM],
        out_specs=VMEM,
        scratch_shapes=[pltpu.VMEM((work_rows, LANES), jnp.float32)] * 2,
        compiler_params=LIMIT,
    )(
        scalar,
        ray_link,
        slot_counts,
        slot_offsets,
        path_delay.reshape(path_rows, LANES),
        path_angle.reshape(path_rows, LANES),
        path_gain.reshape(2, path_rows, LANES).transpose(1, 0, 2),
    )
    arrived = lax.all_to_all(
        packed.reshape(devices, stride, LANES), "cell", split_axis=0, concat_axis=0, tiled=True
    )
    other = lax.ppermute(arrived, "grp", swap)
    own_rows = arrived.reshape(devices * stride, LANES)
    other_rows = other.reshape(devices * stride, LANES)
    sizes = dict(portion=portion, capacity=capacity, stride=stride)

    half = CELL_SECTORS // 2
    part = jax.ShapeDtypeStruct((half, 2 * portion, LANES), jnp.bfloat16)
    serve_pairs = total_users // 2
    low, high = pl.pallas_call(
        functools.partial(serve_kernel, **sizes),
        out_shape=(part, part),
        in_specs=[SMEM, SMEM, SMEM, VMEM, VMEM, VMEM],
        out_specs=(VMEM, VMEM),
        scratch_shapes=link_scratch(link_total, serve_pairs)
        + [
            pltpu.VMEM((CELL_SECTORS, 2 * portion, LANES), jnp.float32),
            pltpu.VMEM((2 * total_users, LANES), jnp.float32),
        ]
        + table_shapes(serve_pairs, steps),
        compiler_params=LIMIT,
    )(
        scalar,
        nearby_sectors,
        serving_slot,
        own_rows,
        other_rows,
        symbols.reshape(2 * total_users, LANES),
    )

    up = [(n, n + 1) for n in range(devices - 1)]
    down = [(m, n) for n, m in up]
    before = lax.ppermute(high, "cell", up)
    after = lax.ppermute(low, "cell", down)

    pair_total = link_total // 2
    block = 16
    response = pl.pallas_call(
        functools.partial(respond_kernel, **sizes),
        out_shape=jax.ShapeDtypeStruct((pair_total, 4 * portion, LANES), jnp.bfloat16),
        grid=(pair_total // block,),
        in_specs=[SMEM, VMEM, VMEM],
        out_specs=pl.BlockSpec((block, 4 * portion, LANES), lambda n: (n, 0, 0)),
        scratch_shapes=link_scratch(link_total, block) + table_shapes(block, steps),
        cost_estimate=pl.CostEstimate(
            flops=pair_total * 2 * 128 * 128 * 256 * 40,
            bytes_accessed=pair_total * 4 * portion * LANES * 2,
            transcendentals=0,
        ),
        compiler_params=LIMIT,
    )(scalar, own_rows, other_rows)

    user_block = 8
    partial_value = pl.pallas_call(
        functools.partial(receive_kernel, portion=portion),
        out_shape=jax.ShapeDtypeStruct((2 * total_users, LANES), jnp.float32),
        grid=(total_users // user_block,),
        in_specs=[
            SMEM,
            SMEM,
            pl.BlockSpec(
                (user_block * NEARBY_COUNT // 2, 4 * portion, LANES), lambda n: (n, 0, 0)
            ),
            VMEM,
            VMEM,
            VMEM,
            VMEM,
        ],
        out_specs=pl.BlockSpec((2 * user_block, LANES), lambda n: (n, 0)),
        scratch_shapes=[
            pltpu.VMEM((CELL_SECTORS + 2 * REACH, 2 * portion, LANES), jnp.float32)
        ],
        compiler_params=LIMIT,
    )(scalar, nearby_sectors, response, before, low, high, after)
    summed = partial_value + lax.ppermute(partial_value, "grp", swap)
    return summed.reshape(total_users, 2, FRAME_TONES)


def solution(mesh):
    placed = (
        P("cell"),
        P("cell"),
        P(None, "cell"),
        P("cell"),
        P("cell"),
        P("cell"),
        P(None, "cell"),
        P("cell"),
        P("cell", None, None),
    )
    return jax.shard_map(
        shards, mesh=mesh, in_specs=placed, out_specs=P("cell", None, None), check_vma=False
    )
```

time: 61.8 us -> 57 us (0.922)
  blocking collectives: 0 us -> 14.9 us
  starting transfers between devices: 17.6 us -> 11.3 us
  other arithmetic: 6.4 us -> 0.69 us
  Pallas kernels: 26.3 us -> 21 us
  waiting for transfers between devices: 6.78 us -> 2.12 us
  local copies, waits for them, and re-layouts: 4.04 us -> 6.52 us
    all_to_all x0 -> x1, blocking collectives: none -> 14.9 us  [shards(): lax.all_to_all(packed.reshape(devices, stride, LANES), 'cell', split_axis...]
    all_to_all x1 -> x0, starting transfers between devices: 6.66 us -> none  [shards(): lax.all_to_all(packed.reshape(devices, stride, LANES), 'cell', split_axis...]
    all_to_all x1 -> x0, waiting for transfers between devices: 5.7 us -> none  [shards(): lax.all_to_all(packed.reshape(devices, stride, LANES), 'cell', split_axis...]
    unnamed x8 -> x20, local copies, waits for them, and re-layouts: 1.52 us -> 6.52 us
    reduce_sum x3 -> x0, other arithmetic: 2.76 us -> none  [the longest x2 1.48 us: find(): jnp.sum(jnp.where(links[:, None] == tags[None, :], slot_rows[None, :], 0)...]
    pallas_call x1, Pallas kernels: 5.2 us -> 3.01 us  [shards(): pl.pallas_call(functools.partial(receive_kernel, portion=portion), out_sh...]
    pallas_call x2, Pallas kernels: 16 us -> 14.3 us  [the longest x1 11 us: shards(): pl.pallas_call(functools.partial(respond_kernel, **sizes), out_shape=jax....]
    pallas_call x1, Pallas kernels: 5.12 us -> 3.72 us  [shards(): pl.pallas_call(functools.partial(pack_kernel, link_total=link_total, capa...]
  transfers between devices with their start and end apart: 5 -> 4, of which waited for: 2 -> 2; matrix products, arithmetic and copies ran while one was open for 7% -> 0% of each run, Pallas kernels for 18% -> 19%
where the time goes in v2:
time: 57 us; the launch traced here: 56.5 us
  Pallas kernels  21 us (37%)
  blocking collectives  14.9 us (26%)
  starting transfers between devices  11.3 us (20%)
  local copies, waits for them, and re-layouts  6.52 us (11%)
  waiting for transfers between devices  2.12 us (4%)
  other arithmetic  0.69 us (1%)
    all_to_all x1, blocking collectives, shards(): lax.all_to_all(packed.reshape(devices, stride, LANES), 'cell', split_axis...  14.9 us
    pallas_call x1, Pallas kernels, shards(): pl.pallas_call(functools.partial(respond_kernel, **sizes), out_shape=jax....  11 us
    unnamed x20, local copies, waits for them, and re-layouts  6.52 us
    ppermute x1, starting transfers between devices, shards(): after = lax.ppermute(low, 'cell', down)  4.89 us
    pallas_call x1, Pallas kernels, shards(): pl.pallas_call(functools.partial(pack_kernel, link_total=link_total, capa...  3.72 us
    pallas_call x1, Pallas kernels, shards(): pl.pallas_call(functools.partial(serve_kernel, **sizes), out_shape=(part,...  3.28 us
    ppermute x1, starting transfers between devices, shards(): other = lax.ppermute(arrived, 'grp', swap)  3.23 us
    pallas_call x1, Pallas kernels, shards(): pl.pallas_call(functools.partial(receive_kernel, portion=portion), out_sh...  3.01 us
  transfers between devices with their start and end apart: 4, of which 2 were waited for; matrix products, arithmetic and copies ran while one was open for 0% of the time, Pallas kernels for 19%

profile of v2, /device:TPU:9, one launch (start us, length us, event | category | flops | bytes accessed | tf_op | source)
XLA Modules:
  0.0 56.5 jit_solution(11180082485644602389)
XLA Ops:
  0.0 0.1 pad_add_fusion.scalar_ref
  0.1 0.9 %copy-done = f32[2,8320]{1,0:T(2,128)S(1)} copy-done((f32[2,8320]{1,0:T(2,128)S(1)}, f32[2,8320]{1,0:T(2,128)}, u32[]{:S(2)}) %copy-start) | copy-done | bytes 66584
  1.0 0.8 %copy-done.1 = f32[8320]{0:T(1024)S(1)} copy-done((f32[8320]{0:T(1024)S(1)}, f32[8320]{0:T(1024)}, u32[]{:S(2)}) %copy-start.1) | copy-done | bytes 33304
  1.7 0.8 %copy-done.2 = f32[8320]{0:T(1024)S(1)} copy-done((f32[8320]{0:T(1024)S(1)}, f32[8320]{0:T(1024)}, u32[]{:S(2)}) %copy-start.2) | copy-done | bytes 33304
  2.5 0.7 %copy-done.6 = s32[256]{0:T(256)S(1)} copy-done((s32[256]{0:T(256)S(1)}, s32[256]{0:T(256)}, u32[]{:S(2)}) %copy-start.6) | copy-done | bytes 1048
  3.2 0.7 %copy-done.7 = s32[256]{0:T(256)S(1)} copy-done((s32[256]{0:T(256)S(1)}, s32[256]{0:T(256)}, u32[]{:S(2)}) %copy-start.7) | copy-done | bytes 1048
  3.9 0.7 %copy-done.8 = s32[256]{0:T(256)S(1)} copy-done((s32[256]{0:T(256)S(1)}, s32[256]{0:T(256)}, u32[]{:S(2)}) %copy-start.8) | copy-done | bytes 1048
  4.5 3.7 %shard_map.91 = f32[640,128]{1,0:T(8,128)S(1)} custom-call(s32[2]{0:T(128)S(1)} %pad_add_fusion.scalar_ref, s32[256]{0:T(256)S(1)} %copy-done.6, s32[256]{0:T(256)S(1)} %copy-done.7, s32[256]{0:T(256)S(1)} %copy-done.8, f32[65,128]{1,0:T(8,128)S(1)} %bitcast.18, f32[65,128]{1,0:T(8,128)S(1)} %bitcast.19, f32[65,2,128]{2,1,0:T(2,128)S(1)} %bitcast.17), custom_call_target="tpu_custom_call" | custom-call | tf_op jit(solution)/shard_map/pallas_call | solution.py:428
  8.3 14.9 %all_to_all.5 = f32[16,40,128]{2,1,0:T(8,128)S(1)} all-to-all(f32[16,40,128]{2,1,0:T(8,128)S(1)} %bitcast.14), channel_id=1, replica_groups=mesh['grp'=2,'cell'=16] {'cell'}, dimensions={0} | all-to-all | bytes 655360 | tf_op jit(solution)/shard_map/all_to_all | solution.py:446
  23.1 3.2 %collective-permute-start = (f32[16,40,128]{2,1,0:T(8,128)S(1)}, f32[16,40,128]{2,1,0:T(8,128)S(1)}, u32[]{:S(2)}, u32[]{:S(2)}) collective-permute-start(f32[16,40,128]{2,1,0:T(8,128)S(1)} %all_to_all.5), channel_id=1, source_target_pairs={{0,16},{16,0},{1,17},{17,1},{2,18},{18,2},{3,19},{19,3},{4,20},{20... | collective-permute-start | bytes 983048 | tf_op jit(solution)/shard_map/ppermute | solution.py:449
  26.3 1.3 %collective-permute-done = f32[16,40,128]{2,1,0:T(8,128)S(1)} collective-permute-done((f32[16,40,128]{2,1,0:T(8,128)S(1)}, f32[16,40,128]{2,1,0:T(8,128)S(1)}, u32[]{:S(2)}, u32[]{:S(2)}) %collective-permute-start) | collective-permute-done | bytes 327712 | tf_op jit(solution)/shard_map/ppermute | solution.py:449
  27.6 0.7 %copy-done.3 = s32[8,32]{1,0:T(8,128)S(1)} copy-done((s32[8,32]{1,0:T(8,128)S(1)}, s32[8,32]{1,0:T(8,128)}, u32[]{:S(2)}) %copy-start.3) | copy-done | bytes 1048
  28.3 0.7 %copy-done.5 = bf16[32,2,128]{2,1,0:T(2,128)(2,1)S(1)} copy-done((bf16[32,2,128]{2,1,0:T(2,128)(2,1)S(1)}, bf16[32,2,128]{2,1,0:T(2,128)(2,1)}, u32[]{:S(2)}) %copy-start.5) | copy-done | bytes 16408
  29.0 0.7 %copy-done.9 = s32[32]{0:T(128)S(1)} copy-done((s32[32]{0:T(128)S(1)}, s32[32]{0:T(128)}, u32[]{:S(2)}) %copy-start.9) | copy-done | bytes 152
  29.7 3.3 %shard_map.93 = (bf16[16,64,128]{2,1,0:T(8,128)(2,1)S(1)}, bf16[16,64,128]{2,1,0:T(8,128)(2,1)S(1)}) custom-call(s32[2]{0:T(128)S(1)} %pad_add_fusion.scalar_ref, s32[8,32]{1,0:T(8,128)S(1)} %copy-done.3, s32[32]{0:T(128)S(1)} %copy-done.9, f32[640,128]{1,0:T(8,128)S(1)} %bitcast.12, f32[640,128]{1,0:T(8,128)S(1)} %bitcast.15, bf16[64,128]{1,0:T(8,128)(2,1)S(1)} %bitcast.20), custom_call_target="tpu_custom_call" | custom-call | tf_op jit(solution)/shard_map/pallas_call | solution.py:457
  32.9 2.2 %collective-permute-start.1 = (bf16[16,64,128]{2,1,0:T(8,128)(2,1)S(1)}, bf16[16,64,128]{2,1,0:T(8,128)(2,1)S(1)}, u32[]{:S(2)}, u32[]{:S(2)}) collective-permute-start(bf16[16,64,128]{2,1,0:T(8,128)(2,1)S(1)} %get-tuple-element.7.high_ref), channel_id=1, source_target_pairs={{0,1},{1,2},{2,3},{3,4},{4,5},{5,6},{6,7},{7,8},{8,9},{9,10},{10,1... | collective-permute-start | bytes 786440 | tf_op jit(solution)/shard_map/ppermute | solution.py:480
  35.1 0.0 copy-start.4
  35.2 4.9 %collective-permute-start.2 = (bf16[16,64,128]{2,1,0:T(8,128)(2,1)S(1)}, bf16[16,64,128]{2,1,0:T(8,128)(2,1)S(1)}, u32[]{:S(2)}, u32[]{:S(2)}) collective-permute-start(bf16[16,64,128]{2,1,0:T(8,128)(2,1)S(1)} %get-tuple-element.8.low_ref), channel_id=1, source_target_pairs={{1,0},{2,1},{3,2},{4,3},{5,4},{6,5},{7,6},{8,7},{9,8},{10,9},{11,1... | collective-permute-start | bytes 786440 | tf_op jit(solution)/shard_map/ppermute | solution.py:481
  40.1 11.0 %shard_map.92.response_ref = bf16[128,128,128]{2,1,0:T(8,128)(2,1)S(1)} custom-call(s32[2]{0:T(128)S(1)} %pad_add_fusion.scalar_ref, f32[640,128]{1,0:T(8,128)S(1)} %bitcast.13, f32[640,128]{1,0:T(8,128)S(1)} %bitcast.16), custom_call_target="tpu_custom_call" | custom-call | flops 42949672960 | bytes 4194304 | tf_op jit(solution)/shard_map/pallas_call | solution.py:485
  51.0 0.0 collective-permute-done.1.before_ref
  51.1 3.0 %shard_map.94 = f32[64,128]{1,0:T(8,128)S(1)} custom-call(s32[2]{0:T(128)S(1)} %pad_add_fusion.scalar_ref, s32[8,32]{1,0:T(8,128)S(1)} %copy-done.4, bf16[128,128,128]{2,1,0:T(8,128)(2,1)S(1)} %shard_map.92.response_ref, bf16[16,64,128]{2,1,0:T(8,128)(2,1)S(1)} %collective-permute-done.1.before_ref, bf16[16,64,128]{2,1,0:T(8,128)(2,1)S(1)} %get-tuple-element.8.low_ref, ...), custom_call_target="tpu_custom_call" | custom-call | tf_op jit(solution)/shard_map/pallas_call | solution.py:501
  54.1 1.0 %collective-permute-start.3 = (f32[64,128]{1,0:T(8,128)S(1)}, f32[64,128]{1,0:T(8,128)S(1)}, u32[]{:S(2)}, u32[]{:S(2)}) collective-permute-start(f32[64,128]{1,0:T(8,128)S(1)} %shard_map.94), channel_id=1, source_target_pairs={{0,16},{16,0},{1,17},{17,1},{2,18},{18,2},{3,19},{19,3},{4,20},{20... | collective-permute-start | bytes 98312 | tf_op jit(solution)/shard_map/ppermute | solution.py:522
  55.1 0.9 %collective-permute-done.3 = f32[64,128]{1,0:T(8,128)S(1)} collective-permute-done((f32[64,128]{1,0:T(8,128)S(1)}, f32[64,128]{1,0:T(8,128)S(1)}, u32[]{:S(2)}, u32[]{:S(2)}) %collective-permute-start.3) | collective-permute-done | bytes 32800 | tf_op jit(solution)/shard_map/ppermute | solution.py:522
  55.9 0.6 %add.3 = f32[64,128]{1,0:T(8,128)} add(f32[64,128]{1,0:T(8,128)S(1)} %shard_map.94, f32[64,128]{1,0:T(8,128)S(1)} %collective-permute-done.3) | non-fusion elementwise | flops 8192 | bytes 98304 | tf_op jit(solution)/shard_map/add | solution.py:522
  (11 shorter events, 0.0 us)
Async XLA Ops:
  0.1 0.9 %copy-start = (f32[2,8320]{1,0:T(2,128)S(1)}, f32[2,8320]{1,0:T(2,128)}, u32[]{:S(2)}) copy-start(f32[2,8320]{1,0:T(2,128)} %param.11) | copy-start | bytes 199684
  1.0 0.8 %copy-start.1 = (f32[8320]{0:T(1024)S(1)}, f32[8320]{0:T(1024)}, u32[]{:S(2)}) copy-start(f32[8320]{0:T(1024)} %param.9) | copy-start | bytes 99844
  1.7 0.8 %copy-start.2 = (f32[8320]{0:T(1024)S(1)}, f32[8320]{0:T(1024)}, u32[]{:S(2)}) copy-start(f32[8320]{0:T(1024)} %param.10) | copy-start | bytes 99844
  2.5 0.7 %copy-start.6 = (s32[256]{0:T(256)S(1)}, s32[256]{0:T(256)}, u32[]{:S(2)}) copy-start(s32[256]{0:T(256)} %link_ref.1) | copy-start | bytes 3076
  3.2 0.7 %copy-start.7 = (s32[256]{0:T(256)S(1)}, s32[256]{0:T(256)}, u32[]{:S(2)}) copy-start(s32[256]{0:T(256)} %count_ref.1) | copy-start | bytes 3076
  3.9 0.7 %copy-start.8 = (s32[256]{0:T(256)S(1)}, s32[256]{0:T(256)}, u32[]{:S(2)}) copy-start(s32[256]{0:T(256)} %offset_ref.1) | copy-start | bytes 3076
  23.1 4.5 %collective-permute-start = (f32[16,40,128]{2,1,0:T(8,128)S(1)}, f32[16,40,128]{2,1,0:T(8,128)S(1)}, u32[]{:S(2)}, u32[]{:S(2)}) collective-permute-start(f32[16,40,128]{2,1,0:T(8,128)S(1)} %all_to_all.5), channel_id=1, source_target_pairs={{0,16},{16,0},{1,17},{17,1},{2,18},{18,2},{3,19},{19,3},{4,20},{20... | collective-permute-start | bytes 983048 | tf_op jit(solution)/shard_map/ppermute | solution.py:449
  27.6 0.7 %copy-start.3 = (s32[8,32]{1,0:T(8,128)S(1)}, s32[8,32]{1,0:T(8,128)}, u32[]{:S(2)}) copy-start(s32[8,32]{1,0:T(8,128)} %nearby_ref.3) | copy-start | bytes 3076
  28.3 0.7 %copy-start.5 = (bf16[32,2,128]{2,1,0:T(2,128)(2,1)S(1)}, bf16[32,2,128]{2,1,0:T(2,128)(2,1)}, u32[]{:S(2)}) copy-start(bf16[32,2,128]{2,1,0:T(2,128)(2,1)} %param.17) | copy-start | bytes 49156
  29.0 0.7 %copy-start.9 = (s32[32]{0:T(128)S(1)}, s32[32]{0:T(128)}, u32[]{:S(2)}) copy-start(s32[32]{0:T(128)} %slot_ref.1) | copy-start | bytes 388
  32.9 18.1 %collective-permute-start.1 = (bf16[16,64,128]{2,1,0:T(8,128)(2,1)S(1)}, bf16[16,64,128]{2,1,0:T(8,128)(2,1)S(1)}, u32[]{:S(2)}, u32[]{:S(2)}) collective-permute-start(bf16[16,64,128]{2,1,0:T(8,128)(2,1)S(1)} %get-tuple-element.7.high_ref), channel_id=1, source_target_pairs={{0,1},{1,2},{2,3},{3,4},{4,5},{5,6},{6,7},{7,8},{8,9},{9,10},{10,1... | collective-permute-start | bytes 786440 | tf_op jit(solution)/shard_map/ppermute | solution.py:480
  35.1 15.9 %copy-start.4 = (s32[8,32]{1,0:T(8,128)S(1)}, s32[8,32]{1,0:T(8,128)}, u32[]{:S(2)}) copy-start(s32[8,32]{1,0:T(8,128)} %nearby_ref.3) | copy-start | bytes 3076
  35.2 15.9 %collective-permute-start.2 = (bf16[16,64,128]{2,1,0:T(8,128)(2,1)S(1)}, bf16[16,64,128]{2,1,0:T(8,128)(2,1)S(1)}, u32[]{:S(2)}, u32[]{:S(2)}) collective-permute-start(bf16[16,64,128]{2,1,0:T(8,128)(2,1)S(1)} %get-tuple-element.8.low_ref), channel_id=1, source_target_pairs={{1,0},{2,1},{3,2},{4,3},{5,4},{6,5},{7,6},{8,7},{9,8},{10,9},{11,1... | collective-permute-start | bytes 786440 | tf_op jit(solution)/shard_map/ppermute | solution.py:481
  54.1 1.8 %collective-permute-start.3 = (f32[64,128]{1,0:T(8,128)S(1)}, f32[64,128]{1,0:T(8,128)S(1)}, u32[]{:S(2)}, u32[]{:S(2)}) collective-permute-start(f32[64,128]{1,0:T(8,128)S(1)} %shard_map.94), channel_id=1, source_target_pairs={{0,16},{16,0},{1,17},{17,1},{2,18},{18,2},{3,19},{19,3},{4,20},{20... | collective-permute-start | bytes 98312 | tf_op jit(solution)/shard_map/ppermute | solution.py:522

commit v3 on v2

v3 whole, which is shorter than its diff:
```python
import functools
import math

import jax
import jax.numpy as jnp
from jax import lax
from jax.experimental import pallas as pl
from jax.experimental.pallas import tpu as pltpu
from jax.sharding import PartitionSpec as P

SECTOR_ANTENNAS = 64
FRAME_TONES = 128
PMAX = 64
NEARBY_COUNT = 8
CELL_SECTORS = 32
REACH = 16
EPSILON = 1e-06

LANES = 128
GROUP = 8
HALF = FRAME_TONES // 2
SPANS = HALF // (2 * GROUP)
LEVELS = 32767.0
DELAY_STEP = 64.0 / 65535.0
SYMBOL_TOP = 4.0

SIN_TERMS = tuple((-1.0) ** n / math.factorial(2 * n + 1) for n in range(6))
COS_TERMS = tuple((-1.0) ** n / math.factorial(2 * n) for n in range(8))


def polynomial(terms, square):
    total = terms[-1]
    for term in terms[-2::-1]:
        total = total * square + term
    return total


def quarter_cos_sin(x):
    square = x * x
    return polynomial(COS_TERMS, square), x * polynomial(SIN_TERMS, square)


def cos_sin_turns(turns):
    turns = turns - jnp.round(turns)
    c, s = quarter_cos_sin(math.pi * turns)
    return 1.0 - 2.0 * s * s, 2.0 * s * c


def times(x, y):
    return x[0] * y[0] - x[1] * y[1], x[0] * y[1] + x[1] * y[0]


def powers(base, count):
    found = {1: base}
    for n in range(2, count + 1):
        found[n] = times(found[n // 2], found[n - n // 2])
    return found


def join(high, low):
    return (high.astype(jnp.int32) << 16) | (low.astype(jnp.int32) & 0xFFFF)


def split(word):
    return (word >> 16).astype(jnp.float32), ((word << 16) >> 16).astype(jnp.float32)


def root_code(value):
    root = jnp.sqrt(jnp.sqrt(jnp.sqrt(jnp.abs(value)))) * LEVELS
    return jnp.round(jnp.where(value < 0, -root, root))


def root_value(code):
    unit = code * (1.0 / LEVELS)
    power = unit * unit
    power = power * power
    power = power * power
    return jnp.where(code < 0, -power, power)


def lane_index(rows):
    return lax.broadcasted_iota(jnp.int32, (rows, LANES), 1)


def fetch(pairs, sems):
    copies = [pltpu.make_async_copy(a, b, sems.at[n]) for n, (a, b) in enumerate(pairs)]
    for copy in copies:
        copy.start()
    return copies


def pack_kernel(
    link_hbm, count_hbm, offset_hbm, delay_hbm, angle_hbm, gain_hbm, out_ref,
    link_ref, count_ref, offset_ref, delay_ref, angle_ref, gain_ref, word_ref, sems,
    *, link_total, capacity, stride,
):
    copies = fetch(
        [
            (link_hbm, link_ref),
            (count_hbm, count_ref),
            (offset_hbm, offset_ref),
            (delay_hbm, delay_ref),
            (angle_hbm, angle_ref),
            (gain_hbm, gain_ref),
        ],
        sems,
    )
    lane = lane_index(1)
    out_ref[...] = jnp.zeros_like(out_ref)
    empty = jnp.full((1, LANES), -1, jnp.int32)
    tag_row = capacity // 2
    for owner in range(out_ref.shape[0] // stride):
        out_ref[owner * stride + tag_row : owner * stride + tag_row + 1, :] = empty
    for copy in copies:
        copy.wait()
    rows = delay_ref.shape[0]
    lower = lax.axis_index("grp") == 0
    c, s = quarter_cos_sin(angle_ref[...] * 0.5)
    gain_re, gain_im = gain_ref[:, 0, :], gain_ref[:, 1, :]
    high = jnp.where(lower, jnp.round(delay_ref[...] * (1.0 / DELAY_STEP)) - 32768.0, root_code(gain_re))
    low = jnp.where(lower, jnp.round(2.0 * LEVELS * s * c), root_code(gain_im))
    word_ref[:rows, :] = join(high, low)
    link_bits = link_total.bit_length() - 1

    def step(slot, carry):
        last_owner, place, tags = carry
        link = link_ref[slot]
        owner = link >> link_bits
        fresh = owner != last_owner
        place = jnp.where(fresh, 0, place + 1)
        offset = offset_ref[slot]
        row = offset >> 7
        shift = offset & (LANES - 1)
        word = jnp.where(lane >= shift, word_ref[pl.ds(row, 1), :], word_ref[pl.ds(row + 1, 1), :])
        start = (place & 1) * PMAX
        word = pltpu.roll(word, (start - shift) & (LANES - 1), 1)
        within = lane - start
        live = (within >= 0) & (within < count_ref[slot])
        base = owner * stride
        pltpu.store(out_ref.at[pl.ds(base + (place >> 1), 1), :], word, mask=live)
        tags = jnp.where(fresh, -1, tags)
        tags = jnp.where(lane == place, link - (owner << link_bits), tags)
        out_ref[pl.ds(base + tag_row, 1), :] = tags
        return owner, place, tags

    lax.fori_loop(0, link_total, step, (jnp.int32(-1), jnp.int32(0), empty), unroll=16)


def find_rows(own_ref, table_ref, capacity, stride):
    total_rows = own_ref.shape[0]
    senders = total_rows // stride
    tags = own_ref[pl.ds(capacity // 2, senders, stride=stride), :].astype(jnp.float32).T
    depth = min(pl.cdiv(capacity, GROUP) * GROUP, LANES)
    tags = tags[:depth]
    place = lax.broadcasted_iota(jnp.int32, (depth, LANES), 0)
    inside = place < capacity
    lane = lane_index(depth)
    value = ((place >> 1) + total_rows * ((place ^ lane) & 1)).astype(jnp.float32)
    lane = lane.astype(jnp.float32)
    rows = table_ref.shape[0]
    totals = [jnp.zeros((depth, LANES), jnp.float32) for _ in range(rows)]
    for sender in range(senders):
        column = jnp.broadcast_to(tags[:, sender : sender + 1], (depth, LANES))
        column = jnp.where(inside, column, -1.0)
        here = value + float(sender * stride)
        for n in range(rows):
            totals[n] += jnp.where(column == lane + float(n * LANES), here, 0.0)
    for n in range(rows):
        table_ref[n : n + 1, :] = jnp.sum(totals[n], axis=0, keepdims=True).astype(jnp.int32)


def sort_kernel(
    nearby_hbm, slot_hbm, symbol_hbm, own_ref, other_ref, rows_ref, table_ref, list_ref,
    nearby_ref, slot_ref, symbol_ref, place_ref, sems, *, capacity, stride,
):
    copies = fetch(
        [(nearby_hbm, nearby_ref), (slot_hbm, slot_ref), (symbol_hbm, symbol_ref)], sems
    )
    find_rows(own_ref, table_ref, capacity, stride)
    copies += fetch([(table_ref, place_ref)], sems.at[pl.ds(3, 1)])
    total_rows = own_ref.shape[0]
    lower = lax.axis_index("grp") == 0
    own, other = own_ref[...], other_ref[...]
    for n, words in enumerate((jnp.where(lower, own, other), jnp.where(lower, other, own))):
        rows_ref[n, :total_rows, :] = words
        rows_ref[n, total_rows:, :] = pltpu.roll(words, PMAX, 1)
    for copy in copies:
        copy.wait()
    users = slot_ref.shape[0]
    pairs = users // 2
    left = lane_index(1) < PMAX
    lane = lane_index(1)
    sectors = jnp.zeros((1, LANES), jnp.int32)
    first_sector = lax.axis_index("cell") * CELL_SECTORS
    for pair in range(pairs):
        found = []
        for user in (2 * pair, 2 * pair + 1):
            slot = slot_ref[user]
            link = user * NEARBY_COUNT + slot
            row = place_ref[user * NEARBY_COUNT // LANES, link & (LANES - 1)]
            turned = jnp.where(row < total_rows, row + total_rows, row - total_rows)
            found.append(jnp.where(((slot ^ user) & 1) == 0, row, turned))
            sectors = jnp.where(lane == user, nearby_ref[slot, user] - first_sector, sectors)
        for n in range(2):
            even = rows_ref[n, pl.ds(found[0], 1), :]
            odd = rows_ref[n, pl.ds(found[1], 1), :]
            list_ref[n * pairs + pair : n * pairs + pair + 1, :] = jnp.where(left, even, odd)
    symbols = symbol_ref[...].astype(jnp.float32) * (1.0 / SYMBOL_TOP)
    code_ref = list_ref.at[2 * pairs : 2 * pairs + users, :]
    codes = root_code(symbols).reshape(users, 2, LANES)
    code_ref[...] = join(codes[:, 0, :], codes[:, 1, :])
    base = 2 * pairs + users
    list_ref[base : base + GROUP, :] = jnp.broadcast_to(sectors, (GROUP, LANES))


def make_tables(words_ref, groups, first_antenna, tables):
    fine, centre, last, near, far = tables
    steps = far.shape[1] // last.shape[1]
    for group in groups:
        rows = pl.ds(group * GROUP, GROUP)
        delay, sine = split(words_ref[0, rows, :])
        delay = (delay + 32768.0) * DELAY_STEP
        sine = sine * (1.0 / LEVELS)
        gain_re, gain_im = (root_value(code) for code in split(words_ref[1, rows, :]))

        def put(ref, n, count, value):
            at = pl.ds(group * (GROUP * count) + n, GROUP, stride=count) if count > 1 else rows
            ref[0, at, :] = value[0]
            ref[1, at, :] = value[1]

        def half_steps(half):
            whole = times(half, half)
            up = powers(whole, GROUP - 1)
            return whole, [half] + [times(half, up[n]) for n in range(1, GROUP)]

        c, s = quarter_cos_sin(delay * (math.pi / FRAME_TONES))
        whole, found = half_steps((c, -s))
        for n in range(GROUP):
            put(fine, n, GROUP, found[n])
        top = found[GROUP - 1]
        wide = times(times(top, top), whole)
        value = top
        for n in range(SPANS):
            if n:
                value = times(value, wide)
            put(centre, n, SPANS, value)
        put(last, 0, 1, times(value, times(top, whole)))

        c, s = cos_sin_turns(sine * 0.25)
        whole, found = half_steps((c, -s))
        for n in range(GROUP):
            put(near, n, GROUP, found[n])
        top = found[GROUP - 1]
        wide = times(times(top, top), whole)
        c, s = cos_sin_turns(sine * (0.5 * first_antenna))
        value = times(times((gain_re, gain_im), (c, -s)), top)
        for n in range(steps):
            if n:
                value = times(value, wide)
            put(far, n, steps, value)


def both_sides(centre, fine):
    a, b = centre[0] * fine[0], centre[1] * fine[1]
    c, d = centre[0] * fine[1], centre[1] * fine[0]
    return (a - b, c + d), (a + b, d - c)


def sides_of(centre_ref, fine_ref, pair, spans):
    at = pl.ds(pl.multiple_of(pair * GROUP, GROUP), GROUP)
    fine = (fine_ref[0, at, :], fine_ref[1, at, :])
    found = []
    for n in range(spans):
        row = pl.ds(pair * spans + n, 1)
        found.extend(both_sides((centre_ref[0, row, :], centre_ref[1, row, :]), fine))
    return found


def stack(values, part):
    return jnp.concatenate([v[part] for v in values], axis=0).astype(jnp.bfloat16)


def build_operands(pair, tables, tone_ref, mix_ref):
    fine, centre, last, near, far = tables
    delay = sides_of(centre, fine, pair, SPANS)
    row = pl.ds(pair, 1)
    final = lax.broadcasted_iota(jnp.int32, (GROUP, LANES), 0) == GROUP - 1
    steps = far.shape[1] // last.shape[1]
    spread = sides_of(far, near, pair, steps)
    portion = mix_ref.shape[0] // 2
    for n in range(2):
        tone_ref[n * HALF : (n + 1) * HALF, :] = stack(delay, n)
        swapped = jnp.where(final, last[n, row, :], delay[1][n])
        head = jnp.concatenate([delay[0][n], swapped], axis=0).astype(jnp.bfloat16)
        at = 2 * HALF + 2 * GROUP * n
        tone_ref[at : at + 2 * GROUP, :] = head
        mix_ref[n * portion : (n + 1) * portion, :] = stack(spread, n)


def multiply_operands(tone_ref, mix_ref):
    re, im = tone_ref[:HALF, :], tone_ref[HALF : 2 * HALF, :]
    head = [tone_ref[2 * HALF + 2 * GROUP * n : 2 * HALF + 2 * GROUP * (n + 1), :] for n in range(2)]
    low_re = jnp.concatenate([head[0], re[2 * GROUP :]], axis=0)
    low_im = jnp.concatenate([head[1], im[2 * GROUP :]], axis=0)
    tones = jnp.concatenate(
        [jnp.concatenate([re, -im], axis=1), jnp.concatenate([low_re, low_im], axis=1)], axis=0
    )
    portion = mix_ref.shape[0] // 2
    spread_re, spread_im = mix_ref[:portion, :], mix_ref[portion:, :]
    lane = lane_index(1)
    blocks = []
    for keep in (lane < PMAX, lane >= PMAX):
        keep = jnp.where(keep, 1.0, 0.0).astype(jnp.bfloat16)
        a, b, c = spread_re * keep, spread_im * keep, spread_re * -keep
        blocks.append(jnp.concatenate([a, b], axis=1))
        blocks.append(jnp.concatenate([b, c], axis=1))
    return lax.dot_general(
        jnp.concatenate(blocks, axis=0),
        tones,
        (((1,), (1,)), ((), ())),
        preferred_element_type=jnp.float32,
    )


def all_responses(pairs, tables, buffers, emit):
    tone_a, mix_a, tone_b, mix_b = buffers
    block = tone_a.shape[0]
    blocks = pairs // block

    def build(index, tone_ref, mix_ref):
        for n in range(block):
            build_operands(index * block + n, tables, tone_ref.at[n], mix_ref.at[n])

    def multiply(index, tone_ref, mix_ref):
        for n in range(block):
            emit(index * block + n, multiply_operands(tone_ref.at[n], mix_ref.at[n]))

    build(0, tone_a, mix_a)

    def step(n, carry):
        once = jnp.minimum(n + 1, 1)

        def first(_, carry):
            multiply(2 * n, tone_a, mix_a)
            build(2 * n + 1, tone_b, mix_b)
            return carry

        def second(_, carry):
            multiply(2 * n + 1, tone_b, mix_b)
            build(jnp.minimum(2 * n + 2, blocks - 1), tone_a, mix_a)
            return carry

        lax.fori_loop(0, once, first, 0)
        lax.fori_loop(0, once, second, 0)
        return carry

    lax.fori_loop(0, blocks // 2, step, 0)


def tone_of_place(lane):
    place = lane & (HALF - 1)
    within = place & 15
    above = (place & ~15) + jnp.where(within < GROUP, within + GROUP, 15 - within)
    below = jnp.where(above == 0, HALF, above)
    return HALF + jnp.where(lane < HALF, above, -below)


def place_of_tone(lane):
    away = jnp.where(lane >= HALF, lane - HALF, (HALF - lane) & (HALF - 1))
    within = away & 15
    place = (away & ~15) + jnp.where(within >= GROUP, within - GROUP, 15 - within)
    return jnp.where(lane >= HALF, place, HALF + place)


def reorder(values, index):
    pieces = [
        jnp.take_along_axis(values[n : n + GROUP], index, axis=1)
        for n in range(0, values.shape[0], GROUP)
    ]
    return jnp.concatenate(pieces, axis=0)


def respond_kernel(rows_ref, table_ref, out_ref, place_ref, words, sem, *scratch, portion):
    tables, buffers = scratch[:5], scratch[5:]
    for copy in fetch([(table_ref, place_ref)], sem):
        copy.wait()
    pairs = out_ref.shape[0]
    left = lane_index(1) < PMAX
    chunk = 16

    def take(index, carry):
        first = index * (2 * chunk)
        row = first >> 7
        base = first & (LANES - 1)
        for n in range(chunk):
            even = place_ref[row, base + 2 * n]
            odd = place_ref[row, base + 2 * n + 1]
            for field in range(2):
                value = jnp.where(
                    left, rows_ref[field, pl.ds(even, 1), :], rows_ref[field, pl.ds(odd, 1), :]
                )
                words[field, pl.ds(index * chunk + n, 1), :] = value
        return carry

    lax.fori_loop(0, pairs // chunk, take, 0)
    first_antenna = (lax.axis_index("grp") * portion).astype(jnp.float32)
    batch = 4

    def tabulate(index, carry):
        make_tables(words, [index * batch + n for n in range(batch)], first_antenna, tables)
        return carry

    lax.fori_loop(0, pairs // (GROUP * batch), tabulate, 0)

    def emit(pair, response):
        out_ref[pair] = response

    all_responses(pairs, tables, buffers, emit)


def receive_kernel(
    nearby_hbm, slot_hbm, symbol_hbm, response_ref, first_ref, second_ref, out_ref,
    nearby_ref, slot_ref, symbol_ref, sector_ref, sems, words, symbols, remote, *scratch, portion,
):
    tables, buffers = scratch[:5], scratch[5:]
    users = nearby_hbm.shape[1]
    pairs = users // 2
    base = 2 * pairs + users
    copies = fetch(
        [
            (nearby_hbm, nearby_ref),
            (slot_hbm, slot_ref),
            (symbol_hbm, symbol_ref),
            (first_ref.at[base : base + 1, :], sector_ref.at[0:1, :]),
            (second_ref.at[base : base + 1, :], sector_ref.at[1:2, :]),
        ],
        sems,
    )
    remote[...] = jnp.zeros_like(remote)
    order = tone_of_place(lane_index(GROUP))
    for n, ref in enumerate((first_ref, second_ref)):
        for field in range(2):
            words[field, n * pairs : (n + 1) * pairs, :] = ref[field * pairs : (field + 1) * pairs, :]
        codes = split(ref[2 * pairs : 2 * pairs + users, :])
        for part in range(2):
            symbols[part, n * users : (n + 1) * users, :] = reorder(
                root_value(codes[part]) * SYMBOL_TOP, order
            )
    first_antenna = (lax.axis_index("grp") * portion).astype(jnp.float32)
    make_tables(words, list(range(2 * pairs // GROUP)), first_antenna, tables)
    for copy in copies:
        copy.wait()
    own = reorder(symbol_ref[...].astype(jnp.float32), order).reshape(users, 2, LANES)
    for part in range(2):
        symbols[part, 2 * users :, :] = own[:, part, :]

    def contribute(place, row, re, im):
        sym_re = symbols[0, pl.ds(row, 1), :]
        sym_im = symbols[1, pl.ds(row, 1), :]
        remote[place, :portion, :] += re * sym_re + im * sym_im
        remote[place, portion:, :] += re * sym_im - im * sym_re

    window = CELL_SECTORS + 2 * REACH
    here = lax.axis_index("cell")
    first_sector = here * CELL_SECTORS - REACH

    def own_user(user, carry):
        slot = slot_ref[user]
        pair = user * (NEARBY_COUNT // 2) + (slot >> 1)
        at = pl.multiple_of((slot & 1) * (2 * portion), 2 * portion)
        re = response_ref[pair, pl.ds(at, portion), :]
        im = response_ref[pair, pl.ds(at + portion, portion), :]
        contribute(nearby_ref[slot, user] - first_sector, 2 * users + user, re, im)
        return carry

    lax.fori_loop(0, users, own_user, 0, unroll=2)
    after_first = (here & 1) == 0

    def emit(pair, response):
        for n in range(2):
            row = pair * 2 + n
            second = row >= users
            user = jnp.where(second, row - users, row)
            sector = sector_ref[jnp.where(second, 1, 0), user]
            place = jnp.where(second != after_first, sector + CELL_SECTORS, sector - CELL_SECTORS) + REACH
            place = jnp.where((place >= 0) & (place < window), place, window)
            re = response[2 * n * portion : (2 * n + 1) * portion]
            im = response[(2 * n + 1) * portion : (2 * n + 2) * portion]
            contribute(place, row, re, im)

    all_responses(2 * pairs, tables, buffers, emit)

    def normalise(sector, carry):
        value = remote[sector]
        re, im = value[:portion], value[portion:]
        power = jnp.sum(re * re + im * im, axis=1, keepdims=True) * (1.0 / FRAME_TONES)
        scale = 1.0 / jnp.sqrt(power + EPSILON)
        remote[sector, :portion, :] = (re * scale).astype(jnp.bfloat16).astype(jnp.float32)
        remote[sector, portion:, :] = (im * scale).astype(jnp.bfloat16).astype(jnp.float32)
        return carry

    lax.fori_loop(0, window, normalise, 0, unroll=8)

    def one_user(user, carry):
        total_re = jnp.zeros((GROUP, LANES), jnp.float32)
        total_im = jnp.zeros((GROUP, LANES), jnp.float32)
        for k in range(NEARBY_COUNT):
            sector = nearby_ref[k, user] - first_sector
            pair = user * (NEARBY_COUNT // 2) + k // 2
            at = (k % 2) * 2 * portion
            for n in range(0, portion, GROUP):
                re = response_ref[pair, at + n : at + n + GROUP, :]
                im = response_ref[pair, at + portion + n : at + portion + n + GROUP, :]
                other_re = remote[sector, n : n + GROUP, :]
                other_im = remote[sector, portion + n : portion + n + GROUP, :]
                total_re = total_re + (re * other_re - im * other_im)
                total_im = total_im + (re * other_im + im * other_re)
        scale = 1.0 / math.sqrt(SECTOR_ANTENNAS)
        out_ref[pl.ds(user * 2, 1), :] = jnp.sum(total_re, axis=0, keepdims=True) * scale
        out_ref[pl.ds(user * 2 + 1, 1), :] = jnp.sum(total_im, axis=0, keepdims=True) * scale
        return carry

    lax.fori_loop(0, users, one_user, 0, unroll=2)
    out_ref[...] = reorder(out_ref[...], place_of_tone(lane_index(GROUP)))


VMEM = pl.BlockSpec(memory_space=pltpu.VMEM)
HBM = pl.BlockSpec(memory_space=pltpu.HBM)
LIMIT = pltpu.CompilerParams(vmem_limit_bytes=16 << 20)
BLOCK = 8


def in_hbm(values):
    return pltpu.with_memory_space_constraint(values, pltpu.HBM)


def response_scratch(pairs, portion):
    counts = (GROUP, SPANS, 1, GROUP, portion // (2 * GROUP))
    tables = [pltpu.VMEM((2, pairs * n, LANES), jnp.float32) for n in counts]
    factors = [
        pltpu.VMEM((BLOCK, 2 * HALF + 4 * GROUP, LANES), jnp.bfloat16),
        pltpu.VMEM((BLOCK, 2 * portion, LANES), jnp.bfloat16),
    ]
    return tables + factors + factors


def shards(
    path_delay,
    path_angle,
    path_gain,
    slot_counts,
    slot_offsets,
    ray_link,
    nearby_sectors,
    serving_slot,
    symbols,
):
    devices = lax.axis_size("cell")
    worker_count = lax.axis_size("grp")
    path_total = path_delay.shape[0]
    link_total = slot_counts.shape[0]
    total_users = serving_slot.shape[0]
    capacity = 2 * link_total // devices
    stride = pl.cdiv(capacity // 2 + 1, GROUP) * GROUP
    portion = SECTOR_ANTENNAS // worker_count
    swap = [(n, worker_count - 1 - n) for n in range(worker_count)]
    path_rows = path_total // LANES
    link_rows = link_total // LANES
    sizes = dict(capacity=capacity, stride=stride)

    packed = pl.pallas_call(
        functools.partial(pack_kernel, link_total=link_total, **sizes),
        out_shape=jax.ShapeDtypeStruct((devices * stride, LANES), jnp.int32),
        in_specs=[HBM] * 6,
        out_specs=VMEM,
        scratch_shapes=[pltpu.SMEM((link_total,), jnp.int32)] * 3
        + [
            pltpu.VMEM((path_rows, LANES), jnp.float32),
            pltpu.VMEM((path_rows, LANES), jnp.float32),
            pltpu.VMEM((path_rows, 2, LANES), jnp.float32),
            pltpu.VMEM((pl.cdiv(path_rows + 1, GROUP) * GROUP, LANES), jnp.int32),
            pltpu.SemaphoreType.DMA((6,)),
        ],
        compiler_params=LIMIT,
    )(
        in_hbm(ray_link),
        in_hbm(slot_counts),
        in_hbm(slot_offsets),
        in_hbm(path_delay.reshape(path_rows, LANES)),
        in_hbm(path_angle.reshape(path_rows, LANES)),
        in_hbm(path_gain.reshape(2, path_rows, LANES).transpose(1, 0, 2)),
    )
    arrived = lax.all_to_all(
        packed.reshape(devices, stride, LANES), "cell", split_axis=0, concat_axis=0, tiled=True
    )
    other = lax.ppermute(arrived, "grp", swap)

    row_total = devices * stride
    list_rows = 2 * total_users + GROUP
    symbol_rows = in_hbm(symbols.reshape(2 * total_users, LANES))
    nearby_sectors = in_hbm(nearby_sectors)
    serving_slot = in_hbm(serving_slot)
    small_scratch = [
        pltpu.SMEM(nearby_sectors.shape, jnp.int32),
        pltpu.SMEM((total_users,), jnp.int32),
        pltpu.VMEM((2 * total_users, LANES), jnp.bfloat16),
    ]
    rows, table, listed = pl.pallas_call(
        functools.partial(sort_kernel, **sizes),
        out_shape=(
            jax.ShapeDtypeStruct((2, 2 * row_total, LANES), jnp.int32),
            jax.ShapeDtypeStruct((link_rows, LANES), jnp.int32),
            jax.ShapeDtypeStruct((list_rows, LANES), jnp.int32),
        ),
        in_specs=[HBM] * 3 + [VMEM] * 2,
        out_specs=(VMEM, VMEM, VMEM),
        scratch_shapes=small_scratch
        + [pltpu.SMEM((link_rows, LANES), jnp.int32), pltpu.SemaphoreType.DMA((4,))],
        compiler_params=LIMIT,
    )(
        nearby_sectors,
        serving_slot,
        symbol_rows,
        arrived.reshape(row_total, LANES),
        other.reshape(row_total, LANES),
    )

    def exchange(first):
        pairs = [(n, n + 1) for n in range(first, devices - 1, 2)]
        return lax.ppermute(listed, "cell", pairs + [(m, n) for n, m in pairs])

    first_list, second_list = exchange(0), exchange(1)

    pair_total = link_total // 2
    response = pl.pallas_call(
        functools.partial(respond_kernel, portion=portion),
        out_shape=jax.ShapeDtypeStruct((pair_total, 4 * portion, LANES), jnp.float32),
        in_specs=[VMEM, VMEM],
        out_specs=VMEM,
        scratch_shapes=[
            pltpu.SMEM((link_rows, LANES), jnp.int32),
            pltpu.VMEM((2, pair_total, LANES), jnp.int32),
            pltpu.SemaphoreType.DMA((1,)),
        ]
        + response_scratch(pair_total, portion),
        cost_estimate=pl.CostEstimate(
            flops=pair_total * 2 * 128 * 128 * 256 * 40,
            bytes_accessed=pair_total * 4 * portion * LANES * 2,
            transcendentals=0,
        ),
        compiler_params=LIMIT,
    )(rows, table)

    partial_value = pl.pallas_call(
        functools.partial(receive_kernel, portion=portion),
        out_shape=jax.ShapeDtypeStruct((2 * total_users, LANES), jnp.float32),
        in_specs=[HBM] * 3 + [VMEM] * 3,
        out_specs=VMEM,
        scratch_shapes=small_scratch
        + [
            pltpu.SMEM((2, LANES), jnp.int32),
            pltpu.SemaphoreType.DMA((5,)),
            pltpu.VMEM((2, total_users, LANES), jnp.int32),
            pltpu.VMEM((2, 3 * total_users, LANES), jnp.float32),
            pltpu.VMEM((CELL_SECTORS + 2 * REACH + 1, 2 * portion, LANES), jnp.float32),
        ]
        + response_scratch(total_users, portion),
        compiler_params=LIMIT,
    )(nearby_sectors, serving_slot, symbol_rows, response, first_list, second_list)
    summed = partial_value + lax.ppermute(partial_value, "grp", swap)
    return summed.reshape(total_users, 2, FRAME_TONES)


def solution(mesh):
    placed = (
        P("cell"),
        P("cell"),
        P(None, "cell"),
        P("cell"),
        P("cell"),
        P("cell"),
        P(None, "cell"),
        P("cell"),
        P("cell", None, None),
    )
    return jax.shard_map(
        shards, mesh=mesh, in_specs=placed, out_specs=P("cell", None, None), check_vma=False
    )
```

time: 57 us -> 42.1 us (0.74)
  local copies, waits for them, and re-layouts: 6.52 us -> 0 us
  starting transfers between devices: 11.3 us -> 7.98 us
  Pallas kernels: 21 us -> 18.6 us
  blocking collectives: 14.9 us -> 12.6 us
    unnamed x20 -> x0, local copies, waits for them, and re-layouts: 6.52 us -> none
    pallas_call x3, Pallas kernels: 18 us -> 12.4 us  [the longest x1 7.02 us: shards(): pl.pallas_call(functools.partial(respond_kernel, portion=portion), out_sh...]
    pallas_call x1, Pallas kernels: 3.01 us -> 6.17 us  [shards(): pl.pallas_call(functools.partial(receive_kernel, portion=portion), out_sh...]
    ppermute x2, starting transfers between devices: 7.08 us -> 4.19 us  [exchange(): return lax.ppermute(listed, 'cell', pairs + [(m, n) for n, m in pairs])]
    all_to_all x1, blocking collectives: 14.9 us -> 12.6 us  [shards(): lax.all_to_all(packed.reshape(devices, stride, LANES), 'cell', split_axis...]
  transfers between devices with their start and end apart: 4 -> 4, of which waited for: 2 -> 2; matrix products, arithmetic and copies ran while one was open for 0% -> 0% of each run, Pallas kernels for 19% -> 17%
where the time goes in v3:
time: 42.1 us; the launch traced here: 41.7 us
  Pallas kernels  18.6 us (44%)
  blocking collectives  12.6 us (30%)
  starting transfers between devices  7.98 us (19%)
  waiting for transfers between devices  1.94 us (5%)
  other arithmetic  0.62 us (1%)
    all_to_all x1, blocking collectives, shards(): lax.all_to_all(packed.reshape(devices, stride, LANES), 'cell', split_axis...  12.6 us
    pallas_call x1, Pallas kernels, shards(): pl.pallas_call(functools.partial(respond_kernel, portion=portion), out_sh...  7.02 us
    pallas_call x1, Pallas kernels, shards(): pl.pallas_call(functools.partial(receive_kernel, portion=portion), out_sh...  6.17 us
    pallas_call x1, Pallas kernels, shards(): pl.pallas_call(functools.partial(pack_kernel, link_total=link_total, **si...  4.35 us
    ppermute x2, starting transfers between devices, exchange(): return lax.ppermute(listed, 'cell', pairs + [(m, n) for n, m in pairs])  4.19 us
    ppermute x1, starting transfers between devices, shards(): other = lax.ppermute(arrived, 'grp', swap)  2.79 us
    ppermute x1, waiting for transfers between devices, shards(): other = lax.ppermute(arrived, 'grp', swap)  1.07 us
    pallas_call x1, Pallas kernels, shards(): pl.pallas_call(functools.partial(sort_kernel, **sizes), out_shape=(jax.Sh...  1.03 us
  transfers between devices with their start and end apart: 4, of which 2 were waited for; matrix products, arithmetic and copies ran while one was open for 0% of the time, Pallas kernels for 17%

profile of v3, /device:TPU:9, one launch (start us, length us, event | category | flops | bytes accessed | tf_op | source)
XLA Modules:
  0.0 41.7 jit_solution(10248139275358630441)
XLA Ops:
  0.0 4.4 %shard_map.91 = s32[384,128]{1,0:T(8,128)S(1)} custom-call(s32[256]{0:T(256)} %link_hbm.1, s32[256]{0:T(256)} %count_hbm.1, s32[256]{0:T(256)} %offset_hbm.1, f32[65,128]{1,0:T(8,128)} %bitcast.16, f32[65,128]{1,0:T(8,128)} %bitcast.17, f32[65,2,128]{2,1,0:T(2,128)} %bitcast.13), custom_call_target="tpu_custom_call" | custom-call | tf_op jit(solution)/shard_map/pallas_call | solution.py:571
  4.4 12.6 %all_to_all.5 = s32[16,24,128]{2,1,0:T(8,128)S(1)} all-to-all(s32[16,24,128]{2,1,0:T(8,128)S(1)} %bitcast.11), channel_id=1, replica_groups=mesh['grp'=2,'cell'=16] {'cell'}, dimensions={0} | all-to-all | bytes 393216 | tf_op jit(solution)/shard_map/all_to_all | solution.py:593
  16.9 2.8 %collective-permute-start = (s32[16,24,128]{2,1,0:T(8,128)S(1)}, s32[16,24,128]{2,1,0:T(8,128)S(1)}, u32[]{:S(2)}, u32[]{:S(2)}) collective-permute-start(s32[16,24,128]{2,1,0:T(8,128)S(1)} %all_to_all.5), channel_id=1, source_target_pairs={{0,16},{16,0},{1,17},{17,1},{2,18},{18,2},{3,19},{19,3},{4,20},{20... | collective-permute-start | bytes 589832 | tf_op jit(solution)/shard_map/ppermute | solution.py:596
  19.7 1.1 %collective-permute-done = s32[16,24,128]{2,1,0:T(8,128)S(1)} collective-permute-done((s32[16,24,128]{2,1,0:T(8,128)S(1)}, s32[16,24,128]{2,1,0:T(8,128)S(1)}, u32[]{:S(2)}, u32[]{:S(2)}) %collective-permute-start) | collective-permute-done | bytes 196640 | tf_op jit(solution)/shard_map/ppermute | solution.py:596
  20.8 1.0 %shard_map.92 = (s32[2,768,128]{2,1,0:T(8,128)S(1)}, s32[2,128]{1,0:T(2,128)S(1)}, s32[72,128]{1,0:T(8,128)S(1)}) custom-call(s32[8,32]{1,0:T(8,128)} %nearby_hbm.3, s32[32]{0:T(128)} %slot_hbm.3, bf16[64,128]{1,0:T(8,128)(2,1)} %bitcast.14, s32[384,128]{1,0:T(8,128)S(1)} %bitcast.10, s32[384,128]{1,0:T(8,128)S(1)} %bitcast.12), custom_call_target="tpu_custom_call" | custom-call | tf_op jit(solution)/shard_map/pallas_call | solution.py:608
  21.8 0.3 collective-permute-start.1
  22.2 3.8 %collective-permute-start.2 = (s32[72,128]{1,0:T(8,128)S(1)}, s32[72,128]{1,0:T(8,128)S(1)}, u32[]{:S(2)}, u32[]{:S(2)}) collective-permute-start(s32[72,128]{1,0:T(8,128)S(1)} %get-tuple-element.10), channel_id=1, source_target_pairs={{1,2},{3,4},{5,6},{7,8},{9,10},{11,12},{13,14},{2,1},{4,3},{6,5},{... | collective-permute-start | bytes 110600 | tf_op jit(solution)/shard_map/ppermute | solution.py:630
  26.0 7.0 %shard_map.93.response_ref = f32[128,128,128]{2,1,0:T(8,128)S(1)} custom-call(s32[2,768,128]{2,1,0:T(8,128)S(1)} %get-tuple-element.8.rows_ref, s32[2,128]{1,0:T(2,128)S(1)} %get-tuple-element.9.table_ref), custom_call_target="tpu_custom_call" | custom-call | flops 42949672960 | bytes 4194304 | tf_op jit(solution)/shard_map/pallas_call | solution.py:635
  33.1 0.0 collective-permute-done.1.first_ref
  33.1 0.0 collective-permute-done.2.second_ref
  33.1 6.2 %shard_map.94 = f32[64,128]{1,0:T(8,128)S(1)} custom-call(s32[8,32]{1,0:T(8,128)} %nearby_hbm.3, s32[32]{0:T(128)} %slot_hbm.3, bf16[64,128]{1,0:T(8,128)(2,1)} %bitcast.15, f32[128,128,128]{2,1,0:T(8,128)S(1)} %shard_map.93.response_ref, s32[72,128]{1,0:T(8,128)S(1)} %collective-permute-done.1.first_ref, s32[72,128]{1,0:T(8,128)S(1)} %collective-permute-done.2.second_ref), custom_call_target="tpu_custom_call" | custom-call | tf_op jit(solution)/shard_map/pallas_call | solution.py:654
  39.3 1.0 %collective-permute-start.3 = (f32[64,128]{1,0:T(8,128)S(1)}, f32[64,128]{1,0:T(8,128)S(1)}, u32[]{:S(2)}, u32[]{:S(2)}) collective-permute-start(f32[64,128]{1,0:T(8,128)S(1)} %shard_map.94), channel_id=1, source_target_pairs={{0,16},{16,0},{1,17},{17,1},{2,18},{18,2},{3,19},{19,3},{4,20},{20... | collective-permute-start | bytes 98312 | tf_op jit(solution)/shard_map/ppermute | solution.py:670
  40.3 0.9 %collective-permute-done.3 = f32[64,128]{1,0:T(8,128)S(1)} collective-permute-done((f32[64,128]{1,0:T(8,128)S(1)}, f32[64,128]{1,0:T(8,128)S(1)}, u32[]{:S(2)}, u32[]{:S(2)}) %collective-permute-start.3) | collective-permute-done | bytes 32800 | tf_op jit(solution)/shard_map/ppermute | solution.py:670
  41.1 0.6 %add.3 = f32[64,128]{1,0:T(8,128)} add(f32[64,128]{1,0:T(8,128)S(1)} %shard_map.94, f32[64,128]{1,0:T(8,128)S(1)} %collective-permute-done.3) | non-fusion elementwise | flops 8192 | bytes 98304 | tf_op jit(solution)/shard_map/add | solution.py:670
Async XLA Ops:
  16.9 3.9 %collective-permute-start = (s32[16,24,128]{2,1,0:T(8,128)S(1)}, s32[16,24,128]{2,1,0:T(8,128)S(1)}, u32[]{:S(2)}, u32[]{:S(2)}) collective-permute-start(s32[16,24,128]{2,1,0:T(8,128)S(1)} %all_to_all.5), channel_id=1, source_target_pairs={{0,16},{16,0},{1,17},{17,1},{2,18},{18,2},{3,19},{19,3},{4,20},{20... | collective-permute-start | bytes 589832 | tf_op jit(solution)/shard_map/ppermute | solution.py:596
  21.8 11.2 %collective-permute-start.1 = (s32[72,128]{1,0:T(8,128)S(1)}, s32[72,128]{1,0:T(8,128)S(1)}, u32[]{:S(2)}, u32[]{:S(2)}) collective-permute-start(s32[72,128]{1,0:T(8,128)S(1)} %get-tuple-element.10), channel_id=1, source_target_pairs={{0,1},{2,3},{4,5},{6,7},{8,9},{10,11},{12,13},{14,15},{1,0},{3,2},... | collective-permute-start | bytes 110600 | tf_op jit(solution)/shard_map/ppermute | solution.py:630
  22.2 10.9 %collective-permute-start.2 = (s32[72,128]{1,0:T(8,128)S(1)}, s32[72,128]{1,0:T(8,128)S(1)}, u32[]{:S(2)}, u32[]{:S(2)}) collective-permute-start(s32[72,128]{1,0:T(8,128)S(1)} %get-tuple-element.10), channel_id=1, source_target_pairs={{1,2},{3,4},{5,6},{7,8},{9,10},{11,12},{13,14},{2,1},{4,3},{6,5},{... | collective-permute-start | bytes 110600 | tf_op jit(solution)/shard_map/ppermute | solution.py:630
  39.3 1.9 %collective-permute-start.3 = (f32[64,128]{1,0:T(8,128)S(1)}, f32[64,128]{1,0:T(8,128)S(1)}, u32[]{:S(2)}, u32[]{:S(2)}) collective-permute-start(f32[64,128]{1,0:T(8,128)S(1)} %shard_map.94), channel_id=1, source_target_pairs={{0,16},{16,0},{1,17},{17,1},{2,18},{18,2},{3,19},{19,3},{4,20},{20... | collective-permute-start | bytes 98312 | tf_op jit(solution)/shard_map/ppermute | solution.py:670

commit v4 on v3

--- a/solution.py
+++ b/solution.py
@@ -21,6 +21,8 @@
 HALF = FRAME_TONES // 2
 SPANS = HALF // (2 * GROUP)
 LEVELS = 32767.0
+PITCH = 64
+UNROLL = 32
 DELAY_STEP = 64.0 / 65535.0
 SYMBOL_TOP = 4.0
 
@@ -91,7 +93,7 @@
 
 def pack_kernel(
     link_hbm, count_hbm, offset_hbm, delay_hbm, angle_hbm, gain_hbm, out_ref,
-    link_ref, count_ref, offset_ref, delay_ref, angle_ref, gain_ref, word_ref, sems,
+    link_ref, count_ref, offset_ref, delay_ref, angle_ref, real_ref, imag_ref, word_ref, stage_ref, sems,
     *, link_total, capacity, stride,
 ):
     copies = fetch(
@@ -101,55 +103,61 @@
             (offset_hbm, offset_ref),
             (delay_hbm, delay_ref),
             (angle_hbm, angle_ref),
-            (gain_hbm, gain_ref),
+            (gain_hbm.at[:, 0, :], real_ref),
+            (gain_hbm.at[:, 1, :], imag_ref),
         ],
         sems,
     )
     lane = lane_index(1)
-    out_ref[...] = jnp.zeros_like(out_ref)
-    empty = jnp.full((1, LANES), -1, jnp.int32)
-    tag_row = capacity // 2
-    for owner in range(out_ref.shape[0] // stride):
-        out_ref[owner * stride + tag_row : owner * stride + tag_row + 1, :] = empty
+    stage_ref[...] = jnp.zeros_like(stage_ref)
     for copy in copies:
         copy.wait()
     rows = delay_ref.shape[0]
     lower = lax.axis_index("grp") == 0
     c, s = quarter_cos_sin(angle_ref[...] * 0.5)
-    gain_re, gain_im = gain_ref[:, 0, :], gain_ref[:, 1, :]
+    gain_re, gain_im = real_ref[...], imag_ref[...]
+    sine = 2.0 * s * c
+    code = jnp.round(LEVELS * sine)
+    turn = (sine - code * (1.0 / LEVELS)) * (0.5 * math.pi * (SECTOR_ANTENNAS - 1))
+    gain_re, gain_im = gain_re + gain_im * turn, gain_im - gain_re * turn
     high = jnp.where(lower, jnp.round(delay_ref[...] * (1.0 / DELAY_STEP)) - 32768.0, root_code(gain_re))
-    low = jnp.where(lower, jnp.round(2.0 * LEVELS * s * c), root_code(gain_im))
+    low = jnp.where(lower, code, root_code(gain_im))
     word_ref[:rows, :] = join(high, low)
     link_bits = link_total.bit_length() - 1
+    owners = out_ref.shape[0] // stride
+    tag_rows = max(owners, GROUP)
+    tag_place = lax.broadcasted_iota(jnp.int32, (tag_rows, LANES), 0) * LANES + lane_index(tag_rows)
 
     def step(slot, carry):
-        last_owner, place, tags = carry
+        last_owner, key, tags = carry
         link = link_ref[slot]
         owner = link >> link_bits
-        fresh = owner != last_owner
-        place = jnp.where(fresh, 0, place + 1)
+        key = jnp.where(owner != last_owner, owner << 7, key + 1)
         offset = offset_ref[slot]
         row = offset >> 7
         shift = offset & (LANES - 1)
         word = jnp.where(lane >= shift, word_ref[pl.ds(row, 1), :], word_ref[pl.ds(row + 1, 1), :])
-        start = (place & 1) * PMAX
+        start = (key & 1) << 6
         word = pltpu.roll(word, (start - shift) & (LANES - 1), 1)
         within = lane - start
         live = (within >= 0) & (within < count_ref[slot])
-        base = owner * stride
-        pltpu.store(out_ref.at[pl.ds(base + (place >> 1), 1), :], word, mask=live)
-        tags = jnp.where(fresh, -1, tags)
-        tags = jnp.where(lane == place, link - (owner << link_bits), tags)
-        out_ref[pl.ds(base + tag_row, 1), :] = tags
-        return owner, place, tags
-
-    lax.fori_loop(0, link_total, step, (jnp.int32(-1), jnp.int32(0), empty), unroll=16)
+        pltpu.store(stage_ref.at[pl.ds(key >> 1, 1), :], word, mask=live)
+        return owner, key, jnp.where(tag_place == key, link, tags)
+
+    empty = jnp.full((tag_rows, LANES), -1, jnp.int32)
+    tags = lax.fori_loop(0, link_total, step, (jnp.int32(-1), jnp.int32(0), empty), unroll=UNROLL)[2]
+    for owner in range(owners):
+        out_ref[owner * stride : (owner + 1) * stride, :] = stage_ref[
+            owner * PITCH : owner * PITCH + stride, :
+        ]
+    out_ref[pl.ds(capacity // 2, owners, stride=stride), :] = tags[:owners]
 
 
 def find_rows(own_ref, table_ref, capacity, stride):
     total_rows = own_ref.shape[0]
     senders = total_rows // stride
-    tags = own_ref[pl.ds(capacity // 2, senders, stride=stride), :].astype(jnp.float32).T
+    tags = own_ref[pl.ds(capacity // 2, senders, stride=stride), :]
+    tags = (tags - lax.axis_index("cell") * (table_ref.shape[0] * LANES)).astype(jnp.float32).T
     depth = min(pl.cdiv(capacity, GROUP) * GROUP, LANES)
     tags = tags[:depth]
     place = lax.broadcasted_iota(jnp.int32, (depth, LANES), 0)
@@ -326,6 +334,7 @@
     tone_a, mix_a, tone_b, mix_b = buffers
     block = tone_a.shape[0]
     blocks = pairs // block
+    once = jnp.minimum(lax.axis_index("cell") + 1, 1)
 
     def build(index, tone_ref, mix_ref):
         for n in range(block):
@@ -335,26 +344,27 @@
         for n in range(block):
             emit(index * block + n, multiply_operands(tone_ref.at[n], mix_ref.at[n]))
 
-    build(0, tone_a, mix_a)
+    def stage(index, now, later):
+        def body(_, carry):
+            if now is not None:
+                multiply(index, *now)
+            if later is not None:
+                build(index + 1, *later)
+            return carry
+
+        lax.fori_loop(0, once, body, 0)
+
+    first, second = (tone_a, mix_a), (tone_b, mix_b)
+    stage(-1, None, first)
 
     def step(n, carry):
-        once = jnp.minimum(n + 1, 1)
-
-        def first(_, carry):
-            multiply(2 * n, tone_a, mix_a)
-            build(2 * n + 1, tone_b, mix_b)
-            return carry
-
-        def second(_, carry):
-            multiply(2 * n + 1, tone_b, mix_b)
-            build(jnp.minimum(2 * n + 2, blocks - 1), tone_a, mix_a)
-            return carry
-
-        lax.fori_loop(0, once, first, 0)
-        lax.fori_loop(0, once, second, 0)
+        stage(2 * n, first, second)
+        stage(2 * n + 1, second, first)
         return carry
 
-    lax.fori_loop(0, blocks // 2, step, 0)
+    lax.fori_loop(0, blocks // 2 - 1, step, 0)
+    stage(blocks - 2, first, second)
+    stage(blocks - 1, second, None)
 
 
 def tone_of_place(lane):
@@ -473,7 +483,7 @@
         contribute(nearby_ref[slot, user] - first_sector, 2 * users + user, re, im)
         return carry
 
-    lax.fori_loop(0, users, own_user, 0, unroll=2)
+    lax.fori_loop(0, users, own_user, 0, unroll=8)
     after_first = (here & 1) == 0
 
     def emit(pair, response):
@@ -520,12 +530,13 @@
         out_ref[pl.ds(user * 2 + 1, 1), :] = jnp.sum(total_im, axis=0, keepdims=True) * scale
         return carry
 
-    lax.fori_loop(0, users, one_user, 0, unroll=2)
+    lax.fori_loop(0, users, one_user, 0, unroll=4)
     out_ref[...] = reorder(out_ref[...], place_of_tone(lane_index(GROUP)))
 
 
 VMEM = pl.BlockSpec(memory_space=pltpu.VMEM)
 HBM = pl.BlockSpec(memory_space=pltpu.HBM)
+ANY = pl.BlockSpec(memory_space=pl.ANY)
 LIMIT = pltpu.CompilerParams(vmem_limit_bytes=16 << 20)
 BLOCK = 8
 
@@ -577,9 +588,11 @@
         + [
             pltpu.VMEM((path_rows, LANES), jnp.float32),
             pltpu.VMEM((path_rows, LANES), jnp.float32),
-            pltpu.VMEM((path_rows, 2, LANES), jnp.float32),
+            pltpu.VMEM((path_rows, LANES), jnp.float32),
+            pltpu.VMEM((path_rows, LANES), jnp.float32),
             pltpu.VMEM((pl.cdiv(path_rows + 1, GROUP) * GROUP, LANES), jnp.int32),
-            pltpu.SemaphoreType.DMA((6,)),
+            pltpu.VMEM((devices * PITCH, LANES), jnp.int32),
+            pltpu.SemaphoreType.DMA((7,)),
         ],
         compiler_params=LIMIT,
     )(
@@ -597,9 +610,7 @@
 
     row_total = devices * stride
     list_rows = 2 * total_users + GROUP
-    symbol_rows = in_hbm(symbols.reshape(2 * total_users, LANES))
-    nearby_sectors = in_hbm(nearby_sectors)
-    serving_slot = in_hbm(serving_slot)
+    symbol_rows = symbols.reshape(2 * total_users, LANES)
     small_scratch = [
         pltpu.SMEM(nearby_sectors.shape, jnp.int32),
         pltpu.SMEM((total_users,), jnp.int32),
@@ -618,9 +629,9 @@
         + [pltpu.SMEM((link_rows, LANES), jnp.int32), pltpu.SemaphoreType.DMA((4,))],
         compiler_params=LIMIT,
     )(
-        nearby_sectors,
-        serving_slot,
-        symbol_rows,
+        in_hbm(nearby_sectors),
+        in_hbm(serving_slot),
+        in_hbm(symbol_rows),
         arrived.reshape(row_total, LANES),
         other.reshape(row_total, LANES),
     )
@@ -654,7 +665,7 @@
     partial_value = pl.pallas_call(
         functools.partial(receive_kernel, portion=portion),
         out_shape=jax.ShapeDtypeStruct((2 * total_users, LANES), jnp.float32),
-        in_specs=[HBM] * 3 + [VMEM] * 3,
+        in_specs=[ANY] * 3 + [VMEM] * 3,
         out_specs=VMEM,
         scratch_shapes=small_scratch
         + [

time: 42.1 us -> 39.6 us (0.941)
  Pallas kernels: 18.6 us -> 16.1 us
    pallas_call x1, Pallas kernels: 4.35 us -> 2.73 us  [shards(): pl.pallas_call(functools.partial(pack_kernel, link_total=link_total, **si...]
    pallas_call x1, Pallas kernels: 6.17 us -> 5.23 us  [shards(): pl.pallas_call(functools.partial(receive_kernel, portion=portion), out_sh...]
  transfers between devices with their start and end apart: 4 -> 4, of which waited for: 2 -> 2; matrix products, arithmetic and copies ran while one was open for 0% -> 0% of each run, Pallas kernels for 17% -> 18%
where the time goes in v4:
time: 39.6 us; the launch traced here: 39.3 us
  Pallas kernels  16.1 us (41%)
  blocking collectives  12.6 us (32%)
  starting transfers between devices  7.97 us (20%)
  waiting for transfers between devices  1.94 us (5%)
  other arithmetic  0.62 us (2%)
    all_to_all x1, blocking collectives, shards(): lax.all_to_all(packed.reshape(devices, stride, LANES), 'cell', split_axis...  12.6 us
    pallas_call x1, Pallas kernels, shards(): pl.pallas_call(functools.partial(respond_kernel, portion=portion), out_sh...  7.06 us
    pallas_call x1, Pallas kernels, shards(): pl.pallas_call(functools.partial(receive_kernel, portion=portion), out_sh...  5.23 us
    ppermute x2, starting transfers between devices, exchange(): return lax.ppermute(listed, 'cell', pairs + [(m, n) for n, m in pairs])  4.19 us
    ppermute x1, starting transfers between devices, shards(): other = lax.ppermute(arrived, 'grp', swap)  2.79 us
    pallas_call x1, Pallas kernels, shards(): pl.pallas_call(functools.partial(pack_kernel, link_total=link_total, **si...  2.73 us
    ppermute x1, waiting for transfers between devices, shards(): other = lax.ppermute(arrived, 'grp', swap)  1.07 us
    pallas_call x1, Pallas kernels, shards(): pl.pallas_call(functools.partial(sort_kernel, **sizes), out_shape=(jax.Sh...  1.03 us
  transfers between devices with their start and end apart: 4, of which 2 were waited for; matrix products, arithmetic and copies ran while one was open for 0% of the time, Pallas kernels for 18%

profile of v4, /device:TPU:9, one launch (start us, length us, event | category | flops | bytes accessed | tf_op | source)
XLA Modules:
  0.0 39.3 jit_solution(14693026102274327262)
XLA Ops:
  0.0 2.7 %shard_map.91 = s32[384,128]{1,0:T(8,128)S(1)} custom-call(s32[256]{0:T(256)} %link_hbm.1, s32[256]{0:T(256)} %count_hbm.1, s32[256]{0:T(256)} %offset_hbm.1, f32[65,128]{1,0:T(8,128)} %bitcast.16, f32[65,128]{1,0:T(8,128)} %bitcast.17, f32[65,2,128]{2,1,0:T(2,128)} %bitcast.15), custom_call_target="tpu_custom_call" | custom-call | tf_op jit(solution)/shard_map/pallas_call | solution.py:582
  2.7 12.6 %all_to_all.5 = s32[16,24,128]{2,1,0:T(8,128)S(1)} all-to-all(s32[16,24,128]{2,1,0:T(8,128)S(1)} %bitcast.11), channel_id=1, replica_groups=mesh['grp'=2,'cell'=16] {'cell'}, dimensions={0} | all-to-all | bytes 393216 | tf_op jit(solution)/shard_map/all_to_all | solution.py:606
  15.3 2.8 %collective-permute-start = (s32[16,24,128]{2,1,0:T(8,128)S(1)}, s32[16,24,128]{2,1,0:T(8,128)S(1)}, u32[]{:S(2)}, u32[]{:S(2)}) collective-permute-start(s32[16,24,128]{2,1,0:T(8,128)S(1)} %all_to_all.5), channel_id=1, source_target_pairs={{0,16},{16,0},{1,17},{17,1},{2,18},{18,2},{3,19},{19,3},{4,20},{20... | collective-permute-start | bytes 589832 | tf_op jit(solution)/shard_map/ppermute | solution.py:609
  18.1 1.1 %collective-permute-done = s32[16,24,128]{2,1,0:T(8,128)S(1)} collective-permute-done((s32[16,24,128]{2,1,0:T(8,128)S(1)}, s32[16,24,128]{2,1,0:T(8,128)S(1)}, u32[]{:S(2)}, u32[]{:S(2)}) %collective-permute-start) | collective-permute-done | bytes 196640 | tf_op jit(solution)/shard_map/ppermute | solution.py:609
  19.2 1.0 %shard_map.92 = (s32[2,768,128]{2,1,0:T(8,128)S(1)}, s32[2,128]{1,0:T(2,128)S(1)}, s32[72,128]{1,0:T(8,128)S(1)}) custom-call(s32[8,32]{1,0:T(8,128)} %nearby_hbm.3, s32[32]{0:T(128)} %slot_hbm.3, bf16[64,128]{1,0:T(8,128)(2,1)} %bitcast.13, s32[384,128]{1,0:T(8,128)S(1)} %bitcast.10, s32[384,128]{1,0:T(8,128)S(1)} %bitcast.12), custom_call_target="tpu_custom_call" | custom-call | tf_op jit(solution)/shard_map/pallas_call | solution.py:619
  20.2 0.3 collective-permute-start.1
  20.6 3.8 %collective-permute-start.2 = (s32[72,128]{1,0:T(8,128)S(1)}, s32[72,128]{1,0:T(8,128)S(1)}, u32[]{:S(2)}, u32[]{:S(2)}) collective-permute-start(s32[72,128]{1,0:T(8,128)S(1)} %get-tuple-element.10), channel_id=1, source_target_pairs={{1,2},{3,4},{5,6},{7,8},{9,10},{11,12},{13,14},{2,1},{4,3},{6,5},{... | collective-permute-start | bytes 110600 | tf_op jit(solution)/shard_map/ppermute | solution.py:641
  24.4 0.0 copy-start
  24.4 0.0 copy-start.1
  24.4 0.0 copy-start.2
  24.5 7.1 %shard_map.93.response_ref = f32[128,128,128]{2,1,0:T(8,128)S(1)} custom-call(s32[2,768,128]{2,1,0:T(8,128)S(1)} %get-tuple-element.8.rows_ref, s32[2,128]{1,0:T(2,128)S(1)} %get-tuple-element.9.table_ref), custom_call_target="tpu_custom_call" | custom-call | flops 42949672960 | bytes 4194304 | tf_op jit(solution)/shard_map/pallas_call | solution.py:646
  31.5 0.0 collective-permute-done.1.first_ref
  31.5 0.0 collective-permute-done.2.second_ref
  31.5 0.0 copy-done
  31.6 0.0 copy-done.1
  31.6 0.0 copy-done.2
  31.6 5.2 %shard_map.94 = f32[64,128]{1,0:T(8,128)S(1)} custom-call(s32[8,32]{1,0:T(8,128)S(1)} %copy-done.1, s32[32]{0:T(128)S(1)} %copy-done.2, bf16[64,128]{1,0:T(8,128)(2,1)S(1)} %bitcast.14, f32[128,128,128]{2,1,0:T(8,128)S(1)} %shard_map.93.response_ref, s32[72,128]{1,0:T(8,128)S(1)} %collective-permute-done.1.first_ref, ...), custom_call_target="tpu_custom_call" | custom-call | tf_op jit(solution)/shard_map/pallas_call | solution.py:665
  36.8 1.0 %collective-permute-start.3 = (f32[64,128]{1,0:T(8,128)S(1)}, f32[64,128]{1,0:T(8,128)S(1)}, u32[]{:S(2)}, u32[]{:S(2)}) collective-permute-start(f32[64,128]{1,0:T(8,128)S(1)} %shard_map.94), channel_id=1, source_target_pairs={{0,16},{16,0},{1,17},{17,1},{2,18},{18,2},{3,19},{19,3},{4,20},{20... | collective-permute-start | bytes 98312 | tf_op jit(solution)/shard_map/ppermute | solution.py:681
  37.8 0.9 %collective-permute-done.3 = f32[64,128]{1,0:T(8,128)S(1)} collective-permute-done((f32[64,128]{1,0:T(8,128)S(1)}, f32[64,128]{1,0:T(8,128)S(1)}, u32[]{:S(2)}, u32[]{:S(2)}) %collective-permute-start.3) | collective-permute-done | bytes 32800 | tf_op jit(solution)/shard_map/ppermute | solution.py:681
  38.7 0.6 %add.3 = f32[64,128]{1,0:T(8,128)} add(f32[64,128]{1,0:T(8,128)S(1)} %shard_map.94, f32[64,128]{1,0:T(8,128)S(1)} %collective-permute-done.3) | non-fusion elementwise | flops 8192 | bytes 98304 | tf_op jit(solution)/shard_map/add | solution.py:681
Async XLA Ops:
  15.3 3.9 %collective-permute-start = (s32[16,24,128]{2,1,0:T(8,128)S(1)}, s32[16,24,128]{2,1,0:T(8,128)S(1)}, u32[]{:S(2)}, u32[]{:S(2)}) collective-permute-start(s32[16,24,128]{2,1,0:T(8,128)S(1)} %all_to_all.5), channel_id=1, source_target_pairs={{0,16},{16,0},{1,17},{17,1},{2,18},{18,2},{3,19},{19,3},{4,20},{20... | collective-permute-start | bytes 589832 | tf_op jit(solution)/shard_map/ppermute | solution.py:609
  20.2 11.3 %collective-permute-start.1 = (s32[72,128]{1,0:T(8,128)S(1)}, s32[72,128]{1,0:T(8,128)S(1)}, u32[]{:S(2)}, u32[]{:S(2)}) collective-permute-start(s32[72,128]{1,0:T(8,128)S(1)} %get-tuple-element.10), channel_id=1, source_target_pairs={{0,1},{2,3},{4,5},{6,7},{8,9},{10,11},{12,13},{14,15},{1,0},{3,2},... | collective-permute-start | bytes 110600 | tf_op jit(solution)/shard_map/ppermute | solution.py:641
  20.6 11.0 %collective-permute-start.2 = (s32[72,128]{1,0:T(8,128)S(1)}, s32[72,128]{1,0:T(8,128)S(1)}, u32[]{:S(2)}, u32[]{:S(2)}) collective-permute-start(s32[72,128]{1,0:T(8,128)S(1)} %get-tuple-element.10), channel_id=1, source_target_pairs={{1,2},{3,4},{5,6},{7,8},{9,10},{11,12},{13,14},{2,1},{4,3},{6,5},{... | collective-permute-start | bytes 110600 | tf_op jit(solution)/shard_map/ppermute | solution.py:641
  24.4 7.1 %copy-start = (bf16[32,2,128]{2,1,0:T(2,128)(2,1)S(1)}, bf16[32,2,128]{2,1,0:T(2,128)(2,1)}, u32[]{:S(2)}) copy-start(bf16[32,2,128]{2,1,0:T(2,128)(2,1)} %param.17) | copy-start | bytes 49156
  24.4 7.1 %copy-start.1 = (s32[8,32]{1,0:T(8,128)S(1)}, s32[8,32]{1,0:T(8,128)}, u32[]{:S(2)}) copy-start(s32[8,32]{1,0:T(8,128)} %nearby_hbm.3) | copy-start | bytes 3076
  24.4 7.1 %copy-start.2 = (s32[32]{0:T(128)S(1)}, s32[32]{0:T(128)}, u32[]{:S(2)}) copy-start(s32[32]{0:T(128)} %slot_hbm.3) | copy-start | bytes 388
  36.8 1.8 %collective-permute-start.3 = (f32[64,128]{1,0:T(8,128)S(1)}, f32[64,128]{1,0:T(8,128)S(1)}, u32[]{:S(2)}, u32[]{:S(2)}) collective-permute-start(f32[64,128]{1,0:T(8,128)S(1)} %shard_map.94), channel_id=1, source_target_pairs={{0,16},{16,0},{1,17},{17,1},{2,18},{18,2},{3,19},{19,3},{4,20},{20... | collective-permute-start | bytes 98312 | tf_op jit(solution)/shard_map/ppermute | solution.py:681

commit v5 on v4

--- a/solution.py
+++ b/solution.py
@@ -21,7 +21,7 @@
 HALF = FRAME_TONES // 2
 SPANS = HALF // (2 * GROUP)
 LEVELS = 32767.0
-PITCH = 64
+TAG_LANE = LANES - PMAX // 2
 UNROLL = 32
 DELAY_STEP = 64.0 / 65535.0
 SYMBOL_TOP = 4.0
@@ -93,7 +93,7 @@
 
 def pack_kernel(
     link_hbm, count_hbm, offset_hbm, delay_hbm, angle_hbm, gain_hbm, out_ref,
-    link_ref, count_ref, offset_ref, delay_ref, angle_ref, real_ref, imag_ref, word_ref, stage_ref, sems,
+    link_ref, count_ref, offset_ref, delay_ref, angle_ref, real_ref, imag_ref, word_ref, sems,
     *, link_total, capacity, stride,
 ):
     copies = fetch(
@@ -109,7 +109,7 @@
         sems,
     )
     lane = lane_index(1)
-    stage_ref[...] = jnp.zeros_like(stage_ref)
+    out_ref[...] = jnp.zeros_like(out_ref)
     for copy in copies:
         copy.wait()
     rows = delay_ref.shape[0]
@@ -126,40 +126,47 @@
     link_bits = link_total.bit_length() - 1
     owners = out_ref.shape[0] // stride
     tag_rows = max(owners, GROUP)
-    tag_place = lax.broadcasted_iota(jnp.int32, (tag_rows, LANES), 0) * LANES + lane_index(tag_rows)
+    column = lane_index(tag_rows)
+    tag_place = lax.broadcasted_iota(jnp.int32, (tag_rows, LANES), 0) * (2 * stride) + column - TAG_LANE
+    tag_place = jnp.where(column >= TAG_LANE, tag_place, -1)
 
     def step(slot, carry):
-        last_owner, key, tags = carry
+        last_owner, free, taken, tags = carry
         link = link_ref[slot]
+        count = count_ref[slot]
         owner = link >> link_bits
-        key = jnp.where(owner != last_owner, owner << 7, key + 1)
+        fresh = owner != last_owner
+        first = owner * (2 * stride)
+        free = jnp.where(fresh, first, free)
+        taken = jnp.where(fresh, 0, taken)
+        short = jnp.where(count <= PMAX // 2, 1 - taken, 0)
+        place = jnp.where(short == 1, first + (capacity - 1), free)
         offset = offset_ref[slot]
         row = offset >> 7
         shift = offset & (LANES - 1)
         word = jnp.where(lane >= shift, word_ref[pl.ds(row, 1), :], word_ref[pl.ds(row + 1, 1), :])
-        start = (key & 1) << 6
+        start = (place & 1) << 6
         word = pltpu.roll(word, (start - shift) & (LANES - 1), 1)
         within = lane - start
-        live = (within >= 0) & (within < count_ref[slot])
-        pltpu.store(stage_ref.at[pl.ds(key >> 1, 1), :], word, mask=live)
-        return owner, key, jnp.where(tag_place == key, link, tags)
+        live = (within >= 0) & (within < count)
+        pltpu.store(out_ref.at[pl.ds(place >> 1, 1), :], word, mask=live)
+        tags = jnp.where(tag_place == place, link, tags)
+        return owner, free + 1 - short, taken + short, tags
 
     empty = jnp.full((tag_rows, LANES), -1, jnp.int32)
-    tags = lax.fori_loop(0, link_total, step, (jnp.int32(-1), jnp.int32(0), empty), unroll=UNROLL)[2]
-    for owner in range(owners):
-        out_ref[owner * stride : (owner + 1) * stride, :] = stage_ref[
-            owner * PITCH : owner * PITCH + stride, :
-        ]
-    out_ref[pl.ds(capacity // 2, owners, stride=stride), :] = tags[:owners]
+    zero = jnp.int32(0)
+    tags = lax.fori_loop(0, link_total, step, (jnp.int32(-1), zero, zero, empty), unroll=UNROLL)[3]
+    last = pl.ds(capacity // 2 - 1, owners, stride=stride)
+    out_ref[last, :] = jnp.where(lane >= TAG_LANE, tags[:owners], out_ref[last, :])
 
 
 def find_rows(own_ref, table_ref, capacity, stride):
     total_rows = own_ref.shape[0]
     senders = total_rows // stride
-    tags = own_ref[pl.ds(capacity // 2, senders, stride=stride), :]
+    tags = own_ref[pl.ds(capacity // 2 - 1, senders, stride=stride), :]
     tags = (tags - lax.axis_index("cell") * (table_ref.shape[0] * LANES)).astype(jnp.float32).T
-    depth = min(pl.cdiv(capacity, GROUP) * GROUP, LANES)
-    tags = tags[:depth]
+    depth = pl.cdiv(capacity, GROUP) * GROUP
+    tags = tags[TAG_LANE : TAG_LANE + depth]
     place = lax.broadcasted_iota(jnp.int32, (depth, LANES), 0)
     inside = place < capacity
     lane = lane_index(depth)
@@ -192,6 +199,11 @@
     for n, words in enumerate((jnp.where(lower, own, other), jnp.where(lower, other, own))):
         rows_ref[n, :total_rows, :] = words
         rows_ref[n, total_rows:, :] = pltpu.roll(words, PMAX, 1)
+        senders = total_rows // stride
+        for m, at in enumerate((TAG_LANE, TAG_LANE - PMAX)):
+            last = pl.ds(m * total_rows + capacity // 2 - 1, senders, stride=stride)
+            kept = (lane_index(senders) < at) | (lane_index(senders) >= at + PMAX // 2)
+            rows_ref[n, last, :] = jnp.where(kept, rows_ref[n, last, :], 0)
     for copy in copies:
         copy.wait()
     users = slot_ref.shape[0]
@@ -504,7 +516,7 @@
         value = remote[sector]
         re, im = value[:portion], value[portion:]
         power = jnp.sum(re * re + im * im, axis=1, keepdims=True) * (1.0 / FRAME_TONES)
-        scale = 1.0 / jnp.sqrt(power + EPSILON)
+        scale = lax.rsqrt(power + EPSILON)
         remote[sector, :portion, :] = (re * scale).astype(jnp.bfloat16).astype(jnp.float32)
         remote[sector, portion:, :] = (im * scale).astype(jnp.bfloat16).astype(jnp.float32)
         return carry
@@ -572,7 +584,7 @@
     link_total = slot_counts.shape[0]
     total_users = serving_slot.shape[0]
     capacity = 2 * link_total // devices
-    stride = pl.cdiv(capacity // 2 + 1, GROUP) * GROUP
+    stride = pl.cdiv(capacity // 2, GROUP) * GROUP
     portion = SECTOR_ANTENNAS // worker_count
     swap = [(n, worker_count - 1 - n) for n in range(worker_count)]
     path_rows = path_total // LANES
@@ -591,7 +603,6 @@
             pltpu.VMEM((path_rows, LANES), jnp.float32),
             pltpu.VMEM((path_rows, LANES), jnp.float32),
             pltpu.VMEM((pl.cdiv(path_rows + 1, GROUP) * GROUP, LANES), jnp.int32),
-            pltpu.VMEM((devices * PITCH, LANES), jnp.int32),
             pltpu.SemaphoreType.DMA((7,)),
         ],
         compiler_params=LIMIT,

time: 39.6 us -> 39.2 us (0.990)
  starting transfers between devices: 7.97 us -> 7.32 us
  Pallas kernels: 16.1 us -> 16.7 us
    pallas_call x1, Pallas kernels: 2.73 us -> 3.58 us  [shards(): pl.pallas_call(functools.partial(pack_kernel, link_total=link_total, **si...]
    ppermute x1, starting transfers between devices: 2.79 us -> 2.03 us  [shards(): other = lax.ppermute(arrived, 'grp', swap)]
where the time goes in v5:
time: 39.2 us; the launch traced here: 38.8 us
  Pallas kernels  16.7 us (43%)
  blocking collectives  12.3 us (31%)
  starting transfers between devices  7.32 us (19%)
  waiting for transfers between devices  1.85 us (5%)
  other arithmetic  0.62 us (2%)
    all_to_all x1, blocking collectives, shards(): lax.all_to_all(packed.reshape(devices, stride, LANES), 'cell', split_axis...  12.3 us
    pallas_call x1, Pallas kernels, shards(): pl.pallas_call(functools.partial(respond_kernel, portion=portion), out_sh...  7.05 us
    pallas_call x1, Pallas kernels, shards(): pl.pallas_call(functools.partial(receive_kernel, portion=portion), out_sh...  4.96 us
    ppermute x2, starting transfers between devices, exchange(): return lax.ppermute(listed, 'cell', pairs + [(m, n) for n, m in pairs])  4.32 us
    pallas_call x1, Pallas kernels, shards(): pl.pallas_call(functools.partial(pack_kernel, link_total=link_total, **si...  3.58 us
    ppermute x1, starting transfers between devices, shards(): other = lax.ppermute(arrived, 'grp', swap)  2.03 us
    pallas_call x1, Pallas kernels, shards(): pl.pallas_call(functools.partial(sort_kernel, **sizes), out_shape=(jax.Sh...  1.07 us
    ppermute x1, waiting for transfers between devices, shards(): other = lax.ppermute(arrived, 'grp', swap)  0.99 us
  transfers between devices with their start and end apart: 4, of which 2 were waited for; matrix products, arithmetic and copies ran while one was open for 0% of the time, Pallas kernels for 18%

profile of v5, /device:TPU:9, one launch (start us, length us, event | category | flops | bytes accessed | tf_op | source)
XLA Modules:
  0.0 38.8 jit_solution(3054166466397236029)
XLA Ops:
  0.0 3.6 %shard_map.91 = s32[256,128]{1,0:T(8,128)S(1)} custom-call(s32[256]{0:T(256)} %link_hbm.1, s32[256]{0:T(256)} %count_hbm.1, s32[256]{0:T(256)} %offset_hbm.1, f32[65,128]{1,0:T(8,128)} %bitcast.16, f32[65,128]{1,0:T(8,128)} %bitcast.17, f32[65,2,128]{2,1,0:T(2,128)} %bitcast.15), custom_call_target="tpu_custom_call" | custom-call | tf_op jit(solution)/shard_map/pallas_call | solution.py:594
  3.6 12.3 %all_to_all.5 = s32[16,16,128]{2,1,0:T(8,128)S(1)} all-to-all(s32[16,16,128]{2,1,0:T(8,128)S(1)} %bitcast.11), channel_id=1, replica_groups=mesh['grp'=2,'cell'=16] {'cell'}, dimensions={0} | all-to-all | bytes 262144 | tf_op jit(solution)/shard_map/all_to_all | solution.py:617
  15.9 2.0 %collective-permute-start = (s32[16,16,128]{2,1,0:T(8,128)S(1)}, s32[16,16,128]{2,1,0:T(8,128)S(1)}, u32[]{:S(2)}, u32[]{:S(2)}) collective-permute-start(s32[16,16,128]{2,1,0:T(8,128)S(1)} %all_to_all.5), channel_id=1, source_target_pairs={{0,16},{16,0},{1,17},{17,1},{2,18},{18,2},{3,19},{19,3},{4,20},{20... | collective-permute-start | bytes 393224 | tf_op jit(solution)/shard_map/ppermute | solution.py:620
  17.9 1.0 %collective-permute-done = s32[16,16,128]{2,1,0:T(8,128)S(1)} collective-permute-done((s32[16,16,128]{2,1,0:T(8,128)S(1)}, s32[16,16,128]{2,1,0:T(8,128)S(1)}, u32[]{:S(2)}, u32[]{:S(2)}) %collective-permute-start) | collective-permute-done | bytes 131104 | tf_op jit(solution)/shard_map/ppermute | solution.py:620
  18.9 1.1 %shard_map.92 = (s32[2,512,128]{2,1,0:T(8,128)S(1)}, s32[2,128]{1,0:T(2,128)S(1)}, s32[72,128]{1,0:T(8,128)S(1)}) custom-call(s32[8,32]{1,0:T(8,128)} %nearby_hbm.3, s32[32]{0:T(128)} %slot_hbm.3, bf16[64,128]{1,0:T(8,128)(2,1)} %bitcast.13, s32[256,128]{1,0:T(8,128)S(1)} %bitcast.10, s32[256,128]{1,0:T(8,128)S(1)} %bitcast.12), custom_call_target="tpu_custom_call" | custom-call | tf_op jit(solution)/shard_map/pallas_call | solution.py:630
  19.9 0.3 collective-permute-start.1
  20.3 4.0 %collective-permute-start.2 = (s32[72,128]{1,0:T(8,128)S(1)}, s32[72,128]{1,0:T(8,128)S(1)}, u32[]{:S(2)}, u32[]{:S(2)}) collective-permute-start(s32[72,128]{1,0:T(8,128)S(1)} %get-tuple-element.10), channel_id=1, source_target_pairs={{1,2},{3,4},{5,6},{7,8},{9,10},{11,12},{13,14},{2,1},{4,3},{6,5},{... | collective-permute-start | bytes 110600 | tf_op jit(solution)/shard_map/ppermute | solution.py:652
  24.3 0.0 copy-start
  24.3 0.0 copy-start.1
  24.3 0.0 copy-start.2
  24.3 7.1 %shard_map.93.response_ref = f32[128,128,128]{2,1,0:T(8,128)S(1)} custom-call(s32[2,512,128]{2,1,0:T(8,128)S(1)} %get-tuple-element.8.rows_ref, s32[2,128]{1,0:T(2,128)S(1)} %get-tuple-element.9.table_ref), custom_call_target="tpu_custom_call" | custom-call | flops 42949672960 | bytes 4194304 | tf_op jit(solution)/shard_map/pallas_call | solution.py:657
  31.4 0.0 collective-permute-done.1.first_ref
  31.4 0.0 collective-permute-done.2.second_ref
  31.4 0.0 copy-done
  31.4 0.0 copy-done.1
  31.4 0.0 copy-done.2
  31.4 5.0 %shard_map.94 = f32[64,128]{1,0:T(8,128)S(1)} custom-call(s32[8,32]{1,0:T(8,128)S(1)} %copy-done.1, s32[32]{0:T(128)S(1)} %copy-done.2, bf16[64,128]{1,0:T(8,128)(2,1)S(1)} %bitcast.14, f32[128,128,128]{2,1,0:T(8,128)S(1)} %shard_map.93.response_ref, s32[72,128]{1,0:T(8,128)S(1)} %collective-permute-done.1.first_ref, ...), custom_call_target="tpu_custom_call" | custom-call | tf_op jit(solution)/shard_map/pallas_call | solution.py:676
  36.4 1.0 %collective-permute-start.3 = (f32[64,128]{1,0:T(8,128)S(1)}, f32[64,128]{1,0:T(8,128)S(1)}, u32[]{:S(2)}, u32[]{:S(2)}) collective-permute-start(f32[64,128]{1,0:T(8,128)S(1)} %shard_map.94), channel_id=1, source_target_pairs={{0,16},{16,0},{1,17},{17,1},{2,18},{18,2},{3,19},{19,3},{4,20},{20... | collective-permute-start | bytes 98312 | tf_op jit(solution)/shard_map/ppermute | solution.py:692
  37.4 0.9 %collective-permute-done.3 = f32[64,128]{1,0:T(8,128)S(1)} collective-permute-done((f32[64,128]{1,0:T(8,128)S(1)}, f32[64,128]{1,0:T(8,128)S(1)}, u32[]{:S(2)}, u32[]{:S(2)}) %collective-permute-start.3) | collective-permute-done | bytes 32800 | tf_op jit(solution)/shard_map/ppermute | solution.py:692
  38.2 0.6 %add.3 = f32[64,128]{1,0:T(8,128)} add(f32[64,128]{1,0:T(8,128)S(1)} %shard_map.94, f32[64,128]{1,0:T(8,128)S(1)} %collective-permute-done.3) | non-fusion elementwise | flops 8192 | bytes 98304 | tf_op jit(solution)/shard_map/add | solution.py:692
Async XLA Ops:
  15.9 3.0 %collective-permute-start = (s32[16,16,128]{2,1,0:T(8,128)S(1)}, s32[16,16,128]{2,1,0:T(8,128)S(1)}, u32[]{:S(2)}, u32[]{:S(2)}) collective-permute-start(s32[16,16,128]{2,1,0:T(8,128)S(1)} %all_to_all.5), channel_id=1, source_target_pairs={{0,16},{16,0},{1,17},{17,1},{2,18},{18,2},{3,19},{19,3},{4,20},{20... | collective-permute-start | bytes 393224 | tf_op jit(solution)/shard_map/ppermute | solution.py:620
  19.9 11.4 %collective-permute-start.1 = (s32[72,128]{1,0:T(8,128)S(1)}, s32[72,128]{1,0:T(8,128)S(1)}, u32[]{:S(2)}, u32[]{:S(2)}) collective-permute-start(s32[72,128]{1,0:T(8,128)S(1)} %get-tuple-element.10), channel_id=1, source_target_pairs={{0,1},{2,3},{4,5},{6,7},{8,9},{10,11},{12,13},{14,15},{1,0},{3,2},... | collective-permute-start | bytes 110600 | tf_op jit(solution)/shard_map/ppermute | solution.py:652
  20.3 11.1 %collective-permute-start.2 = (s32[72,128]{1,0:T(8,128)S(1)}, s32[72,128]{1,0:T(8,128)S(1)}, u32[]{:S(2)}, u32[]{:S(2)}) collective-permute-start(s32[72,128]{1,0:T(8,128)S(1)} %get-tuple-element.10), channel_id=1, source_target_pairs={{1,2},{3,4},{5,6},{7,8},{9,10},{11,12},{13,14},{2,1},{4,3},{6,5},{... | collective-permute-start | bytes 110600 | tf_op jit(solution)/shard_map/ppermute | solution.py:652
  24.3 7.1 %copy-start = (bf16[32,2,128]{2,1,0:T(2,128)(2,1)S(1)}, bf16[32,2,128]{2,1,0:T(2,128)(2,1)}, u32[]{:S(2)}) copy-start(bf16[32,2,128]{2,1,0:T(2,128)(2,1)} %param.17) | copy-start | bytes 49156
  24.3 7.1 %copy-start.1 = (s32[8,32]{1,0:T(8,128)S(1)}, s32[8,32]{1,0:T(8,128)}, u32[]{:S(2)}) copy-start(s32[8,32]{1,0:T(8,128)} %nearby_hbm.3) | copy-start | bytes 3076
  24.3 7.1 %copy-start.2 = (s32[32]{0:T(128)S(1)}, s32[32]{0:T(128)}, u32[]{:S(2)}) copy-start(s32[32]{0:T(128)} %slot_hbm.3) | copy-start | bytes 388
  36.4 1.8 %collective-permute-start.3 = (f32[64,128]{1,0:T(8,128)S(1)}, f32[64,128]{1,0:T(8,128)S(1)}, u32[]{:S(2)}, u32[]{:S(2)}) collective-permute-start(f32[64,128]{1,0:T(8,128)S(1)} %shard_map.94), channel_id=1, source_target_pairs={{0,16},{16,0},{1,17},{17,1},{2,18},{18,2},{3,19},{19,3},{4,20},{20... | collective-permute-start | bytes 98312 | tf_op jit(solution)/shard_map/ppermute | solution.py:692

commit v6 on v5

--- a/solution.py
+++ b/solution.py
@@ -408,23 +408,12 @@
         copy.wait()
     pairs = out_ref.shape[0]
     left = lane_index(1) < PMAX
-    chunk = 16
-
-    def take(index, carry):
-        first = index * (2 * chunk)
-        row = first >> 7
-        base = first & (LANES - 1)
-        for n in range(chunk):
-            even = place_ref[row, base + 2 * n]
-            odd = place_ref[row, base + 2 * n + 1]
-            for field in range(2):
-                value = jnp.where(
-                    left, rows_ref[field, pl.ds(even, 1), :], rows_ref[field, pl.ds(odd, 1), :]
-                )
-                words[field, pl.ds(index * chunk + n, 1), :] = value
-        return carry
-
-    lax.fori_loop(0, pairs // chunk, take, 0)
+    for pair in range(pairs):
+        even, odd = (place_ref[link // LANES, link % LANES] for link in (2 * pair, 2 * pair + 1))
+        for field in range(2):
+            words[field, pair : pair + 1, :] = jnp.where(
+                left, rows_ref[field, pl.ds(even, 1), :], rows_ref[field, pl.ds(odd, 1), :]
+            )
     first_antenna = (lax.axis_index("grp") * portion).astype(jnp.float32)
     batch = 4
 

time: 39.2 us -> 38.8 us (0.990)
  Pallas kernels: 16.7 us -> 16.3 us
  transfers between devices with their start and end apart: 4 -> 4, of which waited for: 2 -> 2; matrix products, arithmetic and copies ran while one was open for 0% -> 0% of each run, Pallas kernels for 18% -> 17%
where the time goes in v6:
time: 38.8 us; the launch traced here: 38.5 us
  Pallas kernels  16.3 us (42%)
  blocking collectives  12.3 us (32%)
  starting transfers between devices  7.33 us (19%)
  waiting for transfers between devices  1.85 us (5%)
  other arithmetic  0.62 us (2%)
    all_to_all x1, blocking collectives, shards(): lax.all_to_all(packed.reshape(devices, stride, LANES), 'cell', split_axis...  12.3 us
    pallas_call x1, Pallas kernels, shards(): pl.pallas_call(functools.partial(respond_kernel, portion=portion), out_sh...  6.73 us
    pallas_call x1, Pallas kernels, shards(): pl.pallas_call(functools.partial(receive_kernel, portion=portion), out_sh...  4.98 us
    ppermute x2, starting transfers between devices, exchange(): return lax.ppermute(listed, 'cell', pairs + [(m, n) for n, m in pairs])  4.32 us
    pallas_call x1, Pallas kernels, shards(): pl.pallas_call(functools.partial(pack_kernel, link_total=link_total, **si...  3.58 us
    ppermute x1, starting transfers between devices, shards(): other = lax.ppermute(arrived, 'grp', swap)  2.03 us
    pallas_call x1, Pallas kernels, shards(): pl.pallas_call(functools.partial(sort_kernel, **sizes), out_shape=(jax.Sh...  1.07 us
    ppermute x1, waiting for transfers between devices, shards(): other = lax.ppermute(arrived, 'grp', swap)  0.99 us
  transfers between devices with their start and end apart: 4, of which 2 were waited for; matrix products, arithmetic and copies ran while one was open for 0% of the time, Pallas kernels for 17%

profile of v6, /device:TPU:9, one launch (start us, length us, event | category | flops | bytes accessed | tf_op | source)
XLA Modules:
  0.0 38.5 jit_solution(5508482827189725183)
XLA Ops:
  0.0 3.6 %shard_map.91 = s32[256,128]{1,0:T(8,128)S(1)} custom-call(s32[256]{0:T(256)} %link_hbm.1, s32[256]{0:T(256)} %count_hbm.1, s32[256]{0:T(256)} %offset_hbm.1, f32[65,128]{1,0:T(8,128)} %bitcast.16, f32[65,128]{1,0:T(8,128)} %bitcast.17, f32[65,2,128]{2,1,0:T(2,128)} %bitcast.15), custom_call_target="tpu_custom_call" | custom-call | tf_op jit(solution)/shard_map/pallas_call | solution.py:583
  3.6 12.3 %all_to_all.5 = s32[16,16,128]{2,1,0:T(8,128)S(1)} all-to-all(s32[16,16,128]{2,1,0:T(8,128)S(1)} %bitcast.11), channel_id=1, replica_groups=mesh['grp'=2,'cell'=16] {'cell'}, dimensions={0} | all-to-all | bytes 262144 | tf_op jit(solution)/shard_map/all_to_all | solution.py:606
  15.9 2.0 %collective-permute-start = (s32[16,16,128]{2,1,0:T(8,128)S(1)}, s32[16,16,128]{2,1,0:T(8,128)S(1)}, u32[]{:S(2)}, u32[]{:S(2)}) collective-permute-start(s32[16,16,128]{2,1,0:T(8,128)S(1)} %all_to_all.5), channel_id=1, source_target_pairs={{0,16},{16,0},{1,17},{17,1},{2,18},{18,2},{3,19},{19,3},{4,20},{20... | collective-permute-start | bytes 393224 | tf_op jit(solution)/shard_map/ppermute | solution.py:609
  17.9 1.0 %collective-permute-done = s32[16,16,128]{2,1,0:T(8,128)S(1)} collective-permute-done((s32[16,16,128]{2,1,0:T(8,128)S(1)}, s32[16,16,128]{2,1,0:T(8,128)S(1)}, u32[]{:S(2)}, u32[]{:S(2)}) %collective-permute-start) | collective-permute-done | bytes 131104 | tf_op jit(solution)/shard_map/ppermute | solution.py:609
  18.9 1.1 %shard_map.92 = (s32[2,512,128]{2,1,0:T(8,128)S(1)}, s32[2,128]{1,0:T(2,128)S(1)}, s32[72,128]{1,0:T(8,128)S(1)}) custom-call(s32[8,32]{1,0:T(8,128)} %nearby_hbm.3, s32[32]{0:T(128)} %slot_hbm.3, bf16[64,128]{1,0:T(8,128)(2,1)} %bitcast.13, s32[256,128]{1,0:T(8,128)S(1)} %bitcast.10, s32[256,128]{1,0:T(8,128)S(1)} %bitcast.12), custom_call_target="tpu_custom_call" | custom-call | tf_op jit(solution)/shard_map/pallas_call | solution.py:619
  19.9 0.3 collective-permute-start.1
  20.3 4.0 %collective-permute-start.2 = (s32[72,128]{1,0:T(8,128)S(1)}, s32[72,128]{1,0:T(8,128)S(1)}, u32[]{:S(2)}, u32[]{:S(2)}) collective-permute-start(s32[72,128]{1,0:T(8,128)S(1)} %get-tuple-element.10), channel_id=1, source_target_pairs={{1,2},{3,4},{5,6},{7,8},{9,10},{11,12},{13,14},{2,1},{4,3},{6,5},{... | collective-permute-start | bytes 110600 | tf_op jit(solution)/shard_map/ppermute | solution.py:641
  24.3 0.0 copy-start
  24.3 0.0 copy-start.1
  24.3 0.0 copy-start.2
  24.3 6.7 %shard_map.93.response_ref = f32[128,128,128]{2,1,0:T(8,128)S(1)} custom-call(s32[2,512,128]{2,1,0:T(8,128)S(1)} %get-tuple-element.8.rows_ref, s32[2,128]{1,0:T(2,128)S(1)} %get-tuple-element.9.table_ref), custom_call_target="tpu_custom_call" | custom-call | flops 42949672960 | bytes 4194304 | tf_op jit(solution)/shard_map/pallas_call | solution.py:646
  31.1 0.0 collective-permute-done.1.first_ref
  31.1 0.0 collective-permute-done.2.second_ref
  31.1 0.0 copy-done
  31.1 0.0 copy-done.1
  31.1 0.0 copy-done.2
  31.1 5.0 %shard_map.94 = f32[64,128]{1,0:T(8,128)S(1)} custom-call(s32[8,32]{1,0:T(8,128)S(1)} %copy-done.1, s32[32]{0:T(128)S(1)} %copy-done.2, bf16[64,128]{1,0:T(8,128)(2,1)S(1)} %bitcast.14, f32[128,128,128]{2,1,0:T(8,128)S(1)} %shard_map.93.response_ref, s32[72,128]{1,0:T(8,128)S(1)} %collective-permute-done.1.first_ref, ...), custom_call_target="tpu_custom_call" | custom-call | tf_op jit(solution)/shard_map/pallas_call | solution.py:665
  36.1 1.0 %collective-permute-start.3 = (f32[64,128]{1,0:T(8,128)S(1)}, f32[64,128]{1,0:T(8,128)S(1)}, u32[]{:S(2)}, u32[]{:S(2)}) collective-permute-start(f32[64,128]{1,0:T(8,128)S(1)} %shard_map.94), channel_id=1, source_target_pairs={{0,16},{16,0},{1,17},{17,1},{2,18},{18,2},{3,19},{19,3},{4,20},{20... | collective-permute-start | bytes 98312 | tf_op jit(solution)/shard_map/ppermute | solution.py:681
  37.1 0.9 %collective-permute-done.3 = f32[64,128]{1,0:T(8,128)S(1)} collective-permute-done((f32[64,128]{1,0:T(8,128)S(1)}, f32[64,128]{1,0:T(8,128)S(1)}, u32[]{:S(2)}, u32[]{:S(2)}) %collective-permute-start.3) | collective-permute-done | bytes 32800 | tf_op jit(solution)/shard_map/ppermute | solution.py:681
  37.9 0.6 %add.3 = f32[64,128]{1,0:T(8,128)} add(f32[64,128]{1,0:T(8,128)S(1)} %shard_map.94, f32[64,128]{1,0:T(8,128)S(1)} %collective-permute-done.3) | non-fusion elementwise | flops 8192 | bytes 98304 | tf_op jit(solution)/shard_map/add | solution.py:681
Async XLA Ops:
  15.9 3.0 %collective-permute-start = (s32[16,16,128]{2,1,0:T(8,128)S(1)}, s32[16,16,128]{2,1,0:T(8,128)S(1)}, u32[]{:S(2)}, u32[]{:S(2)}) collective-permute-start(s32[16,16,128]{2,1,0:T(8,128)S(1)} %all_to_all.5), channel_id=1, source_target_pairs={{0,16},{16,0},{1,17},{17,1},{2,18},{18,2},{3,19},{19,3},{4,20},{20... | collective-permute-start | bytes 393224 | tf_op jit(solution)/shard_map/ppermute | solution.py:609
  19.9 11.1 %collective-permute-start.1 = (s32[72,128]{1,0:T(8,128)S(1)}, s32[72,128]{1,0:T(8,128)S(1)}, u32[]{:S(2)}, u32[]{:S(2)}) collective-permute-start(s32[72,128]{1,0:T(8,128)S(1)} %get-tuple-element.10), channel_id=1, source_target_pairs={{0,1},{2,3},{4,5},{6,7},{8,9},{10,11},{12,13},{14,15},{1,0},{3,2},... | collective-permute-start | bytes 110600 | tf_op jit(solution)/shard_map/ppermute | solution.py:641
  20.3 10.8 %collective-permute-start.2 = (s32[72,128]{1,0:T(8,128)S(1)}, s32[72,128]{1,0:T(8,128)S(1)}, u32[]{:S(2)}, u32[]{:S(2)}) collective-permute-start(s32[72,128]{1,0:T(8,128)S(1)} %get-tuple-element.10), channel_id=1, source_target_pairs={{1,2},{3,4},{5,6},{7,8},{9,10},{11,12},{13,14},{2,1},{4,3},{6,5},{... | collective-permute-start | bytes 110600 | tf_op jit(solution)/shard_map/ppermute | solution.py:641
  24.3 6.8 %copy-start = (bf16[32,2,128]{2,1,0:T(2,128)(2,1)S(1)}, bf16[32,2,128]{2,1,0:T(2,128)(2,1)}, u32[]{:S(2)}) copy-start(bf16[32,2,128]{2,1,0:T(2,128)(2,1)} %param.17) | copy-start | bytes 49156
  24.3 6.8 %copy-start.1 = (s32[8,32]{1,0:T(8,128)S(1)}, s32[8,32]{1,0:T(8,128)}, u32[]{:S(2)}) copy-start(s32[8,32]{1,0:T(8,128)} %nearby_hbm.3) | copy-start | bytes 3076
  24.3 6.8 %copy-start.2 = (s32[32]{0:T(128)S(1)}, s32[32]{0:T(128)}, u32[]{:S(2)}) copy-start(s32[32]{0:T(128)} %slot_hbm.3) | copy-start | bytes 388
  36.1 1.8 %collective-permute-start.3 = (f32[64,128]{1,0:T(8,128)S(1)}, f32[64,128]{1,0:T(8,128)S(1)}, u32[]{:S(2)}, u32[]{:S(2)}) collective-permute-start(f32[64,128]{1,0:T(8,128)S(1)} %shard_map.94), channel_id=1, source_target_pairs={{0,16},{16,0},{1,17},{17,1},{2,18},{18,2},{3,19},{19,3},{4,20},{20... | collective-permute-start | bytes 98312 | tf_op jit(solution)/shard_map/ppermute | solution.py:681

commit v7 on v6

--- a/solution.py
+++ b/solution.py
@@ -531,7 +531,7 @@
         out_ref[pl.ds(user * 2 + 1, 1), :] = jnp.sum(total_im, axis=0, keepdims=True) * scale
         return carry
 
-    lax.fori_loop(0, users, one_user, 0, unroll=4)
+    lax.fori_loop(0, users, one_user, 0, unroll=8)
     out_ref[...] = reorder(out_ref[...], place_of_tone(lane_index(GROUP)))
 
 

time: 38.8 us -> 38.8 us (level)
  no operation moved by 1% of the time
where the time goes in v7:
time: 38.8 us; the launch traced here: 38.5 us
  Pallas kernels  16.3 us (42%)
  blocking collectives  12.3 us (32%)
  starting transfers between devices  7.34 us (19%)
  waiting for transfers between devices  1.85 us (5%)
  other arithmetic  0.62 us (2%)
    all_to_all x1, blocking collectives, shards(): lax.all_to_all(packed.reshape(devices, stride, LANES), 'cell', split_axis...  12.3 us
    pallas_call x1, Pallas kernels, shards(): pl.pallas_call(functools.partial(respond_kernel, portion=portion), out_sh...  6.72 us
    pallas_call x1, Pallas kernels, shards(): pl.pallas_call(functools.partial(receive_kernel, portion=portion), out_sh...  4.9 us
    ppermute x2, starting transfers between devices, exchange(): return lax.ppermute(listed, 'cell', pairs + [(m, n) for n, m in pairs])  4.32 us
    pallas_call x1, Pallas kernels, shards(): pl.pallas_call(functools.partial(pack_kernel, link_total=link_total, **si...  3.58 us
    ppermute x1, starting transfers between devices, shards(): other = lax.ppermute(arrived, 'grp', swap)  2.03 us
    pallas_call x1, Pallas kernels, shards(): pl.pallas_call(functools.partial(sort_kernel, **sizes), out_shape=(jax.Sh...  1.07 us
    ppermute x1, waiting for transfers between devices, shards(): other = lax.ppermute(arrived, 'grp', swap)  0.99 us
  transfers between devices with their start and end apart: 4, of which 2 were waited for; matrix products, arithmetic and copies ran while one was open for 0% of the time, Pallas kernels for 17%

profile of v7, /device:TPU:9, one launch (start us, length us, event | category | flops | bytes accessed | tf_op | source)
XLA Modules:
  0.0 38.5 jit_solution(2818028677355424827)
XLA Ops:
  0.0 3.6 %shard_map.91 = s32[256,128]{1,0:T(8,128)S(1)} custom-call(s32[256]{0:T(256)} %link_hbm.1, s32[256]{0:T(256)} %count_hbm.1, s32[256]{0:T(256)} %offset_hbm.1, f32[65,128]{1,0:T(8,128)} %bitcast.16, f32[65,128]{1,0:T(8,128)} %bitcast.17, f32[65,2,128]{2,1,0:T(2,128)} %bitcast.15), custom_call_target="tpu_custom_call" | custom-call | tf_op jit(solution)/shard_map/pallas_call | solution.py:583
  3.6 12.3 %all_to_all.5 = s32[16,16,128]{2,1,0:T(8,128)S(1)} all-to-all(s32[16,16,128]{2,1,0:T(8,128)S(1)} %bitcast.11), channel_id=1, replica_groups=mesh['grp'=2,'cell'=16] {'cell'}, dimensions={0} | all-to-all | bytes 262144 | tf_op jit(solution)/shard_map/all_to_all | solution.py:606
  15.9 2.0 %collective-permute-start = (s32[16,16,128]{2,1,0:T(8,128)S(1)}, s32[16,16,128]{2,1,0:T(8,128)S(1)}, u32[]{:S(2)}, u32[]{:S(2)}) collective-permute-start(s32[16,16,128]{2,1,0:T(8,128)S(1)} %all_to_all.5), channel_id=1, source_target_pairs={{0,16},{16,0},{1,17},{17,1},{2,18},{18,2},{3,19},{19,3},{4,20},{20... | collective-permute-start | bytes 393224 | tf_op jit(solution)/shard_map/ppermute | solution.py:609
  17.9 1.0 %collective-permute-done = s32[16,16,128]{2,1,0:T(8,128)S(1)} collective-permute-done((s32[16,16,128]{2,1,0:T(8,128)S(1)}, s32[16,16,128]{2,1,0:T(8,128)S(1)}, u32[]{:S(2)}, u32[]{:S(2)}) %collective-permute-start) | collective-permute-done | bytes 131104 | tf_op jit(solution)/shard_map/ppermute | solution.py:609
  18.9 1.1 %shard_map.92 = (s32[2,512,128]{2,1,0:T(8,128)S(1)}, s32[2,128]{1,0:T(2,128)S(1)}, s32[72,128]{1,0:T(8,128)S(1)}) custom-call(s32[8,32]{1,0:T(8,128)} %nearby_hbm.3, s32[32]{0:T(128)} %slot_hbm.3, bf16[64,128]{1,0:T(8,128)(2,1)} %bitcast.13, s32[256,128]{1,0:T(8,128)S(1)} %bitcast.10, s32[256,128]{1,0:T(8,128)S(1)} %bitcast.12), custom_call_target="tpu_custom_call" | custom-call | tf_op jit(solution)/shard_map/pallas_call | solution.py:619
  19.9 0.3 collective-permute-start.1
  20.3 4.0 %collective-permute-start.2 = (s32[72,128]{1,0:T(8,128)S(1)}, s32[72,128]{1,0:T(8,128)S(1)}, u32[]{:S(2)}, u32[]{:S(2)}) collective-permute-start(s32[72,128]{1,0:T(8,128)S(1)} %get-tuple-element.10), channel_id=1, source_target_pairs={{1,2},{3,4},{5,6},{7,8},{9,10},{11,12},{13,14},{2,1},{4,3},{6,5},{... | collective-permute-start | bytes 110600 | tf_op jit(solution)/shard_map/ppermute | solution.py:641
  24.3 0.0 copy-start
  24.3 0.0 copy-start.1
  24.3 0.0 copy-start.2
  24.3 6.7 %shard_map.93.response_ref = f32[128,128,128]{2,1,0:T(8,128)S(1)} custom-call(s32[2,512,128]{2,1,0:T(8,128)S(1)} %get-tuple-element.8.rows_ref, s32[2,128]{1,0:T(2,128)S(1)} %get-tuple-element.9.table_ref), custom_call_target="tpu_custom_call" | custom-call | flops 42949672960 | bytes 4194304 | tf_op jit(solution)/shard_map/pallas_call | solution.py:646
  31.0 0.0 collective-permute-done.1.first_ref
  31.1 0.0 collective-permute-done.2.second_ref
  31.1 0.0 copy-done
  31.1 0.0 copy-done.1
  31.1 0.0 copy-done.2
  31.1 4.9 %shard_map.94 = f32[64,128]{1,0:T(8,128)S(1)} custom-call(s32[8,32]{1,0:T(8,128)S(1)} %copy-done.1, s32[32]{0:T(128)S(1)} %copy-done.2, bf16[64,128]{1,0:T(8,128)(2,1)S(1)} %bitcast.14, f32[128,128,128]{2,1,0:T(8,128)S(1)} %shard_map.93.response_ref, s32[72,128]{1,0:T(8,128)S(1)} %collective-permute-done.1.first_ref, ...), custom_call_target="tpu_custom_call" | custom-call | tf_op jit(solution)/shard_map/pallas_call | solution.py:665
  36.0 1.0 %collective-permute-start.3 = (f32[64,128]{1,0:T(8,128)S(1)}, f32[64,128]{1,0:T(8,128)S(1)}, u32[]{:S(2)}, u32[]{:S(2)}) collective-permute-start(f32[64,128]{1,0:T(8,128)S(1)} %shard_map.94), channel_id=1, source_target_pairs={{0,16},{16,0},{1,17},{17,1},{2,18},{18,2},{3,19},{19,3},{4,20},{20... | collective-permute-start | bytes 98312 | tf_op jit(solution)/shard_map/ppermute | solution.py:681
  37.0 0.9 %collective-permute-done.3 = f32[64,128]{1,0:T(8,128)S(1)} collective-permute-done((f32[64,128]{1,0:T(8,128)S(1)}, f32[64,128]{1,0:T(8,128)S(1)}, u32[]{:S(2)}, u32[]{:S(2)}) %collective-permute-start.3) | collective-permute-done | bytes 32800 | tf_op jit(solution)/shard_map/ppermute | solution.py:681
  37.8 0.6 %add.3 = f32[64,128]{1,0:T(8,128)} add(f32[64,128]{1,0:T(8,128)S(1)} %shard_map.94, f32[64,128]{1,0:T(8,128)S(1)} %collective-permute-done.3) | non-fusion elementwise | flops 8192 | bytes 98304 | tf_op jit(solution)/shard_map/add | solution.py:681
Async XLA Ops:
  15.9 3.0 %collective-permute-start = (s32[16,16,128]{2,1,0:T(8,128)S(1)}, s32[16,16,128]{2,1,0:T(8,128)S(1)}, u32[]{:S(2)}, u32[]{:S(2)}) collective-permute-start(s32[16,16,128]{2,1,0:T(8,128)S(1)} %all_to_all.5), channel_id=1, source_target_pairs={{0,16},{16,0},{1,17},{17,1},{2,18},{18,2},{3,19},{19,3},{4,20},{20... | collective-permute-start | bytes 393224 | tf_op jit(solution)/shard_map/ppermute | solution.py:609
  19.9 11.1 %collective-permute-start.1 = (s32[72,128]{1,0:T(8,128)S(1)}, s32[72,128]{1,0:T(8,128)S(1)}, u32[]{:S(2)}, u32[]{:S(2)}) collective-permute-start(s32[72,128]{1,0:T(8,128)S(1)} %get-tuple-element.10), channel_id=1, source_target_pairs={{0,1},{2,3},{4,5},{6,7},{8,9},{10,11},{12,13},{14,15},{1,0},{3,2},... | collective-permute-start | bytes 110600 | tf_op jit(solution)/shard_map/ppermute | solution.py:641
  20.3 10.8 %collective-permute-start.2 = (s32[72,128]{1,0:T(8,128)S(1)}, s32[72,128]{1,0:T(8,128)S(1)}, u32[]{:S(2)}, u32[]{:S(2)}) collective-permute-start(s32[72,128]{1,0:T(8,128)S(1)} %get-tuple-element.10), channel_id=1, source_target_pairs={{1,2},{3,4},{5,6},{7,8},{9,10},{11,12},{13,14},{2,1},{4,3},{6,5},{... | collective-permute-start | bytes 110600 | tf_op jit(solution)/shard_map/ppermute | solution.py:641
  24.3 6.8 %copy-start = (bf16[32,2,128]{2,1,0:T(2,128)(2,1)S(1)}, bf16[32,2,128]{2,1,0:T(2,128)(2,1)}, u32[]{:S(2)}) copy-start(bf16[32,2,128]{2,1,0:T(2,128)(2,1)} %param.17) | copy-start | bytes 49156
  24.3 6.8 %copy-start.1 = (s32[8,32]{1,0:T(8,128)S(1)}, s32[8,32]{1,0:T(8,128)}, u32[]{:S(2)}) copy-start(s32[8,32]{1,0:T(8,128)} %nearby_hbm.3) | copy-start | bytes 3076
  24.3 6.8 %copy-start.2 = (s32[32]{0:T(128)S(1)}, s32[32]{0:T(128)}, u32[]{:S(2)}) copy-start(s32[32]{0:T(128)} %slot_hbm.3) | copy-start | bytes 388
  36.0 1.8 %collective-permute-start.3 = (f32[64,128]{1,0:T(8,128)S(1)}, f32[64,128]{1,0:T(8,128)S(1)}, u32[]{:S(2)}, u32[]{:S(2)}) collective-permute-start(f32[64,128]{1,0:T(8,128)S(1)} %shard_map.94), channel_id=1, source_target_pairs={{0,16},{16,0},{1,17},{17,1},{2,18},{18,2},{3,19},{19,3},{4,20},{20... | collective-permute-start | bytes 98312 | tf_op jit(solution)/shard_map/ppermute | solution.py:681
